TPU v7x, 256 devices: a whole 4x4x8 slice. The times are simulated.
256 devices in a mesh: depth: 8 (over y, core), illum: 32 (over x, z).
Axes of the slice: x: 4, y: 4, z: 8, core: 2. Of those that a mesh axis runs over, the one named last changes fastest.
Arguments:
- fields: bfloat16 [24, 64, 2, 256, 256], P('depth', 'illum'), may hold values from -3.5 to 3.5
- screen_real: float32 [24, 256, 256], P('depth'), may hold values from 0.85 to 1.1
- screen_imag: float32 [24, 256, 256], P('depth'), may hold values from -0.3 to 0.3
- measured: float32 [64, 256, 256], P('illum'), may hold values from 0.2 to 2.5
- angles: int32 [64], P('illum'), may hold values from 0 to 255
Outputs:
- gradient: float32 [24, 2, 256, 256], P('depth', None, 'illum')
All inputs are finite; a program needn't handle non-finite values.
Results may differ from a plain program's by a relative error of at most 0.0003.
Values sent between devices are 32-bit elements; how exact they have to be, the bound alone decides.
No kernel may reach another device: no remote copies, remote signals or barrier semaphores. Data moves between devices by JAX's collectives and lax.ppermute only.
A program may use at most 64 MiB of HBM per device.

v0:
```python
import jax
import jax.numpy as jnp
from jax import lax
from jax.sharding import PartitionSpec as P

HIGHEST_PRECISION = lax.Precision.HIGHEST


def shifted(value, axis, steps):
    count = lax.axis_size(axis)
    first, last = (max(0, -steps), min(count, count - steps))
    return lax.ppermute(value, axis, [(source, source + steps) for source in range(first, last)])


def tables(extent):
    counter = jnp.arange(extent, dtype=jnp.int32)
    product = counter[:, None] * counter[None, :] % extent
    phase_angle = 2.0 * jnp.pi / extent * product.astype(jnp.float32)
    frequency = jnp.where(counter < extent // 2, counter, counter - extent)
    square = (
        frequency[:, None] * frequency[:, None] + frequency[None, :] * frequency[None, :]
    ) % 1024
    kernel_phase = 2.0 * jnp.pi / 1024.0 * square.astype(jnp.float32)
    return (
        jnp.cos(phase_angle),
        -jnp.sin(phase_angle),
        jnp.cos(kernel_phase),
        jnp.sin(kernel_phase),
    )


def ramps(angles, extent):
    counter = jnp.arange(extent, dtype=jnp.int32)
    shift_x = angles % 16 - 8
    shift_y = angles // 16 - 8
    phase_int = (
        shift_x[:, None, None] * counter[None, :, None]
        + shift_y[:, None, None] * counter[None, None, :]
    ) % extent
    phase_angle = 2.0 * jnp.pi / extent * phase_int.astype(jnp.float32)
    return (jnp.cos(phase_angle), jnp.sin(phase_angle))


def contract(pattern, first_operand, second_operand):
    return jnp.einsum(
        pattern,
        first_operand,
        second_operand,
        precision=HIGHEST_PRECISION,
        preferred_element_type=jnp.float32,
    )


def transform(real_part, imag_part, table_real, table_imag):
    mid_real = contract("bxy,yk->bxk", real_part, table_real) - contract(
        "bxy,yk->bxk", imag_part, table_imag
    )
    mid_imag = contract("bxy,yk->bxk", real_part, table_imag) + contract(
        "bxy,yk->bxk", imag_part, table_real
    )
    out_real = contract("jx,bxk->bjk", table_real, mid_real) - contract(
        "jx,bxk->bjk", table_imag, mid_imag
    )
    out_imag = contract("jx,bxk->bjk", table_imag, mid_real) + contract(
        "jx,bxk->bjk", table_real, mid_imag
    )
    return (out_real, out_imag)


def propagate(real_part, imag_part, operator_tables, direction):
    table_real, table_imag, kernel_cos, kernel_sin = operator_tables
    spec_real, spec_imag = transform(real_part, imag_part, table_real, table_imag)
    phase_sin = direction * kernel_sin
    mult_real = kernel_cos * spec_real - phase_sin * spec_imag
    mult_imag = kernel_cos * spec_imag + phase_sin * spec_real
    back_real, back_imag = transform(mult_real, mult_imag, table_real, -table_imag)
    inverse_scale = 1.0 / (table_real.shape[0] * table_real.shape[0])
    return (back_real * inverse_scale, back_imag * inverse_scale)


def tilted(stored, slab_index, ramp_cos, ramp_sin):
    env_real = stored[slab_index, :, 0].astype(jnp.float32)
    env_imag = stored[slab_index, :, 1].astype(jnp.float32)
    return (ramp_cos * env_real - ramp_sin * env_imag, ramp_cos * env_imag + ramp_sin * env_real)


def exit_cotangent(stored, ramp_cos, ramp_sin, screen_real, screen_imag, measured, operator_tables):
    field_real, field_imag = tilted(stored, stored.shape[0] - 1, ramp_cos, ramp_sin)
    lit_real = screen_real[-1] * field_real - screen_imag[-1] * field_imag
    lit_imag = screen_real[-1] * field_imag + screen_imag[-1] * field_real
    out_real, out_imag = propagate(lit_real, lit_imag, operator_tables, -1.0)
    weight = 2.0 * (out_real * out_real + out_imag * out_imag - measured)
    return jnp.stack([weight * out_real, weight * out_imag], axis=1)


def section(cotangent, stored, ramp_cos, ramp_sin, screen_real, screen_imag, operator_tables):
    cot_real = cotangent[:, 0]
    cot_imag = cotangent[:, 1]
    gradient_list = []
    for slab_index in reversed(range(stored.shape[0])):
        prop_real, prop_imag = propagate(cot_real, cot_imag, operator_tables, 1.0)
        field_real, field_imag = tilted(stored, slab_index, ramp_cos, ramp_sin)
        grad_real = jnp.sum(field_real * prop_real + field_imag * prop_imag, axis=0)
        grad_imag = jnp.sum(field_real * prop_imag - field_imag * prop_real, axis=0)
        gradient_list.append(jnp.stack([grad_real, grad_imag]))
        cot_real = screen_real[slab_index] * prop_real + screen_imag[slab_index] * prop_imag
        cot_imag = screen_real[slab_index] * prop_imag - screen_imag[slab_index] * prop_real
    return (jnp.stack([cot_real, cot_imag], axis=1), jnp.stack(gradient_list[::-1]))


def on_device(fields, screen_real, screen_imag, measured, angles):
    extent = screen_real.shape[-1]
    local_count = angles.shape[0]
    segments = lax.axis_size("depth")
    position = lax.axis_index("depth")
    illum_total = local_count * lax.axis_size("illum")
    operator_tables = tables(extent)
    ramp_cos, ramp_sin = ramps(angles, extent)
    is_last = position == segments - 1
    zero_cot = jnp.zeros((local_count, 2, extent, extent), jnp.float32)
    exit_value = lax.cond(
        is_last,
        lambda: exit_cotangent(
            fields, ramp_cos, ramp_sin, screen_real, screen_imag, measured, operator_tables
        ),
        lambda: zero_cot,
    )
    zero_grad = jnp.zeros((screen_real.shape[0], 2, extent, extent), jnp.float32)

    def turn_all(turn_index, state_pair):
        outgoing, gradient = state_pair
        incoming = shifted(outgoing, "depth", -1)
        active = turn_index == segments - 1 - position
        entering = jnp.where(is_last, exit_value, incoming)

        def advance():
            leaving, added = section(
                entering, fields, ramp_cos, ramp_sin, screen_real, screen_imag, operator_tables
            )
            return (leaving, gradient + added)

        return lax.cond(active, advance, lambda: (entering, gradient))

    _, gradient = lax.fori_loop(0, segments, turn_all, (zero_cot, zero_grad))
    scaled = gradient * float(illum_total) ** (-0.5)
    return lax.psum_scatter(scaled, "illum", scatter_dimension=2, tiled=True)


def solution(mesh):
    return jax.shard_map(
        on_device,
        mesh=mesh,
        in_specs=(
            P("depth", "illum", None, None, None),
            P("depth", None, None),
            P("depth", None, None),
            P("illum", None, None),
            P("illum"),
        ),
        out_specs=P("depth", None, "illum", None),
        check_vma=False,
    )
```

profile of v0, /device:TPU:32, one launch (start us, length us, event | category | flops | bytes accessed | tf_op | source)
XLA Modules:
  0.0 1079.8 jit_solution(13013563743406397902)
XLA Ops:
  7.6 2.3 copy.164
  11.1 2.7 copy.166
  14.1 2.2 conditional.2
  17.6 835.2 %while.20 = (s32[]{:T(128)}, f32[2,2,256,256]{2,3,0,1:T(8,128)}, f32[3,2,256,256]{2,3,1,0:T(8,128)S(1)}, s32[]{:T(128)}, pred[]{:T(512)}, /*index=5*/f32[2,2,256...) while((s32[]{:T(128)}, f32[2,2,256,256]{2,3,0,1:T(8,128)}, ...), condition=%wide.region_11.12_spmd.clone.clone.clone, body=%wide.region_2.11_spmd.clone.clone.clone.sunk | while | flops 19352780800 | bytes 129504560 | solution.py:144
  26.0 1.6 copy.260
  29.6 2.7 collective-permute-done
  33.7 2.3 conditional.7
  45.3 1.6 copy.260
  48.9 13.6 %collective-permute-done = f32[2,2,256,256]{3,2,0,1:T(8,128)} collective-permute-done((f32[2,2,256,256]{3,2,0,1:T(8,128)S(1)}, f32[2,2,256,256]{3,2,0,1:T(8,128)}, u32[]{:S(2)}, u32[]{:S(2)}) %collective-permute-start) | collective-permute-done | bytes 1048608 | tf_op jit(solution)/shard_map/while/body/eval_jaxpr/ppermute | solution.py:12
  65.2 1.6 copy.260
  68.7 14.3 %collective-permute-done = f32[2,2,256,256]{3,2,0,1:T(8,128)} collective-permute-done((f32[2,2,256,256]{3,2,0,1:T(8,128)S(1)}, f32[2,2,256,256]{3,2,0,1:T(8,128)}, u32[]{:S(2)}, u32[]{:S(2)}) %collective-permute-start) | collective-permute-done | bytes 1048608 | tf_op jit(solution)/shard_map/while/body/eval_jaxpr/ppermute | solution.py:12
  85.7 1.6 copy.260
  89.2 14.3 %collective-permute-done = f32[2,2,256,256]{3,2,0,1:T(8,128)} collective-permute-done((f32[2,2,256,256]{3,2,0,1:T(8,128)S(1)}, f32[2,2,256,256]{3,2,0,1:T(8,128)}, u32[]{:S(2)}, u32[]{:S(2)}) %collective-permute-start) | collective-permute-done | bytes 1048608 | tf_op jit(solution)/shard_map/while/body/eval_jaxpr/ppermute | solution.py:12
  106.2 1.6 copy.260
  109.7 14.3 %collective-permute-done = f32[2,2,256,256]{3,2,0,1:T(8,128)} collective-permute-done((f32[2,2,256,256]{3,2,0,1:T(8,128)S(1)}, f32[2,2,256,256]{3,2,0,1:T(8,128)}, u32[]{:S(2)}, u32[]{:S(2)}) %collective-permute-start) | collective-permute-done | bytes 1048608 | tf_op jit(solution)/shard_map/while/body/eval_jaxpr/ppermute | solution.py:12
  126.6 1.6 copy.260
  130.1 14.3 %collective-permute-done = f32[2,2,256,256]{3,2,0,1:T(8,128)} collective-permute-done((f32[2,2,256,256]{3,2,0,1:T(8,128)S(1)}, f32[2,2,256,256]{3,2,0,1:T(8,128)}, u32[]{:S(2)}, u32[]{:S(2)}) %collective-permute-start) | collective-permute-done | bytes 1048608 | tf_op jit(solution)/shard_map/while/body/eval_jaxpr/ppermute | solution.py:12
  147.1 1.6 copy.260
  150.6 14.3 %collective-permute-done = f32[2,2,256,256]{3,2,0,1:T(8,128)} collective-permute-done((f32[2,2,256,256]{3,2,0,1:T(8,128)S(1)}, f32[2,2,256,256]{3,2,0,1:T(8,128)}, u32[]{:S(2)}, u32[]{:S(2)}) %collective-permute-start) | collective-permute-done | bytes 1048608 | tf_op jit(solution)/shard_map/while/body/eval_jaxpr/ppermute | solution.py:12
  167.6 1.6 copy.260
  171.1 591.5 %collective-permute-done = f32[2,2,256,256]{3,2,0,1:T(8,128)} collective-permute-done((f32[2,2,256,256]{3,2,0,1:T(8,128)S(1)}, f32[2,2,256,256]{3,2,0,1:T(8,128)}, u32[]{:S(2)}, u32[]{:S(2)}) %collective-permute-start) | collective-permute-done | bytes 1048608 | tf_op jit(solution)/shard_map/while/body/eval_jaxpr/ppermute | solution.py:12
  764.0 78.1 %conditional.7 = (f32[2,2,256,256]{2,3,0,1:T(8,128)}, f32[3,2,256,256]{2,3,1,0:T(8,128)S(1)}) conditional(s32[]{:T(128)} %convert_element_type.295, (f32[2,2,256,256]{3,2,0,1:T(8,128)S(1)}, f32[3,2,256,256]{2,3,1,0:T(8,128)S(1)}) %tuple.177, (f32[256,256]{0,1:T(8,128)S(1)}, f32[2,2,256,256]{3,2,0,1:T(8,128)S(1)}, f32[256,256]{1,0:T(8,128)S(1)}, ...), branch_computations={%region_3.3_spmd, %region_4.10_spmd.clone} | conditional | flops 19348848640 | bytes 119013392 | solution.py:142
  764.0 1.5 multiply_bitcast_fusion.2
  768.6 1.4 convolution_add_fusion.15
  773.1 1.7 fusion.50
  774.8 1.7 fusion.101
  778.8 1.7 convolution_add_fusion.13
  780.6 1.7 fusion.91
  784.4 1.7 fusion.48
  786.0 1.7 fusion.100
  790.0 1.8 convolution_add_fusion.11
  791.8 1.8 fusion.92
  795.6 1.7 fusion.46
  797.2 1.7 fusion.99
  801.0 2.1 convolution_add_fusion.9
  803.1 1.7 fusion.93
  806.9 1.7 fusion.44
  808.6 1.7 fusion.98
  812.3 1.9 convolution_add_fusion.7
  814.3 1.8 fusion.94
  818.1 1.7 fusion.42
  819.7 1.7 fusion.97
  823.5 1.7 convolution_add_fusion.5
  825.2 2.0 fusion.95
  829.2 1.7 fusion.96
  830.9 1.7 fusion.40
  832.6 7.7 add_reduce_fusion.1
  854.6 217.8 %reduce-scatter.2.cloned.1.call-done = f32[3,2,8,256]{3,2,1,0:T(8,128)} async-done(((f32[3,2,256,256]{3,2,1,0:T(8,128)}), f32[3,2,8,256]{3,2,1,0:T(8,128)}) %reduce-scatter.2.cloned.1.call-update) | async-done | bytes 49168 | tf_op jit(solution)/shard_map/reduce_scatter | solution.py:146
  (102 shorter events, 78.4 us)
Async XLA Ops:
  6.5 3.4 copy-start
  6.5 1065.9 %reduce-scatter.2.cloned.1.call-start = ((), (), s32[]{:S(2)}) async-start(), calls=%async_computation.1 | async-start | bytes 1622016 | tf_op jit(solution)/shard_map/reduce_scatter | solution.py:146
  11.1 3.1 copy-start.1
  27.6 4.7 collective-permute-start
  46.9 15.6 %collective-permute-start = (f32[2,2,256,256]{3,2,0,1:T(8,128)S(1)}, f32[2,2,256,256]{3,2,0,1:T(8,128)}, u32[]{:S(2)}, u32[]{:S(2)}) collective-permute-start(f32[2,2,256,256]{3,2,0,1:T(8,128)S(1)} %copy.260), channel_id=1, source_target_pairs={{32,0},{64,32},{96,64},{128,96},{160,128},{192,160},{224,192},{33,... | collective-permute-start | bytes 3145736 | tf_op jit(solution)/shard_map/while/body/eval_jaxpr/ppermute | solution.py:12
  66.8 16.2 %collective-permute-start = (f32[2,2,256,256]{3,2,0,1:T(8,128)S(1)}, f32[2,2,256,256]{3,2,0,1:T(8,128)}, u32[]{:S(2)}, u32[]{:S(2)}) collective-permute-start(f32[2,2,256,256]{3,2,0,1:T(8,128)S(1)} %copy.260), channel_id=1, source_target_pairs={{32,0},{64,32},{96,64},{128,96},{160,128},{192,160},{224,192},{33,... | collective-permute-start | bytes 3145736 | tf_op jit(solution)/shard_map/while/body/eval_jaxpr/ppermute | solution.py:12
  87.2 16.2 %collective-permute-start = (f32[2,2,256,256]{3,2,0,1:T(8,128)S(1)}, f32[2,2,256,256]{3,2,0,1:T(8,128)}, u32[]{:S(2)}, u32[]{:S(2)}) collective-permute-start(f32[2,2,256,256]{3,2,0,1:T(8,128)S(1)} %copy.260), channel_id=1, source_target_pairs={{32,0},{64,32},{96,64},{128,96},{160,128},{192,160},{224,192},{33,... | collective-permute-start | bytes 3145736 | tf_op jit(solution)/shard_map/while/body/eval_jaxpr/ppermute | solution.py:12
  107.7 16.2 %collective-permute-start = (f32[2,2,256,256]{3,2,0,1:T(8,128)S(1)}, f32[2,2,256,256]{3,2,0,1:T(8,128)}, u32[]{:S(2)}, u32[]{:S(2)}) collective-permute-start(f32[2,2,256,256]{3,2,0,1:T(8,128)S(1)} %copy.260), channel_id=1, source_target_pairs={{32,0},{64,32},{96,64},{128,96},{160,128},{192,160},{224,192},{33,... | collective-permute-start | bytes 3145736 | tf_op jit(solution)/shard_map/while/body/eval_jaxpr/ppermute | solution.py:12
  128.2 16.2 %collective-permute-start = (f32[2,2,256,256]{3,2,0,1:T(8,128)S(1)}, f32[2,2,256,256]{3,2,0,1:T(8,128)}, u32[]{:S(2)}, u32[]{:S(2)}) collective-permute-start(f32[2,2,256,256]{3,2,0,1:T(8,128)S(1)} %copy.260), channel_id=1, source_target_pairs={{32,0},{64,32},{96,64},{128,96},{160,128},{192,160},{224,192},{33,... | collective-permute-start | bytes 3145736 | tf_op jit(solution)/shard_map/while/body/eval_jaxpr/ppermute | solution.py:12
  148.7 16.2 %collective-permute-start = (f32[2,2,256,256]{3,2,0,1:T(8,128)S(1)}, f32[2,2,256,256]{3,2,0,1:T(8,128)}, u32[]{:S(2)}, u32[]{:S(2)}) collective-permute-start(f32[2,2,256,256]{3,2,0,1:T(8,128)S(1)} %copy.260), channel_id=1, source_target_pairs={{32,0},{64,32},{96,64},{128,96},{160,128},{192,160},{224,192},{33,... | collective-permute-start | bytes 3145736 | tf_op jit(solution)/shard_map/while/body/eval_jaxpr/ppermute | solution.py:12
  169.2 593.5 %collective-permute-start = (f32[2,2,256,256]{3,2,0,1:T(8,128)S(1)}, f32[2,2,256,256]{3,2,0,1:T(8,128)}, u32[]{:S(2)}, u32[]{:S(2)}) collective-permute-start(f32[2,2,256,256]{3,2,0,1:T(8,128)S(1)} %copy.260), channel_id=1, source_target_pairs={{32,0},{64,32},{96,64},{128,96},{160,128},{192,160},{224,192},{33,... | collective-permute-start | bytes 3145736 | tf_op jit(solution)/shard_map/while/body/eval_jaxpr/ppermute | solution.py:12
Sparse Core Ops, SparseCore 0:
  854.7 217.6 reduce-scatter.1
where the time goes:
time: 1090 us; the launch traced here: 1080 us
  waiting for transfers between devices  897 us (82%)
  matrix products  71.9 us (7%)
  local copies, waits for them, and re-layouts  33 us (3%)
  loops' own time  31.8 us (3%)
  other arithmetic  21.6 us (2%)
  between operations  14 us (1%)
    ppermute x8, waiting for transfers between devices, shifted(): lax.ppermute(value, axis, [(source, source + steps) for source in range(f...  679 us
    reduce_scatter x1, waiting for transfers between devices, on_device(): return lax.psum_scatter(scaled, 'illum', scatter_dimension=2, tiled=True)  218 us
    dot_general x48, matrix products, contract(): jnp.einsum(pattern, first_operand, second_operand, precision=HIGHEST_PREC...  71.9 us
    another operation x1, loops' own time, on_device(): _, gradient = lax.fori_loop(0, segments, turn_all, (zero_cot, zero_grad))  28.9 us
  transfers between devices with their start and end apart: 9, of which 9 were waited for; matrix products, arithmetic and copies ran while one was open for 0% of the time, Pallas kernels for 0%

commit v1 on v0

v1 whole, which is shorter than its diff:
```python
import functools

import jax
import jax.numpy as jnp
import ml_dtypes
import numpy as np
from jax import lax
from jax.experimental import pallas as pl
from jax.experimental.pallas import tpu as pltpu
from jax.sharding import PartitionSpec as P

BF16 = jnp.bfloat16
F32 = jnp.float32
VMEM = pl.BlockSpec(memory_space=pltpu.VMEM)
SMEM = pl.BlockSpec(memory_space=pltpu.SMEM)


def operator_matrices(extent):
    counter = np.arange(extent)
    frequency = np.where(counter < extent // 2, counter, counter - extent)
    factor = np.exp(-2j * np.pi * ((frequency * frequency) % 1024) / 1024)
    table = np.exp(-2j * np.pi * ((counter[:, None] * counter[None, :]) % extent) / extent)
    operator = (np.conj(table) * factor[None, :]) @ table / extent
    operator = 0.5 * (operator + operator.T)
    terms = []
    for matrix in (operator.real, operator.imag - operator.real, operator.real + operator.imag):
        high = matrix.astype(np.float32).astype(ml_dtypes.bfloat16)
        low = (matrix - high.astype(np.float64)).astype(np.float32).astype(ml_dtypes.bfloat16)
        terms.append(np.stack([high, low]))
    return np.stack(terms)


def dot(left, right):
    return jnp.dot(left, right, preferred_element_type=F32)


def split(value):
    high = value.astype(BF16)
    return high, (value - high.astype(F32)).astype(BF16)


def from_right(value, matrices, which):
    high, low = split(value)
    w_high, w_low = matrices[which, 0], matrices[which, 1]
    return dot(
        jnp.concatenate([high, low, high], axis=1), jnp.concatenate([w_high, w_high, w_low], axis=0)
    )


def from_left(value, matrices, which):
    high, low = split(value)
    w_high, w_low = matrices[which, 0], matrices[which, 1]
    return dot(
        jnp.concatenate([w_high, w_high, w_low], axis=1), jnp.concatenate([high, low, high], axis=0)
    )


def adjoint(real, imag, matrices):
    both = from_right(real + imag, matrices, 0)
    mid_real = both + from_right(imag, matrices, 1)
    mid_imag = both - from_right(real, matrices, 2)
    both = from_left(mid_real + mid_imag, matrices, 0)
    return both + from_left(mid_imag, matrices, 1), both - from_left(mid_real, matrices, 2)


def exit_body(psi, screen_real, screen_imag, measured, matrices, out):
    last = psi.shape[0] - 1
    s_real, s_imag = screen_real[last], screen_imag[last]
    f_real, f_imag = psi[last, 0], psi[last, 1]
    real, imag = adjoint(
        s_real * f_real - s_imag * f_imag, -(s_real * f_imag + s_imag * f_real), matrices
    )
    weight = 2.0 * (real * real + imag * imag - measured[...])
    out[0] = weight * real
    out[1] = -(weight * imag)


def section_body(scale, active, chi, psi, screen_real, screen_imag, matrices, grad_in, out, grad):
    count = psi.shape[0]
    on = active[0] == 1

    @pl.when(on)
    def _():
        out[...] = chi[...]

        def step(index, carry):
            slab = count - 1 - index
            real, imag = adjoint(out[0], out[1], matrices)
            p_real, p_imag = psi[slab, 0], psi[slab, 1]
            grad[slab, 0] = grad_in[slab, 0] + scale * (p_real * real + p_imag * imag)
            grad[slab, 1] = grad_in[slab, 1] + scale * (p_real * imag - p_imag * real)
            s_real, s_imag = screen_real[slab], screen_imag[slab]
            out[0] = s_real * real + s_imag * imag
            out[1] = s_real * imag - s_imag * real
            return carry

        lax.fori_loop(0, count, step, 0)

    @pl.when(jnp.logical_not(on))
    def _():
        grad[...] = grad_in[...]


def on_device(fields, screen_real, screen_imag, measured, angles, *, columns):
    slabs, lights, _, extent, _ = fields.shape
    segments = lax.axis_size("depth")
    position = lax.axis_index("depth")
    groups = lax.axis_size("illum")
    matrices = jnp.asarray(operator_matrices(extent))
    counter = jnp.arange(extent, dtype=jnp.int32)

    def ramp(shift):
        angle = 2.0 * jnp.pi / extent * ((shift[:, None] * counter) % extent).astype(F32)
        return jnp.cos(angle), jnp.sin(angle)

    x_cos, x_sin = ramp(angles % 16 - 8)
    y_cos, y_sin = ramp(angles // 16 - 8)
    fields = fields.astype(F32)

    def tilted(light):
        c_x, s_x = x_cos[light][:, None], x_sin[light][:, None]
        c_y, s_y = y_cos[light][None, :], y_sin[light][None, :]
        cos, sin = c_x * c_y - s_x * s_y, s_x * c_y + c_x * s_y
        real, imag = fields[:, light, 0], fields[:, light, 1]
        return jnp.stack([cos * real - sin * imag, cos * imag + sin * real], axis=1)

    psi = [tilted(light) for light in range(lights)]
    field_shape = jax.ShapeDtypeStruct((2, extent, extent), F32)
    grad_shape = jax.ShapeDtypeStruct((slabs, 2, extent, extent), F32)
    work = 18 * 2 * extent**3
    params = pltpu.CompilerParams(vmem_limit_bytes=24 << 20)
    exit_call = pl.pallas_call(
        exit_body,
        out_shape=field_shape,
        in_specs=[VMEM] * 5,
        out_specs=VMEM,
        compiler_params=params,
        cost_estimate=pl.CostEstimate(flops=work, bytes_accessed=1 << 20, transcendentals=0),
        name="exit",
    )
    section_call = pl.pallas_call(
        functools.partial(section_body, float(lights * groups) ** -0.5),
        out_shape=[field_shape, grad_shape],
        in_specs=[SMEM] + [VMEM] * 6,
        out_specs=[VMEM, VMEM],
        input_output_aliases={6: 1},
        compiler_params=params,
        cost_estimate=pl.CostEstimate(
            flops=slabs * work, bytes_accessed=1 << 20, transcendentals=0
        ),
        name="section",
    )
    state = [
        exit_call(psi[light], screen_real, screen_imag, measured[light], matrices)
        for light in range(lights)
    ]
    grad = jnp.zeros(grad_shape.shape, F32)
    for turn in range(segments):
        source = segments - 1 - turn
        active = (position == source).astype(jnp.int32)[None]
        for light in range(lights):
            left, grad = section_call(
                active, state[light], psi[light], screen_real, screen_imag, matrices, grad
            )
            if source > 0:
                state[light] = lax.ppermute(left, "depth", [(source, source - 1)])

    rows = extent // groups
    inner = groups // columns
    here = lax.axis_index("illum")
    here_x, here_z = here // inner, here % inner

    def block(value, start, size):
        return lax.dynamic_slice_in_dim(value, start, size, axis=2)

    wide = rows * inner
    total = block(grad, here_x * wide, wide)
    for step in range(1, columns):
        pairs = [
            (x * inner + z, (x + step) % columns * inner + z)
            for x in range(columns)
            for z in range(inner)
        ]
        sent = block(grad, (here_x + step) % columns * wide, wide)
        total = total + lax.ppermute(sent, "illum", pairs)
    result = block(total, here_z * rows, rows)
    for step in range(1, inner):
        pairs = [
            (x * inner + z, x * inner + (z + step) % inner)
            for x in range(columns)
            for z in range(inner)
        ]
        sent = block(total, (here_z + step) % inner * rows, rows)
        result = result + lax.ppermute(sent, "illum", pairs)
    return result


def solution(mesh):
    illums = mesh.shape["illum"]
    columns = 4 if illums % 4 == 0 else 1
    return jax.shard_map(
        functools.partial(on_device, columns=columns),
        mesh=mesh,
        in_specs=(
            P("depth", "illum", None, None, None),
            P("depth", None, None),
            P("depth", None, None),
            P("illum", None, None),
            P("illum"),
        ),
        out_specs=P("depth", None, "illum", None),
        check_vma=False,
    )
```

time: 1090 us -> 171 us (0.16)
  waiting for transfers between devices: 897 us -> 55.4 us
  matrix products: 71.9 us -> 0 us
  Pallas kernels: 0 us -> 41.1 us
  loops' own time: 31.8 us -> 0 us
  starting transfers between devices: 10.3 us -> 41 us
  other arithmetic: 21.6 us -> 4.57 us
  between operations: 14 us -> 0.38 us
    ppermute x8 -> x24, waiting for transfers between devices: 679 us -> 55.4 us  [the longest x14 32 us: on_device(): state[light] = lax.ppermute(left, 'depth', [(source, source - 1)])]
    reduce_scatter x1 -> x0, waiting for transfers between devices: 218 us -> none  [on_device(): return lax.psum_scatter(scaled, 'illum', scatter_dimension=2, tiled=True)]
    dot_general x48 -> x0, matrix products: 71.9 us -> none  [contract(): jnp.einsum(pattern, first_operand, second_operand, precision=HIGHEST_PREC...]
    pallas_call x0 -> x18, Pallas kernels: none -> 41.1 us  [the longest x16 38.8 us: on_device(): section_call(active, state[light], psi[light], screen_real, screen_imag,...]
    another operation x10 -> x0, loops' own time: 31.8 us -> none  [the longest x1 28.9 us: on_device(): _, gradient = lax.fori_loop(0, segments, turn_all, (zero_cot, zero_grad))]
    ppermute x8 -> x24, starting transfers between devices: 10.3 us -> 41 us  [the longest x14 20.1 us: on_device(): state[light] = lax.ppermute(left, 'depth', [(source, source - 1)])]
    unnamed x7 -> x68, local copies, waits for them, and re-layouts: 6.14 us -> 25.3 us
    while x9 -> x0, local copies, waits for them, and re-layouts: 12.9 us -> none
  transfers between devices with their start and end apart: 9 -> 24, of which waited for: 9 -> 7; matrix products, arithmetic and copies ran while one was open for 0% -> 0% of each run, Pallas kernels for 0% -> 20%
where the time goes in v1:
time: 171 us; the launch traced here: 168 us
  waiting for transfers between devices  55.4 us (32%)
  Pallas kernels  41.1 us (24%)
  starting transfers between devices  41 us (24%)
  local copies, waits for them, and re-layouts  25.7 us (15%)
  other arithmetic  4.57 us (3%)
    pallas_call x16, Pallas kernels, on_device(): section_call(active, state[light], psi[light], screen_real, screen_imag,...  38.8 us
    ppermute x14, waiting for transfers between devices, on_device(): state[light] = lax.ppermute(left, 'depth', [(source, source - 1)])  32 us
    unnamed x68, local copies, waits for them, and re-layouts  25.3 us
    ppermute x14, starting transfers between devices, on_device(): state[light] = lax.ppermute(left, 'depth', [(source, source - 1)])  20.1 us
    ppermute x3, waiting for transfers between devices, on_device(): total = total + lax.ppermute(sent, 'illum', pairs)  18.5 us
    ppermute x7, starting transfers between devices, on_device(): result = result + lax.ppermute(sent, 'illum', pairs)  16.3 us
    ppermute x7, waiting for transfers between devices, on_device(): result = result + lax.ppermute(sent, 'illum', pairs)  4.83 us
    ppermute x3, starting transfers between devices, on_device(): total = total + lax.ppermute(sent, 'illum', pairs)  4.53 us
  transfers between devices with their start and end apart: 24, of which 7 were waited for; matrix products, arithmetic and copies ran while one was open for 0% of the time, Pallas kernels for 20%

profile of v1, /device:TPU:32, one launch (start us, length us, event | category | flops | bytes accessed | tf_op | source)
XLA Modules:
  0.0 168.1 jit_solution(13499067612786473239)
XLA Ops:
  0.0 1.8 %copy_convert_fusion = f32[3,2,2,256,256]{4,3,0,2,1:T(8,128)S(1)} fusion(bf16[3,2,2,256,256]{4,3,2,1,0:T(8,128)(2,1)} %param.6), kind=kLoop, calls=%fused_computation.2 | loop fusion | flops 786432 | bytes 4718592 | tf_op jit(solution)/shard_map/convert_element_type | solution.py:118
  4.2 1.1 exit.3.chi
  6.5 1.5 collective-permute-start.1
  8.4 1.2 exit.2.chi
  10.6 1.5 collective-permute-start
  12.0 1.1 copy-done.9
  13.2 1.1 copy-done.17
  15.4 2.2 %section.18 = (f32[2,256,256]{2,1,0:T(8,128)}, f32[3,2,256,256]{3,2,1,0:T(8,128)S(1)}) custom-call(s32[1]{0:T(128)} %bitcast.6.active, f32[2,256,256]{2,1,0:T(8,128)} %collective-permute-done.1.chi, f32[3,2,256,256]{3,2,1,0:T(8,128)S(1)} %copy.24.psi, f32[3,256,256]{2,1,0:T(8,128)S(1)} %copy-done.9, ...), custom_call_target="tpu_custom_call", output_to_operand_aliasing={{1}: (6, {})} | custom-call | flops 1811939328 | bytes 1048576 | tf_op jit(solution)/shard_map/section/pallas_call | solution.py:162
  17.6 1.5 collective-permute-start.3
  19.1 2.0 %section.19 = (f32[2,256,256]{2,1,0:T(8,128)}, f32[3,2,256,256]{3,2,1,0:T(8,128)S(1)}) custom-call(s32[1]{0:T(128)} %bitcast.6.active, f32[2,256,256]{2,1,0:T(8,128)} %collective-permute-done.chi, f32[3,2,256,256]{3,2,1,0:T(8,128)S(1)} %copy-done.1, f32[3,256,256]{2,1,0:T(8,128)S(1)} %copy-done.9, ...), custom_call_target="tpu_custom_call", output_to_operand_aliasing={{1}: (6, {})} | custom-call | flops 1811939328 | bytes 1048576 | tf_op jit(solution)/shard_map/section/pallas_call | solution.py:162
  21.1 1.5 collective-permute-start.2
  22.6 1.1 copy-done.10
  23.7 1.1 copy-done.18
  26.0 2.2 %section.20 = (f32[2,256,256]{2,1,0:T(8,128)}, f32[3,2,256,256]{3,2,1,0:T(8,128)S(1)}) custom-call(s32[1]{0:T(128)} %bitcast.5.active, f32[2,256,256]{2,1,0:T(8,128)} %collective-permute-done.3.chi, f32[3,2,256,256]{3,2,1,0:T(8,128)S(1)} %copy.24.psi, f32[3,256,256]{2,1,0:T(8,128)S(1)} %copy-done.10, ...), custom_call_target="tpu_custom_call", output_to_operand_aliasing={{1}: (6, {})} | custom-call | flops 1811939328 | bytes 1048576 | tf_op jit(solution)/shard_map/section/pallas_call | solution.py:162
  28.1 1.5 collective-permute-start.5
  29.6 2.0 %section.21 = (f32[2,256,256]{2,1,0:T(8,128)}, f32[3,2,256,256]{3,2,1,0:T(8,128)S(1)}) custom-call(s32[1]{0:T(128)} %bitcast.5.active, f32[2,256,256]{2,1,0:T(8,128)} %collective-permute-done.2.chi, f32[3,2,256,256]{3,2,1,0:T(8,128)S(1)} %copy-done.2, f32[3,256,256]{2,1,0:T(8,128)S(1)} %copy-done.10, ...), custom_call_target="tpu_custom_call", output_to_operand_aliasing={{1}: (6, {})} | custom-call | flops 1811939328 | bytes 1048576 | tf_op jit(solution)/shard_map/section/pallas_call | solution.py:162
  31.6 1.5 collective-permute-start.4
  33.1 1.1 copy-done.11
  36.5 2.2 %section.22 = (f32[2,256,256]{2,1,0:T(8,128)}, f32[3,2,256,256]{3,2,1,0:T(8,128)S(1)}) custom-call(s32[1]{0:T(128)} %bitcast.4.active, f32[2,256,256]{2,1,0:T(8,128)} %collective-permute-done.5.chi, f32[3,2,256,256]{3,2,1,0:T(8,128)S(1)} %copy.24.psi, f32[3,256,256]{2,1,0:T(8,128)S(1)} %copy-done.11, ...), custom_call_target="tpu_custom_call", output_to_operand_aliasing={{1}: (6, {})} | custom-call | flops 1811939328 | bytes 1048576 | tf_op jit(solution)/shard_map/section/pallas_call | solution.py:162
  38.7 1.5 collective-permute-start.7
  40.1 2.0 %section.23 = (f32[2,256,256]{2,1,0:T(8,128)}, f32[3,2,256,256]{3,2,1,0:T(8,128)S(1)}) custom-call(s32[1]{0:T(128)} %bitcast.4.active, f32[2,256,256]{2,1,0:T(8,128)} %collective-permute-done.4.chi, f32[3,2,256,256]{3,2,1,0:T(8,128)S(1)} %copy-done.3, f32[3,256,256]{2,1,0:T(8,128)S(1)} %copy-done.11, ...), custom_call_target="tpu_custom_call", output_to_operand_aliasing={{1}: (6, {})} | custom-call | flops 1811939328 | bytes 1048576 | tf_op jit(solution)/shard_map/section/pallas_call | solution.py:162
  42.2 1.5 collective-permute-start.6
  43.6 1.1 copy-done.12
  47.0 2.2 %section.24 = (f32[2,256,256]{2,1,0:T(8,128)}, f32[3,2,256,256]{3,2,1,0:T(8,128)S(1)}) custom-call(s32[1]{0:T(128)} %bitcast.3.active, f32[2,256,256]{2,1,0:T(8,128)} %collective-permute-done.7.chi, f32[3,2,256,256]{3,2,1,0:T(8,128)S(1)} %copy.24.psi, f32[3,256,256]{2,1,0:T(8,128)S(1)} %copy-done.12, ...), custom_call_target="tpu_custom_call", output_to_operand_aliasing={{1}: (6, {})} | custom-call | flops 1811939328 | bytes 1048576 | tf_op jit(solution)/shard_map/section/pallas_call | solution.py:162
  49.2 1.5 collective-permute-start.9
  50.7 2.0 %section.25 = (f32[2,256,256]{2,1,0:T(8,128)}, f32[3,2,256,256]{3,2,1,0:T(8,128)S(1)}) custom-call(s32[1]{0:T(128)} %bitcast.3.active, f32[2,256,256]{2,1,0:T(8,128)} %collective-permute-done.6.chi, f32[3,2,256,256]{3,2,1,0:T(8,128)S(1)} %copy-done.4, f32[3,256,256]{2,1,0:T(8,128)S(1)} %copy-done.12, ...), custom_call_target="tpu_custom_call", output_to_operand_aliasing={{1}: (6, {})} | custom-call | flops 1811939328 | bytes 1048576 | tf_op jit(solution)/shard_map/section/pallas_call | solution.py:162
  52.7 1.5 collective-permute-start.8
  54.2 1.1 copy-done.13
  57.6 2.2 %section.26 = (f32[2,256,256]{2,1,0:T(8,128)}, f32[3,2,256,256]{3,2,1,0:T(8,128)S(1)}) custom-call(s32[1]{0:T(128)} %bitcast.2.active, f32[2,256,256]{2,1,0:T(8,128)} %collective-permute-done.9.chi, f32[3,2,256,256]{3,2,1,0:T(8,128)S(1)} %copy.24.psi, f32[3,256,256]{2,1,0:T(8,128)S(1)} %copy-done.13, ...), custom_call_target="tpu_custom_call", output_to_operand_aliasing={{1}: (6, {})} | custom-call | flops 1811939328 | bytes 1048576 | tf_op jit(solution)/shard_map/section/pallas_call | solution.py:162
  59.7 1.5 collective-permute-start.11
  61.2 2.0 %section.27 = (f32[2,256,256]{2,1,0:T(8,128)}, f32[3,2,256,256]{3,2,1,0:T(8,128)S(1)}) custom-call(s32[1]{0:T(128)} %bitcast.2.active, f32[2,256,256]{2,1,0:T(8,128)} %collective-permute-done.8.chi, f32[3,2,256,256]{3,2,1,0:T(8,128)S(1)} %copy-done.5, f32[3,256,256]{2,1,0:T(8,128)S(1)} %copy-done.13, ...), custom_call_target="tpu_custom_call", output_to_operand_aliasing={{1}: (6, {})} | custom-call | flops 1811939328 | bytes 1048576 | tf_op jit(solution)/shard_map/section/pallas_call | solution.py:162
  63.2 1.5 collective-permute-start.10
  64.7 1.1 copy-done.14
  68.1 2.2 %section.28 = (f32[2,256,256]{2,1,0:T(8,128)}, f32[3,2,256,256]{3,2,1,0:T(8,128)S(1)}) custom-call(s32[1]{0:T(128)} %bitcast.1.active, f32[2,256,256]{2,1,0:T(8,128)} %collective-permute-done.11.chi, f32[3,2,256,256]{3,2,1,0:T(8,128)S(1)} %copy.24.psi, f32[3,256,256]{2,1,0:T(8,128)S(1)} %copy-done.14, ...), custom_call_target="tpu_custom_call", output_to_operand_aliasing={{1}: (6, {})} | custom-call | flops 1811939328 | bytes 1048576 | tf_op jit(solution)/shard_map/section/pallas_call | solution.py:162
  70.3 1.3 collective-permute-start.13
  71.6 2.0 %section.29 = (f32[2,256,256]{2,1,0:T(8,128)}, f32[3,2,256,256]{3,2,1,0:T(8,128)S(1)}) custom-call(s32[1]{0:T(128)} %bitcast.1.active, f32[2,256,256]{2,1,0:T(8,128)} %collective-permute-done.10.chi, f32[3,2,256,256]{3,2,1,0:T(8,128)S(1)} %copy-done.6, f32[3,256,256]{2,1,0:T(8,128)S(1)} %copy-done.14, ...), custom_call_target="tpu_custom_call", output_to_operand_aliasing={{1}: (6, {})} | custom-call | flops 1811939328 | bytes 1048576 | tf_op jit(solution)/shard_map/section/pallas_call | solution.py:162
  73.6 1.3 collective-permute-start.12
  75.0 32.0 %collective-permute-done.13.chi = f32[2,256,256]{2,1,0:T(8,128)} collective-permute-done((f32[2,256,256]{2,1,0:T(8,128)}, f32[2,256,256]{2,1,0:T(8,128)}, u32[]{:S(2)}, u32[]{:S(2)}) %collective-permute-start.13) | collective-permute-done | bytes 524320 | tf_op jit(solution)/shard_map/ppermute | solution.py:166
  107.0 1.1 copy-done.15
  110.4 6.0 %section.30 = (f32[2,256,256]{2,1,0:T(8,128)}, f32[3,2,256,256]{3,2,1,0:T(8,128)S(1)}) custom-call(s32[1]{0:T(128)} %bitcast.active, f32[2,256,256]{2,1,0:T(8,128)} %collective-permute-done.13.chi, f32[3,2,256,256]{3,2,1,0:T(8,128)S(1)} %copy.24.psi, f32[3,256,256]{2,1,0:T(8,128)S(1)} %copy-done.15, ...), custom_call_target="tpu_custom_call", output_to_operand_aliasing={{1}: (6, {})} | custom-call | flops 1811939328 | bytes 1048576 | tf_op jit(solution)/shard_map/section/pallas_call | solution.py:162
  116.4 5.6 %section.31 = (f32[2,256,256]{2,1,0:T(8,128)}, f32[3,2,256,256]{3,2,1,0:T(8,128)S(1)}) custom-call(s32[1]{0:T(128)} %bitcast.active, f32[2,256,256]{2,1,0:T(8,128)} %collective-permute-done.12.chi, f32[3,2,256,256]{3,2,1,0:T(8,128)S(1)} %copy-done.7, f32[3,256,256]{2,1,0:T(8,128)S(1)} %copy-done.15, ...), custom_call_target="tpu_custom_call", output_to_operand_aliasing={{1}: (6, {})} | custom-call | flops 1811939328 | bytes 1048576 | tf_op jit(solution)/shard_map/section/pallas_call | solution.py:162
  122.1 2.9 %collective-permute-start.16 = (f32[3,2,64,256]{3,2,1,0:T(8,128)S(1)}, f32[3,2,64,256]{3,2,1,0:T(8,128)S(1)}, u32[]{:S(2)}, u32[]{:S(2)}) collective-permute-start(f32[3,2,64,256]{3,2,1,0:T(8,128)S(1)} %get-tuple-element.70), channel_id=1, source_target_pairs={{0,24},{1,25},{2,26},{3,27},{4,28},{5,29},{6,30},{7,31},{8,0},{9,1... | collective-permute-start | bytes 1179656 | tf_op jit(solution)/shard_map/ppermute | solution.py:185
  126.7 14.7 %collective-permute-done.16 = f32[3,2,64,256]{3,2,1,0:T(8,128)S(1)} collective-permute-done((f32[3,2,64,256]{3,2,1,0:T(8,128)S(1)}, f32[3,2,64,256]{3,2,1,0:T(8,128)S(1)}, u32[]{:S(2)}, u32[]{:S(2)}) %collective-permute-start.16) | collective-permute-done | bytes 393248 | tf_op jit(solution)/shard_map/ppermute | solution.py:185
  141.4 3.8 %collective-permute-done.14 = f32[3,2,64,256]{3,2,1,0:T(8,128)} collective-permute-done((f32[3,2,64,256]{3,2,1,0:T(8,128)S(1)}, f32[3,2,64,256]{3,2,1,0:T(8,128)}, u32[]{:S(2)}, u32[]{:S(2)}) %collective-permute-start.14) | collective-permute-done | bytes 393248 | tf_op jit(solution)/shard_map/ppermute | solution.py:185
  146.5 6.3 %collective-permute-start.22 = (f32[3,2,8,256]{3,2,1,0:T(8,128)S(1)}, f32[3,2,8,256]{3,2,1,0:T(8,128)S(1)}, u32[]{:S(2)}, u32[]{:S(2)}) collective-permute-start(f32[3,2,8,256]{3,2,1,0:T(8,128)S(1)} %get-tuple-element.76), channel_id=1, source_target_pairs={{0,6},{1,7},{2,0},{3,1},{4,2},{5,3},{6,4},{7,5},{8,14},{9,15},{10,... | collective-permute-start | bytes 147464 | tf_op jit(solution)/shard_map/ppermute | solution.py:194
  153.8 4.5 %collective-permute-start.20 = (f32[3,2,8,256]{3,2,1,0:T(8,128)S(1)}, f32[3,2,8,256]{3,2,1,0:T(8,128)S(1)}, u32[]{:S(2)}, u32[]{:S(2)}) collective-permute-start(f32[3,2,8,256]{3,2,1,0:T(8,128)S(1)} %get-tuple-element.78), channel_id=1, source_target_pairs={{0,4},{1,5},{2,6},{3,7},{4,0},{5,1},{6,2},{7,3},{8,12},{9,13},{10,... | collective-permute-start | bytes 147464 | tf_op jit(solution)/shard_map/ppermute | solution.py:194
  158.7 2.9 %collective-permute-start.18 = (f32[3,2,8,256]{3,2,1,0:T(8,128)S(1)}, f32[3,2,8,256]{3,2,1,0:T(8,128)S(1)}, u32[]{:S(2)}, u32[]{:S(2)}) collective-permute-start(f32[3,2,8,256]{3,2,1,0:T(8,128)S(1)} %get-tuple-element.80), channel_id=1, source_target_pairs={{0,2},{1,3},{2,4},{3,5},{4,6},{5,7},{6,0},{7,1},{8,10},{9,11},{10,... | collective-permute-start | bytes 147464 | tf_op jit(solution)/shard_map/ppermute | solution.py:194
  162.9 3.6 %collective-permute-done.19 = f32[3,2,8,256]{3,2,1,0:T(8,128)S(1)} collective-permute-done((f32[3,2,8,256]{3,2,1,0:T(8,128)S(1)}, f32[3,2,8,256]{3,2,1,0:T(8,128)S(1)}, u32[]{:S(2)}, u32[]{:S(2)}) %collective-permute-start.19) | collective-permute-done | bytes 49184 | tf_op jit(solution)/shard_map/ppermute | solution.py:194
  (106 shorter events, 25.9 us)
Async XLA Ops:
  0.0 1.8 %copy-start.33 = (s32[2]{0:T(128)S(1)}, s32[2]{0:T(128)}, u32[]{:S(2)}) copy-start(s32[2]{0:T(128)} %param.10) | copy-start | bytes 28
  0.0 2.0 %copy-start.32 = (f32[2,256,256]{2,1,0:T(8,128)S(1)}, f32[2,256,256]{2,1,0:T(8,128)}, u32[]{:S(2)}) copy-start(f32[2,256,256]{2,1,0:T(8,128)} %param.9) | copy-start | bytes 1572868
  2.6 1.1 copy-start.8
  2.6 1.4 copy-start.16
  2.6 1.6 copy-start.24
  6.5 5.6 %collective-permute-start.1 = (f32[2,256,256]{2,1,0:T(8,128)}, f32[2,256,256]{2,1,0:T(8,128)}, u32[]{:S(2)}, u32[]{:S(2)}) collective-permute-start(f32[2,256,256]{2,1,0:T(8,128)} %get-tuple-element.37), channel_id=1, source_target_pairs={{224,192},{225,193},{226,194},{227,195},{228,196},{229,197},{230,1... | collective-permute-start | bytes 1572872 | tf_op jit(solution)/shard_map/ppermute | solution.py:166
  8.4 1.2 copy-start
  10.6 8.5 %collective-permute-start = (f32[2,256,256]{2,1,0:T(8,128)}, f32[2,256,256]{2,1,0:T(8,128)}, u32[]{:S(2)}, u32[]{:S(2)}) collective-permute-start(f32[2,256,256]{2,1,0:T(8,128)} %get-tuple-element.36), channel_id=1, source_target_pairs={{224,192},{225,193},{226,194},{227,195},{228,196},{229,197},{230,1... | collective-permute-start | bytes 1572872 | tf_op jit(solution)/shard_map/ppermute | solution.py:166
  12.0 1.1 copy-start.9
  13.2 1.1 copy-start.17
  14.3 1.1 copy-start.25
  15.4 3.6 %copy-start.1 = (f32[3,2,256,256]{3,2,1,0:T(8,128)S(1)}, f32[3,2,256,256]{3,2,1,0:T(8,128)}, u32[]{:S(2)}) copy-start(f32[3,2,256,256]{3,2,1,0:T(8,128)} %copy-done) | copy-start | bytes 4718596
  17.6 5.0 %collective-permute-start.3 = (f32[2,256,256]{2,1,0:T(8,128)}, f32[2,256,256]{2,1,0:T(8,128)}, u32[]{:S(2)}, u32[]{:S(2)}) collective-permute-start(f32[2,256,256]{2,1,0:T(8,128)} %get-tuple-element.41), channel_id=1, source_target_pairs={{192,160},{193,161},{194,162},{195,163},{196,164},{197,165},{198,1... | collective-permute-start | bytes 1572872 | tf_op jit(solution)/shard_map/ppermute | solution.py:166
  21.1 8.5 %collective-permute-start.2 = (f32[2,256,256]{2,1,0:T(8,128)}, f32[2,256,256]{2,1,0:T(8,128)}, u32[]{:S(2)}, u32[]{:S(2)}) collective-permute-start(f32[2,256,256]{2,1,0:T(8,128)} %get-tuple-element.40), channel_id=1, source_target_pairs={{192,160},{193,161},{194,162},{195,163},{196,164},{197,165},{198,1... | collective-permute-start | bytes 1572872 | tf_op jit(solution)/shard_map/ppermute | solution.py:166
  22.6 1.1 copy-start.10
  23.7 1.1 copy-start.18
  24.8 1.1 copy-start.26
  26.0 3.6 %copy-start.2 = (f32[3,2,256,256]{3,2,1,0:T(8,128)S(1)}, f32[3,2,256,256]{3,2,1,0:T(8,128)}, u32[]{:S(2)}) copy-start(f32[3,2,256,256]{3,2,1,0:T(8,128)} %copy-done) | copy-start | bytes 4718596
  28.1 5.0 %collective-permute-start.5 = (f32[2,256,256]{2,1,0:T(8,128)}, f32[2,256,256]{2,1,0:T(8,128)}, u32[]{:S(2)}, u32[]{:S(2)}) collective-permute-start(f32[2,256,256]{2,1,0:T(8,128)} %get-tuple-element.45), channel_id=1, source_target_pairs={{160,128},{161,129},{162,130},{163,131},{164,132},{165,133},{166,1... | collective-permute-start | bytes 1572872 | tf_op jit(solution)/shard_map/ppermute | solution.py:166
  31.6 8.5 %collective-permute-start.4 = (f32[2,256,256]{2,1,0:T(8,128)}, f32[2,256,256]{2,1,0:T(8,128)}, u32[]{:S(2)}, u32[]{:S(2)}) collective-permute-start(f32[2,256,256]{2,1,0:T(8,128)} %get-tuple-element.44), channel_id=1, source_target_pairs={{160,128},{161,129},{162,130},{163,131},{164,132},{165,133},{166,1... | collective-permute-start | bytes 1572872 | tf_op jit(solution)/shard_map/ppermute | solution.py:166
  33.1 1.1 copy-start.11
  36.5 3.6 %copy-start.3 = (f32[3,2,256,256]{3,2,1,0:T(8,128)S(1)}, f32[3,2,256,256]{3,2,1,0:T(8,128)}, u32[]{:S(2)}) copy-start(f32[3,2,256,256]{3,2,1,0:T(8,128)} %copy-done) | copy-start | bytes 4718596
  38.7 5.0 %collective-permute-start.7 = (f32[2,256,256]{2,1,0:T(8,128)}, f32[2,256,256]{2,1,0:T(8,128)}, u32[]{:S(2)}, u32[]{:S(2)}) collective-permute-start(f32[2,256,256]{2,1,0:T(8,128)} %get-tuple-element.49), channel_id=1, source_target_pairs={{128,96},{129,97},{130,98},{131,99},{132,100},{133,101},{134,102},... | collective-permute-start | bytes 1572872 | tf_op jit(solution)/shard_map/ppermute | solution.py:166
  42.2 8.5 %collective-permute-start.6 = (f32[2,256,256]{2,1,0:T(8,128)}, f32[2,256,256]{2,1,0:T(8,128)}, u32[]{:S(2)}, u32[]{:S(2)}) collective-permute-start(f32[2,256,256]{2,1,0:T(8,128)} %get-tuple-element.48), channel_id=1, source_target_pairs={{128,96},{129,97},{130,98},{131,99},{132,100},{133,101},{134,102},... | collective-permute-start | bytes 1572872 | tf_op jit(solution)/shard_map/ppermute | solution.py:166
  43.6 1.1 copy-start.12
  47.0 3.6 %copy-start.4 = (f32[3,2,256,256]{3,2,1,0:T(8,128)S(1)}, f32[3,2,256,256]{3,2,1,0:T(8,128)}, u32[]{:S(2)}) copy-start(f32[3,2,256,256]{3,2,1,0:T(8,128)} %copy-done) | copy-start | bytes 4718596
  49.2 5.0 %collective-permute-start.9 = (f32[2,256,256]{2,1,0:T(8,128)}, f32[2,256,256]{2,1,0:T(8,128)}, u32[]{:S(2)}, u32[]{:S(2)}) collective-permute-start(f32[2,256,256]{2,1,0:T(8,128)} %get-tuple-element.53), channel_id=1, source_target_pairs={{96,64},{97,65},{98,66},{99,67},{100,68},{101,69},{102,70},{103,71... | collective-permute-start | bytes 1572872 | tf_op jit(solution)/shard_map/ppermute | solution.py:166
  52.7 8.5 %collective-permute-start.8 = (f32[2,256,256]{2,1,0:T(8,128)}, f32[2,256,256]{2,1,0:T(8,128)}, u32[]{:S(2)}, u32[]{:S(2)}) collective-permute-start(f32[2,256,256]{2,1,0:T(8,128)} %get-tuple-element.52), channel_id=1, source_target_pairs={{96,64},{97,65},{98,66},{99,67},{100,68},{101,69},{102,70},{103,71... | collective-permute-start | bytes 1572872 | tf_op jit(solution)/shard_map/ppermute | solution.py:166
  54.2 1.1 copy-start.13
  57.6 3.6 %copy-start.5 = (f32[3,2,256,256]{3,2,1,0:T(8,128)S(1)}, f32[3,2,256,256]{3,2,1,0:T(8,128)}, u32[]{:S(2)}) copy-start(f32[3,2,256,256]{3,2,1,0:T(8,128)} %copy-done) | copy-start | bytes 4718596
  59.7 5.0 %collective-permute-start.11 = (f32[2,256,256]{2,1,0:T(8,128)}, f32[2,256,256]{2,1,0:T(8,128)}, u32[]{:S(2)}, u32[]{:S(2)}) collective-permute-start(f32[2,256,256]{2,1,0:T(8,128)} %get-tuple-element.57), channel_id=1, source_target_pairs={{64,32},{65,33},{66,34},{67,35},{68,36},{69,37},{70,38},{71,39},{7... | collective-permute-start | bytes 1572872 | tf_op jit(solution)/shard_map/ppermute | solution.py:166
  63.2 8.3 %collective-permute-start.10 = (f32[2,256,256]{2,1,0:T(8,128)}, f32[2,256,256]{2,1,0:T(8,128)}, u32[]{:S(2)}, u32[]{:S(2)}) collective-permute-start(f32[2,256,256]{2,1,0:T(8,128)} %get-tuple-element.56), channel_id=1, source_target_pairs={{64,32},{65,33},{66,34},{67,35},{68,36},{69,37},{70,38},{71,39},{7... | collective-permute-start | bytes 1572872 | tf_op jit(solution)/shard_map/ppermute | solution.py:166
  64.7 1.1 copy-start.14
  68.1 3.5 %copy-start.6 = (f32[3,2,256,256]{3,2,1,0:T(8,128)S(1)}, f32[3,2,256,256]{3,2,1,0:T(8,128)}, u32[]{:S(2)}) copy-start(f32[3,2,256,256]{3,2,1,0:T(8,128)} %copy-done) | copy-start | bytes 4718596
  70.3 36.7 %collective-permute-start.13 = (f32[2,256,256]{2,1,0:T(8,128)}, f32[2,256,256]{2,1,0:T(8,128)}, u32[]{:S(2)}, u32[]{:S(2)}) collective-permute-start(f32[2,256,256]{2,1,0:T(8,128)} %get-tuple-element.61), channel_id=1, source_target_pairs={{32,0},{33,1},{34,2},{35,3},{36,4},{37,5},{38,6},{39,7},{40,8},{41... | collective-permute-start | bytes 1572872 | tf_op jit(solution)/shard_map/ppermute | solution.py:166
  73.6 42.8 %collective-permute-start.12 = (f32[2,256,256]{2,1,0:T(8,128)}, f32[2,256,256]{2,1,0:T(8,128)}, u32[]{:S(2)}, u32[]{:S(2)}) collective-permute-start(f32[2,256,256]{2,1,0:T(8,128)} %get-tuple-element.60), channel_id=1, source_target_pairs={{32,0},{33,1},{34,2},{35,3},{36,4},{37,5},{38,6},{39,7},{40,8},{41... | collective-permute-start | bytes 1572872 | tf_op jit(solution)/shard_map/ppermute | solution.py:166
  107.0 1.1 copy-start.15
  110.4 6.0 %copy-start.7 = (f32[3,2,256,256]{3,2,1,0:T(8,128)S(1)}, f32[3,2,256,256]{3,2,1,0:T(8,128)}, u32[]{:S(2)}) copy-start(f32[3,2,256,256]{3,2,1,0:T(8,128)} %copy-done) | copy-start | bytes 4718596
  122.1 19.3 %collective-permute-start.16 = (f32[3,2,64,256]{3,2,1,0:T(8,128)S(1)}, f32[3,2,64,256]{3,2,1,0:T(8,128)S(1)}, u32[]{:S(2)}, u32[]{:S(2)}) collective-permute-start(f32[3,2,64,256]{3,2,1,0:T(8,128)S(1)} %get-tuple-element.70), channel_id=1, source_target_pairs={{0,24},{1,25},{2,26},{3,27},{4,28},{5,29},{6,30},{7,31},{8,0},{9,1... | collective-permute-start | bytes 1179656 | tf_op jit(solution)/shard_map/ppermute | solution.py:185
  125.0 16.4 %collective-permute-start.15 = (f32[3,2,64,256]{3,2,1,0:T(8,128)S(1)}, f32[3,2,64,256]{3,2,1,0:T(8,128)S(1)}, u32[]{:S(2)}, u32[]{:S(2)}) collective-permute-start(f32[3,2,64,256]{3,2,1,0:T(8,128)S(1)} %get-tuple-element.71), channel_id=1, source_target_pairs={{0,16},{1,17},{2,18},{3,19},{4,20},{5,21},{6,22},{7,23},{8,24},{9,... | collective-permute-start | bytes 1179656 | tf_op jit(solution)/shard_map/ppermute | solution.py:185
  125.8 19.4 %collective-permute-start.14 = (f32[3,2,64,256]{3,2,1,0:T(8,128)S(1)}, f32[3,2,64,256]{3,2,1,0:T(8,128)}, u32[]{:S(2)}, u32[]{:S(2)}) collective-permute-start(f32[3,2,64,256]{3,2,1,0:T(8,128)S(1)} %get-tuple-element.69), channel_id=1, source_target_pairs={{0,8},{1,9},{2,10},{3,11},{4,12},{5,13},{6,14},{7,15},{8,16},{9,17... | collective-permute-start | bytes 1179656 | tf_op jit(solution)/shard_map/ppermute | solution.py:185
  146.3 12.4 %collective-permute-start.23 = (f32[3,2,8,256]{3,2,1,0:T(8,128)S(1)}, f32[3,2,8,256]{3,2,1,0:T(8,128)S(1)}, u32[]{:S(2)}, u32[]{:S(2)}) collective-permute-start(f32[3,2,8,256]{3,2,1,0:T(8,128)S(1)} %get-tuple-element.75), channel_id=1, source_target_pairs={{0,7},{1,0},{2,1},{3,2},{4,3},{5,4},{6,5},{7,6},{8,15},{9,8},{10,9... | collective-permute-start | bytes 147464 | tf_op jit(solution)/shard_map/ppermute | solution.py:194
  146.5 15.2 %collective-permute-start.22 = (f32[3,2,8,256]{3,2,1,0:T(8,128)S(1)}, f32[3,2,8,256]{3,2,1,0:T(8,128)S(1)}, u32[]{:S(2)}, u32[]{:S(2)}) collective-permute-start(f32[3,2,8,256]{3,2,1,0:T(8,128)S(1)} %get-tuple-element.76), channel_id=1, source_target_pairs={{0,6},{1,7},{2,0},{3,1},{4,2},{5,3},{6,4},{7,5},{8,14},{9,15},{10,... | collective-permute-start | bytes 147464 | tf_op jit(solution)/shard_map/ppermute | solution.py:194
  152.8 10.1 %collective-permute-start.21 = (f32[3,2,8,256]{3,2,1,0:T(8,128)S(1)}, f32[3,2,8,256]{3,2,1,0:T(8,128)S(1)}, u32[]{:S(2)}, u32[]{:S(2)}) collective-permute-start(f32[3,2,8,256]{3,2,1,0:T(8,128)S(1)} %get-tuple-element.77), channel_id=1, source_target_pairs={{0,5},{1,6},{2,7},{3,0},{4,1},{5,2},{6,3},{7,4},{8,13},{9,14},{10,... | collective-permute-start | bytes 147464 | tf_op jit(solution)/shard_map/ppermute | solution.py:194
  153.8 9.1 %collective-permute-start.20 = (f32[3,2,8,256]{3,2,1,0:T(8,128)S(1)}, f32[3,2,8,256]{3,2,1,0:T(8,128)S(1)}, u32[]{:S(2)}, u32[]{:S(2)}) collective-permute-start(f32[3,2,8,256]{3,2,1,0:T(8,128)S(1)} %get-tuple-element.78), channel_id=1, source_target_pairs={{0,4},{1,5},{2,6},{3,7},{4,0},{5,1},{6,2},{7,3},{8,12},{9,13},{10,... | collective-permute-start | bytes 147464 | tf_op jit(solution)/shard_map/ppermute | solution.py:194
  158.3 8.2 %collective-permute-start.19 = (f32[3,2,8,256]{3,2,1,0:T(8,128)S(1)}, f32[3,2,8,256]{3,2,1,0:T(8,128)S(1)}, u32[]{:S(2)}, u32[]{:S(2)}) collective-permute-start(f32[3,2,8,256]{3,2,1,0:T(8,128)S(1)} %get-tuple-element.79), channel_id=1, source_target_pairs={{0,3},{1,4},{2,5},{3,6},{4,7},{5,0},{6,1},{7,2},{8,11},{9,12},{10,... | collective-permute-start | bytes 147464 | tf_op jit(solution)/shard_map/ppermute | solution.py:194
  158.7 8.4 %collective-permute-start.18 = (f32[3,2,8,256]{3,2,1,0:T(8,128)S(1)}, f32[3,2,8,256]{3,2,1,0:T(8,128)S(1)}, u32[]{:S(2)}, u32[]{:S(2)}) collective-permute-start(f32[3,2,8,256]{3,2,1,0:T(8,128)S(1)} %get-tuple-element.80), channel_id=1, source_target_pairs={{0,2},{1,3},{2,4},{3,5},{4,6},{5,7},{6,0},{7,1},{8,10},{9,11},{10,... | collective-permute-start | bytes 147464 | tf_op jit(solution)/shard_map/ppermute | solution.py:194
  161.7 5.8 %collective-permute-start.17 = (f32[3,2,8,256]{3,2,1,0:T(8,128)S(1)}, f32[3,2,8,256]{3,2,1,0:T(8,128)S(1)}, u32[]{:S(2)}, u32[]{:S(2)}) collective-permute-start(f32[3,2,8,256]{3,2,1,0:T(8,128)S(1)} %get-tuple-element.74), channel_id=1, source_target_pairs={{0,1},{1,2},{2,3},{3,4},{4,5},{5,6},{6,7},{7,0},{8,9},{9,10},{10,1... | collective-permute-start | bytes 147464 | tf_op jit(solution)/shard_map/ppermute | solution.py:194
  (10 other events, 11.3 us)

commit v2 on v1

v2 whole, which is shorter than its diff:
```python
import functools

import jax
import jax.numpy as jnp
import ml_dtypes
import numpy as np
from jax import lax
from jax.experimental import pallas as pl
from jax.experimental.pallas import tpu as pltpu
from jax.sharding import PartitionSpec as P

BF16 = jnp.bfloat16
F32 = jnp.float32
VMEM = pl.BlockSpec(memory_space=pltpu.VMEM)
SMEM = pl.BlockSpec(memory_space=pltpu.SMEM)
HBM = pl.BlockSpec(memory_space=pltpu.MemorySpace.HBM)


def operator_matrices(extent):
    counter = np.arange(extent)
    frequency = np.where(counter < extent // 2, counter, counter - extent)
    factor = np.exp(-2j * np.pi * ((frequency * frequency) % 1024) / 1024)
    table = np.exp(-2j * np.pi * ((counter[:, None] * counter[None, :]) % extent) / extent)
    operator = (np.conj(table) * factor[None, :]) @ table / extent
    operator = 0.5 * (operator + operator.T)
    terms = []
    for matrix in (operator.real, operator.imag - operator.real, operator.real + operator.imag):
        high = matrix.astype(np.float32).astype(ml_dtypes.bfloat16)
        low = (matrix - high.astype(np.float64)).astype(np.float32).astype(ml_dtypes.bfloat16)
        terms.append(np.stack([high, low]))
    return np.stack(terms)


def dot(left, right):
    return jnp.dot(left, right, preferred_element_type=F32)


def split(value):
    high = value.astype(BF16)
    return high, (value - high.astype(F32)).astype(BF16)


def from_right(value, matrices, which):
    high, low = split(value)
    w_high, w_low = matrices[which, 0], matrices[which, 1]
    return dot(
        jnp.concatenate([high, low, high], axis=1), jnp.concatenate([w_high, w_high, w_low], axis=0)
    )


def from_left(value, matrices, which):
    high, low = split(value)
    w_high, w_low = matrices[which, 0], matrices[which, 1]
    return dot(
        jnp.concatenate([w_high, w_high, w_low], axis=1), jnp.concatenate([high, low, high], axis=0)
    )


def adjoint(real, imag, matrices):
    both = from_right(real + imag, matrices, 0)
    mid_real = both + from_right(imag, matrices, 1)
    mid_imag = both - from_right(real, matrices, 2)
    both = from_left(mid_real + mid_imag, matrices, 0)
    return both + from_left(mid_imag, matrices, 1), both - from_left(mid_real, matrices, 2)


def entry_body(light, fields, s_real, s_imag, measured, table, x_ramp, y_ramp, out, psi, *refs):
    if light == 0:
        s_near, i_near, t_near, field, seen, sems = refs
    else:
        s_near, i_near, t_near = s_real, s_imag, table
        field, seen, sems = refs
    slabs = field.shape[0]
    last = slabs - 1
    copies = [pltpu.make_async_copy(fields.at[last, light], field.at[last], sems.at[0])]
    if light == 0:
        copies += [
            pltpu.make_async_copy(s_real, s_near, sems.at[1]),
            pltpu.make_async_copy(s_imag, i_near, sems.at[2]),
            pltpu.make_async_copy(table.at[0], t_near.at[0], sems.at[3]),
            pltpu.make_async_copy(table.at[1], t_near.at[1], sems.at[4]),
            pltpu.make_async_copy(table.at[2], t_near.at[2], sems.at[5]),
        ]
    later = [pltpu.make_async_copy(measured.at[light], seen, sems.at[6])]
    later += [
        pltpu.make_async_copy(fields.at[slab, light], field.at[slab], sems.at[7 + slab])
        for slab in range(last)
    ]
    for copy in copies + later:
        copy.start()
    c_x, d_x = x_ramp[0], x_ramp[1]
    c_y, d_y = y_ramp[0], y_ramp[1]
    cos, sin = c_x * c_y - d_x * d_y, d_x * c_y + c_x * d_y

    def tilt(slab):
        real, imag = field[slab, 0].astype(F32), field[slab, 1].astype(F32)
        psi[slab, 0] = cos * real - sin * imag
        psi[slab, 1] = cos * imag + sin * real

    for copy in copies:
        copy.wait()
    tilt(last)
    a_real, a_imag = s_near[last], i_near[last]
    f_real, f_imag = psi[last, 0], psi[last, 1]
    real, imag = adjoint(
        a_real * f_real - a_imag * f_imag, -(a_real * f_imag + a_imag * f_real), t_near
    )
    for copy in later:
        copy.wait()
    weight = 2.0 * (real * real + imag * imag - seen[...])
    out[0] = weight * real
    out[1] = -(weight * imag)
    for slab in range(last):
        tilt(slab)


def keep_body(flag, _, *refs):
    sources, targets, sems = refs[: len(refs) // 2], refs[len(refs) // 2 : -1], refs[-1]
    copies = [
        pltpu.make_async_copy(source, target, sems.at[index])
        for index, (source, target) in enumerate(zip(sources, targets))
    ]

    @pl.when(flag[0] > 0)
    def _():
        for copy in copies:
            copy.start()
        for copy in copies:
            copy.wait()


def section_body(scale, entries, chains, flag, *refs):
    chis, refs = refs[:entries], refs[entries:]
    s_real, s_imag, table, psi, *refs = refs
    if chains:
        low_real, low_imag, grad_in, out, middle, grad, fields, screens, sems = refs
    else:
        grad_in, out, grad, fields, sems = refs
    slabs = fields.shape[0]
    shape = (grad.shape[0], grad.shape[3], grad.shape[4])

    def field_copy(slab):
        return pltpu.make_async_copy(psi.at[slab], fields.at[slab], sems.at[slab])

    def low_copies(slab):
        return [
            pltpu.make_async_copy(low_real.at[slab], screens.at[0, slab], sems.at[slabs + slab]),
            pltpu.make_async_copy(low_imag.at[slab], screens.at[1, slab], sems.at[2 * slabs + slab]),
        ]

    @pl.when(flag[0] > 0)
    def _():
        for slab in reversed(range(slabs)):
            field_copy(slab).start()
        if chains:

            @pl.when(flag[0] == 1)
            def _():
                for slab in reversed(range(slabs)):
                    for copy in low_copies(slab):
                        copy.start()

        for index, chi in enumerate(chis):

            @pl.when(flag[0] == (index + 1 if entries > 1 or chains else flag[0]))
            def _(chi=chi):
                out[...] = chi[...]

        def step(index, carry):
            slab = slabs - 1 - index
            real, imag = adjoint(out[0], out[1], table)
            a_real, a_imag = s_real[slab], s_imag[slab]
            out[0] = a_real * real + a_imag * imag
            out[1] = a_real * imag - a_imag * real
            field_copy(slab).wait()
            p_real, p_imag = fields[slab, 0], fields[slab, 1]
            g_real = scale * (p_real * real + p_imag * imag)
            g_imag = scale * (p_real * imag - p_imag * real)
            grad[:, slab, 0] = grad_in[:, slab, 0] + g_real.reshape(shape)
            grad[:, slab, 1] = grad_in[:, slab, 1] + g_imag.reshape(shape)
            return carry

        lax.fori_loop(0, slabs, step, 0)
        if chains:
            middle[...] = out[...]

            @pl.when(flag[0] == 1)
            def _():
                def onward(index, carry):
                    slab = slabs - 1 - index
                    real, imag = adjoint(out[0], out[1], table)
                    for copy in low_copies(slab):
                        copy.wait()
                    a_real, a_imag = screens[0, slab], screens[1, slab]
                    out[0] = a_real * real + a_imag * imag
                    out[1] = a_real * imag - a_imag * real
                    return carry

                lax.fori_loop(0, slabs, onward, 0)

    @pl.when(flag[0] == 0)
    def _():
        grad[...] = grad_in[...]


def on_device(fields, screen_real, screen_imag, measured, angles, *, columns):
    slabs, lights, _, extent, _ = fields.shape
    segments = lax.axis_size("depth")
    position = lax.axis_index("depth")
    groups = lax.axis_size("illum")
    counter = jnp.arange(extent, dtype=jnp.int32)

    def ramp(shift):
        angle = 2.0 * jnp.pi / extent * ((shift[:, None] * counter) % extent).astype(F32)
        return jnp.stack([jnp.cos(angle), jnp.sin(angle)], axis=1)

    x_ramp = ramp(angles % 16 - 8)[..., None]
    y_ramp = ramp(angles // 16 - 8)[:, :, None, :]

    def far(value):
        return pltpu.with_memory_space_constraint(value, pltpu.MemorySpace.HBM)

    def like(value):
        return jax.ShapeDtypeStruct(value.shape, value.dtype)

    state_shape = jax.ShapeDtypeStruct((2, extent, extent), F32)
    psi_shape = jax.ShapeDtypeStruct((slabs, 2, extent, extent), F32)
    grad_shape = jax.ShapeDtypeStruct((groups, slabs, 2, extent // groups, extent), F32)
    work = 18 * 2 * extent**3
    params = pltpu.CompilerParams(vmem_limit_bytes=24 << 20)
    scale = float(lights * groups) ** -0.5

    def cost(count):
        return pl.CostEstimate(flops=count * work, bytes_accessed=1 << 20, transcendentals=0)

    def keep(flag, after, *values):
        return pl.pallas_call(
            keep_body,
            out_shape=[like(value) for value in values],
            in_specs=[SMEM] + [HBM] * (len(values) + 1),
            out_specs=[VMEM] * len(values),
            scratch_shapes=[pltpu.SemaphoreType.DMA((len(values),))],
            compiler_params=params,
            cost_estimate=cost(1),
            name="keep",
        )(flag, far(after), *map(far, values))

    def entry(light, s_real, s_imag, table):
        first = light == 0
        return pl.pallas_call(
            functools.partial(entry_body, light),
            out_shape=[state_shape, psi_shape]
            + ([like(s_real), like(s_imag), like(table)] if first else []),
            in_specs=[HBM] + ([HBM] if first else [VMEM]) * 2 + [HBM, HBM if first else VMEM, VMEM, VMEM],
            out_specs=[VMEM] * (5 if first else 2),
            scratch_shapes=[
                pltpu.VMEM((slabs, 2, extent, extent), BF16),
                pltpu.VMEM((extent, extent), F32),
                pltpu.SemaphoreType.DMA((7 + slabs,)),
            ],
            compiler_params=params,
            cost_estimate=cost(2),
            name="entry",
        )(far(fields), *((far(s_real), far(s_imag)) if first else (s_real, s_imag)), far(measured),
          far(table) if first else table, x_ramp[light], y_ramp[light])

    def section(flag, chis, s_real, s_imag, table, psi, low, grad):
        entries, chains = len(chis), low is not None
        outs = 2 if chains else 1
        aliased = 1 + entries + 4 + (2 if chains else 0)
        return pl.pallas_call(
            functools.partial(section_body, scale, entries, chains),
            out_shape=[state_shape] * outs + [grad_shape],
            in_specs=[SMEM] + [VMEM] * (entries + 3) + [HBM] * (3 if chains else 1) + [VMEM],
            out_specs=[VMEM] * (outs + 1),
            scratch_shapes=[pltpu.VMEM(psi_shape.shape, F32)]
            + ([pltpu.VMEM((2, slabs, extent, extent), F32)] if chains else [])
            + [pltpu.SemaphoreType.DMA((3 * slabs,))],
            input_output_aliases={aliased: outs},
            compiler_params=params,
            cost_estimate=cost(slabs * outs),
            name="section",
        )(flag, *chis, s_real, s_imag, table, far(psi), *([far(part) for part in low] if chains else []), grad)

    pairs = segments // 2
    swap = [(2 * c + 1, 2 * c) for c in range(pairs)] + [(2 * c, 2 * c + 1) for c in range(pairs)]
    down = [(2 * c + 1, 2 * ((c - 1) % pairs) + 1) for c in range(pairs)]
    low = [lax.ppermute(screen_real, "depth", swap), lax.ppermute(screen_imag, "depth", swap)]
    matrices = jnp.asarray(operator_matrices(extent))
    upper = position % 2 == 1
    stage_of = pairs - 1 - position // 2
    arrived, psis, near = [], [], [screen_real, screen_imag, matrices]
    for light in range(lights):
        chi, psi, *held = entry(light, *near)
        near = held or near
        arrived.append(chi)
        psis.append(psi)
    grad = jnp.zeros(grad_shape.shape, F32)
    middle = [None] * lights
    for stage in range(pairs + 1):
        first = jnp.logical_and(upper, stage_of == stage).astype(jnp.int32)[None]
        second = jnp.logical_and(jnp.logical_not(upper), stage_of == stage - 1)
        second = second.astype(jnp.int32)[None]
        flag = first + 2 * second if stage < pairs else second
        if stage > 0:
            near = keep(flag, before, screen_real, screen_imag, matrices)
        for light in range(lights):
            chis = [value for value in (arrived[light], middle[light]) if value is not None]
            left, *middles, grad = section(
                flag, chis, *near, psis[light], low if stage < pairs - 1 else None, grad
            )
            if light == 0:
                before = left
            arrived[light] = middle[light] = None
            if stage < pairs - 1:
                arrived[light] = lax.ppermute(left, "depth", down)
                middle[light] = lax.ppermute(middles[0], "depth", swap)
            elif stage < pairs:
                middle[light] = lax.ppermute(left, "depth", swap)
    return owned_sum(grad, groups, columns)


def owned_sum(value, groups, columns):
    pair = 2
    quarters = groups // (columns * pair)
    blocks = value.reshape(columns, quarters, pair, *value.shape[1:])
    here = lax.axis_index("illum")
    column, quarter, digit = here // (quarters * pair), here // pair % quarters, here % pair

    def index(c, q, d):
        return (c % columns * quarters + q % quarters) * pair + d % pair

    places = [(c, q, d) for c in range(columns) for q in range(quarters) for d in range(pair)]

    def block(c, d):
        part = lax.dynamic_index_in_dim(blocks, (column + c) % columns, 0, keepdims=False)
        return lax.dynamic_index_in_dim(part, (digit + d) % pair, 1, keepdims=False)

    total = block(0, 0)
    for d in range(pair):
        for c in range(columns):
            if (c, d) != (0, 0):
                route = [(index(*p), index(p[0] + c, p[1], p[2] + d)) for p in places]
                total = total + lax.ppermute(block(c, d), "illum", route)
    result = lax.dynamic_index_in_dim(total, quarter, 0, keepdims=False)
    for q in range(1, quarters):
        route = [(index(*p), index(p[0], p[1] + q, p[2])) for p in places]
        sent = lax.dynamic_index_in_dim(total, (quarter + q) % quarters, 0, keepdims=False)
        result = result + lax.ppermute(sent, "illum", route)
    return result


def solution(mesh):
    illums = mesh.shape["illum"]
    columns = 4 if illums % 8 == 0 else 1
    return jax.shard_map(
        functools.partial(on_device, columns=columns),
        mesh=mesh,
        in_specs=(
            P("depth", "illum", None, None, None),
            P("depth", None, None),
            P("depth", None, None),
            P("illum", None, None),
            P("illum"),
        ),
        out_specs=P("depth", None, "illum", None),
        check_vma=False,
    )
```

time: 171 us -> 134 us (0.78); the launches traced: 168 us -> 133 us
  waiting for transfers between devices: 55.4 us -> 9.75 us
  starting transfers between devices: 41 us -> 85.3 us
  local copies, waits for them, and re-layouts: 25.7 us -> 3.26 us
  Pallas kernels: 41.1 us -> 32 us
  other arithmetic: 4.57 us -> 2.64 us
    ppermute x24 -> x26, waiting for transfers between devices: 55.4 us -> 9.75 us  [the longest x7 5.55 us: owned_sum(): total = total + lax.ppermute(block(c, d), 'illum', route)]
    ppermute x24 -> x26, starting transfers between devices: 41 us -> 85.3 us  [the longest x6 38.1 us: on_device(): middle[light] = lax.ppermute(middles[0], 'depth', swap)]
    unnamed x68 -> x16, local copies, waits for them, and re-layouts: 25.3 us -> 2.61 us
    pallas_call x18 -> x16, Pallas kernels: 41.1 us -> 32 us  [the longest x10 24.5 us: section(): pl.pallas_call(functools.partial(section_body, scale, entries, chains), o...]
    convert_element_type x1 -> x0, other arithmetic: 1.77 us -> none  [on_device(): fields = fields.astype(F32)]
  transfers between devices with their start and end apart: 24 -> 26, of which waited for: 7 -> 4; matrix products, arithmetic and copies ran while one was open for 0% -> 1% of each run, Pallas kernels for 20% -> 19%
where the time goes in v2:
time: 134 us; the launch traced here: 133 us
  starting transfers between devices  85.3 us (64%)
  Pallas kernels  32 us (24%)
  waiting for transfers between devices  9.75 us (7%)
  local copies, waits for them, and re-layouts  3.26 us (2%)
  other arithmetic  2.64 us (2%)
    ppermute x6, starting transfers between devices, on_device(): middle[light] = lax.ppermute(middles[0], 'depth', swap)  38.1 us
    pallas_call x10, Pallas kernels, section(): pl.pallas_call(functools.partial(section_body, scale, entries, chains), o...  24.5 us
    ppermute x2, starting transfers between devices, on_device(): middle[light] = lax.ppermute(left, 'depth', swap)  17 us
    ppermute x7, starting transfers between devices, owned_sum(): total = total + lax.ppermute(block(c, d), 'illum', route)  13.1 us
    ppermute x3, starting transfers between devices, owned_sum(): result = result + lax.ppermute(sent, 'illum', route)  10 us
    ppermute x6, starting transfers between devices, on_device(): arrived[light] = lax.ppermute(left, 'depth', down)  6.48 us
    pallas_call x2, Pallas kernels, entry(): pl.pallas_call(functools.partial(entry_body, light), out_shape=[state_sha...  5.77 us
    ppermute x7, waiting for transfers between devices, owned_sum(): total = total + lax.ppermute(block(c, d), 'illum', route)  5.55 us
  transfers between devices with their start and end apart: 26, of which 4 were waited for; matrix products, arithmetic and copies ran while one was open for 1% of the time, Pallas kernels for 19%

profile of v2, /device:TPU:32, one launch (start us, length us, event | category | flops | bytes accessed | tf_op | source)
XLA Modules:
  0.0 133.3 jit_solution(9986712384714857738)
XLA Ops:
  0.0 0.5 collective-permute-start.1
  0.5 0.7 fusion.25
  1.7 3.2 %entry.2 = (f32[2,256,256]{2,1,0:T(8,128)S(1)}, f32[3,2,256,256]{3,2,1,0:T(8,128)S(1)}, f32[3,256,256]{2,1,0:T(8,128)S(1)}, f32[3,256,256]{2,1,0:T(8,128)S(1)}, bf16[3,2,256,256]{3,2,1,0:T(8,128)(2,1)S(1)}) custom-call(bf16[3,2,2,256,256]{4,3,2,1,0:T(8,128)(2,1)} %fields.3, f32[3,256,256]{2,1,0:T(8,128)} %refs_0_.7, f32[3,256,256]{2,1,0:T(8,128)} %refs_1_.7, ...), custom_call_target="tpu_custom_call" | custom-call | flops 1207959552 | bytes 1048576 | tf_op jit(solution)/shard_map/entry/pallas_call | solution.py:250
  5.0 1.0 copy-done.7
  6.3 0.3 copy-done.6
  6.6 1.1 section.10
  7.7 0.7 collective-permute-start.4
  8.4 11.7 %collective-permute-start.5 = (f32[2,256,256]{2,1,0:T(8,128)}, f32[2,256,256]{2,1,0:T(8,128)}, u32[]{:S(2)}, u32[]{:S(2)}) collective-permute-start(f32[2,256,256]{2,1,0:T(8,128)} %get-tuple-element.62), channel_id=1, source_target_pairs={{32,0},{96,64},{160,128},{224,192},{0,32},{64,96},{128,160},{192,2... | collective-permute-start | bytes 1572872 | tf_op jit(solution)/shard_map/ppermute | solution.py:317
  20.1 2.5 %entry.3 = (f32[2,256,256]{2,1,0:T(8,128)S(1)}, f32[3,2,256,256]{3,2,1,0:T(8,128)S(1)}) custom-call(bf16[3,2,2,256,256]{4,3,2,1,0:T(8,128)(2,1)} %fields.3, f32[3,256,256]{2,1,0:T(8,128)S(1)} %get-tuple-element.48.s_real.refs_1_, f32[3,256,256]{2,1,0:T(8,128)S(1)} %get-tuple-element.49.s_imag.refs_2_, f32[2,256,256]{2,1,0:T(8,128)} %measured.3, ...), custom_call_target="tpu_custom_call" | custom-call | flops 1207959552 | bytes 1048576 | tf_op jit(solution)/shard_map/entry/pallas_call | solution.py:250
  22.6 1.1 copy-done.5
  23.8 1.1 section.11
  24.9 1.5 %collective-permute-start.2 = (f32[2,256,256]{2,1,0:T(8,128)}, f32[2,256,256]{2,1,0:T(8,128)}, u32[]{:S(2)}, u32[]{:S(2)}) collective-permute-start(f32[2,256,256]{2,1,0:T(8,128)} %get-tuple-element.56), channel_id=1, source_target_pairs={{32,224},{96,32},{160,96},{224,160},{33,225},{97,33},{161,97},{225... | collective-permute-start | bytes 1572872 | tf_op jit(solution)/shard_map/ppermute | solution.py:316
  26.3 8.2 %collective-permute-start.3 = (f32[2,256,256]{2,1,0:T(8,128)S(1)}, f32[2,256,256]{2,1,0:T(8,128)}, u32[]{:S(2)}, u32[]{:S(2)}) collective-permute-start(f32[2,256,256]{2,1,0:T(8,128)S(1)} %get-tuple-element.57), channel_id=1, source_target_pairs={{32,0},{96,64},{160,128},{224,192},{0,32},{64,96},{128,160},{192,2... | collective-permute-start | bytes 1572872 | tf_op jit(solution)/shard_map/ppermute | solution.py:317
  34.6 2.1 %section.12 = (f32[2,256,256]{2,1,0:T(8,128)S(1)}, f32[2,256,256]{2,1,0:T(8,128)}, f32[32,3,2,8,256]{4,3,2,1,0:T(8,128)S(1)}) custom-call(s32[1]{0:T(128)} %bitcast.3.flag, f32[2,256,256]{2,1,0:T(8,128)S(1)} %collective-permute-done.4.refs_0_, f32[2,256,256]{2,1,0:T(8,128)} %collective-permute-done.5.refs_1_, ...), custom_call_target="tpu_custom_call", output_to_operand_aliasing={{2}: (9, {})} | custom-call | flops 3623878656 | bytes 1048576 | tf_op jit(solution)/shard_map/section/pallas_call | solution.py:271
  36.7 0.7 collective-permute-start.8
  37.4 1.4 %collective-permute-start.9 = (f32[2,256,256]{2,1,0:T(8,128)}, f32[2,256,256]{2,1,0:T(8,128)}, u32[]{:S(2)}, u32[]{:S(2)}) collective-permute-start(f32[2,256,256]{2,1,0:T(8,128)} %get-tuple-element.71), channel_id=1, source_target_pairs={{32,0},{96,64},{160,128},{224,192},{0,32},{64,96},{128,160},{192,2... | collective-permute-start | bytes 1572872 | tf_op jit(solution)/shard_map/ppermute | solution.py:317
  38.8 2.5 %section.13 = (f32[2,256,256]{2,1,0:T(8,128)}, f32[2,256,256]{2,1,0:T(8,128)}, f32[32,3,2,8,256]{4,3,2,1,0:T(8,128)S(1)}) custom-call(s32[1]{0:T(128)} %bitcast.3.flag, f32[2,256,256]{2,1,0:T(8,128)} %collective-permute-done.2.refs_0_, f32[2,256,256]{2,1,0:T(8,128)} %collective-permute-done.3.refs_1_, ...), custom_call_target="tpu_custom_call", output_to_operand_aliasing={{2}: (9, {})} | custom-call | flops 3623878656 | bytes 1048576 | tf_op jit(solution)/shard_map/section/pallas_call | solution.py:271
  41.3 1.5 %collective-permute-start.6 = (f32[2,256,256]{2,1,0:T(8,128)}, f32[2,256,256]{2,1,0:T(8,128)}, u32[]{:S(2)}, u32[]{:S(2)}) collective-permute-start(f32[2,256,256]{2,1,0:T(8,128)} %get-tuple-element.65), channel_id=1, source_target_pairs={{32,224},{96,32},{160,96},{224,160},{33,225},{97,33},{161,97},{225... | collective-permute-start | bytes 1572872 | tf_op jit(solution)/shard_map/ppermute | solution.py:316
  42.8 5.7 %collective-permute-start.7 = (f32[2,256,256]{2,1,0:T(8,128)}, f32[2,256,256]{2,1,0:T(8,128)}, u32[]{:S(2)}, u32[]{:S(2)}) collective-permute-start(f32[2,256,256]{2,1,0:T(8,128)} %get-tuple-element.66), channel_id=1, source_target_pairs={{32,0},{96,64},{160,128},{224,192},{0,32},{64,96},{128,160},{192,2... | collective-permute-start | bytes 1572872 | tf_op jit(solution)/shard_map/ppermute | solution.py:317
  48.6 1.3 section.14
  49.9 0.7 collective-permute-start.12
  50.6 7.8 %collective-permute-start.13 = (f32[2,256,256]{2,1,0:T(8,128)S(1)}, f32[2,256,256]{2,1,0:T(8,128)}, u32[]{:S(2)}, u32[]{:S(2)}) collective-permute-start(f32[2,256,256]{2,1,0:T(8,128)S(1)} %get-tuple-element.80), channel_id=1, source_target_pairs={{32,0},{96,64},{160,128},{224,192},{0,32},{64,96},{128,160},{192,2... | collective-permute-start | bytes 1572872 | tf_op jit(solution)/shard_map/ppermute | solution.py:317
  58.4 2.5 %section.15 = (f32[2,256,256]{2,1,0:T(8,128)}, f32[2,256,256]{2,1,0:T(8,128)}, f32[32,3,2,8,256]{4,3,2,1,0:T(8,128)S(1)}) custom-call(s32[1]{0:T(128)} %bitcast.2.flag, f32[2,256,256]{2,1,0:T(8,128)} %collective-permute-done.6.refs_0_, f32[2,256,256]{2,1,0:T(8,128)} %collective-permute-done.7.refs_1_, ...), custom_call_target="tpu_custom_call", output_to_operand_aliasing={{2}: (9, {})} | custom-call | flops 3623878656 | bytes 1048576 | tf_op jit(solution)/shard_map/section/pallas_call | solution.py:271
  61.0 1.5 %collective-permute-start.10 = (f32[2,256,256]{2,1,0:T(8,128)}, f32[2,256,256]{2,1,0:T(8,128)}, u32[]{:S(2)}, u32[]{:S(2)}) collective-permute-start(f32[2,256,256]{2,1,0:T(8,128)} %get-tuple-element.74), channel_id=1, source_target_pairs={{32,224},{96,32},{160,96},{224,160},{33,225},{97,33},{161,97},{225... | collective-permute-start | bytes 1572872 | tf_op jit(solution)/shard_map/ppermute | solution.py:316
  62.4 3.4 %collective-permute-start.11 = (f32[2,256,256]{2,1,0:T(8,128)}, f32[2,256,256]{2,1,0:T(8,128)}, u32[]{:S(2)}, u32[]{:S(2)}) collective-permute-start(f32[2,256,256]{2,1,0:T(8,128)} %get-tuple-element.75), channel_id=1, source_target_pairs={{32,0},{96,64},{160,128},{224,192},{0,32},{64,96},{128,160},{192,2... | collective-permute-start | bytes 1572872 | tf_op jit(solution)/shard_map/ppermute | solution.py:317
  65.9 1.3 section.16
  67.2 5.6 %collective-permute-start.15 = (f32[2,256,256]{2,1,0:T(8,128)S(1)}, f32[2,256,256]{2,1,0:T(8,128)S(1)}, u32[]{:S(2)}, u32[]{:S(2)}) collective-permute-start(f32[2,256,256]{2,1,0:T(8,128)S(1)} %get-tuple-element.84._), channel_id=1, source_target_pairs={{32,0},{96,64},{160,128},{224,192},{0,32},{64,96},{128,160},{192,2... | collective-permute-start | bytes 1572872 | tf_op jit(solution)/shard_map/ppermute | solution.py:319
  72.9 1.5 %section.17 = (f32[2,256,256]{2,1,0:T(8,128)S(1)}, f32[32,3,2,8,256]{4,3,2,1,0:T(8,128)S(1)}) custom-call(s32[1]{0:T(128)} %bitcast.1.flag, f32[2,256,256]{2,1,0:T(8,128)} %collective-permute-done.10.refs_0_, f32[2,256,256]{2,1,0:T(8,128)} %collective-permute-done.11.refs_1_, ...), custom_call_target="tpu_custom_call", output_to_operand_aliasing={{1}: (7, {})} | custom-call | flops 1811939328 | bytes 1048576 | tf_op jit(solution)/shard_map/section/pallas_call | solution.py:271
  74.4 11.4 %collective-permute-start.14 = (f32[2,256,256]{2,1,0:T(8,128)S(1)}, f32[2,256,256]{2,1,0:T(8,128)}, u32[]{:S(2)}, u32[]{:S(2)}) collective-permute-start(f32[2,256,256]{2,1,0:T(8,128)S(1)} %get-tuple-element.83), channel_id=1, source_target_pairs={{32,0},{96,64},{160,128},{224,192},{0,32},{64,96},{128,160},{192,2... | collective-permute-start | bytes 1572872 | tf_op jit(solution)/shard_map/ppermute | solution.py:319
  85.8 1.6 %keep.7 = (f32[3,256,256]{2,1,0:T(8,128)S(1)}, f32[3,256,256]{2,1,0:T(8,128)S(1)}, bf16[3,2,256,256]{3,2,1,0:T(8,128)(2,1)S(1)}) custom-call(s32[1]{0:T(128)} %bitcast.flag, f32[2,256,256]{2,1,0:T(8,128)} %copy-done, f32[3,256,256]{2,1,0:T(8,128)} %refs_0_.7, f32[3,256,256]{2,1,0:T(8,128)} %refs_1_.7, bf16[3,2,256,256]{3,2,1,0:T(8,128)(2,1)} %constant.488.clone.table.refs_2_), custom_call_target="tpu_custom_call" | custom-call | flops 603979776 | bytes 1048576 | tf_op jit(solution)/shard_map/keep/pallas_call | solution.py:237
  87.4 5.0 %section.18 = (f32[2,256,256]{2,1,0:T(8,128)}, f32[32,3,2,8,256]{4,3,2,1,0:T(8,128)S(1)}) custom-call(s32[1]{0:T(128)} %bitcast.flag, f32[2,256,256]{2,1,0:T(8,128)S(1)} %collective-permute-done.15.refs_0_, f32[3,256,256]{2,1,0:T(8,128)S(1)} %get-tuple-element.85.refs_1_, ...), custom_call_target="tpu_custom_call", output_to_operand_aliasing={{1}: (6, {})} | custom-call | flops 1811939328 | bytes 1048576 | tf_op jit(solution)/shard_map/section/pallas_call | solution.py:271
  92.4 6.0 %section.19 = (f32[2,256,256]{2,1,0:T(8,128)}, f32[32,3,2,8,256]{4,3,2,1,0:T(8,128)S(1)}) custom-call(s32[1]{0:T(128)} %bitcast.flag, f32[2,256,256]{2,1,0:T(8,128)} %collective-permute-done.14.refs_0_, f32[3,256,256]{2,1,0:T(8,128)S(1)} %get-tuple-element.85.refs_1_, f32[3,256,256]{2,1,0:T(8,128)S(1)} %get-tuple-element.86.refs_2_, ...), custom_call_target="tpu_custom_call", output_to_operand_aliasing={{1}: (6, {})} | custom-call | flops 1811939328 | bytes 1048576 | tf_op jit(solution)/shard_map/section/pallas_call | solution.py:271
  98.6 2.4 %collective-permute-start.22 = (f32[4,3,2,8,256]{4,3,2,1,0:T(8,128)S(1)}, f32[4,3,2,8,256]{4,3,2,1,0:T(8,128)S(1)}, u32[]{:S(2)}, u32[]{:S(2)}) collective-permute-start(f32[4,3,2,8,256]{4,3,2,1,0:T(8,128)S(1)} %get-tuple-element.92), channel_id=1, source_target_pairs={{0,25},{1,24},{2,27},{3,26},{4,29},{5,28},{6,31},{7,30},{8,1},{9,0... | collective-permute-start | bytes 589832 | tf_op jit(solution)/shard_map/ppermute | solution.py:344
  101.0 2.1 %collective-permute-start.21 = (f32[4,3,2,8,256]{4,3,2,1,0:T(8,128)S(1)}, f32[4,3,2,8,256]{4,3,2,1,0:T(8,128)S(1)}, u32[]{:S(2)}, u32[]{:S(2)}) collective-permute-start(f32[4,3,2,8,256]{4,3,2,1,0:T(8,128)S(1)} %get-tuple-element.93), channel_id=1, source_target_pairs={{0,17},{1,16},{2,19},{3,18},{4,21},{5,20},{6,23},{7,22},{8,25},{9,... | collective-permute-start | bytes 589832 | tf_op jit(solution)/shard_map/ppermute | solution.py:344
  103.1 0.4 collective-permute-start.20
  103.6 1.9 %collective-permute-start.19 = (f32[4,3,2,8,256]{4,3,2,1,0:T(8,128)S(1)}, f32[4,3,2,8,256]{4,3,2,1,0:T(8,128)S(1)}, u32[]{:S(2)}, u32[]{:S(2)}) collective-permute-start(f32[4,3,2,8,256]{4,3,2,1,0:T(8,128)S(1)} %get-tuple-element.95), channel_id=1, source_target_pairs={{0,1},{1,0},{2,3},{3,2},{4,5},{5,4},{6,7},{7,6},{8,9},{9,8},{10,11... | collective-permute-start | bytes 589832 | tf_op jit(solution)/shard_map/ppermute | solution.py:344
  105.5 2.3 %collective-permute-start.18 = (f32[4,3,2,8,256]{4,3,2,1,0:T(8,128)S(1)}, f32[4,3,2,8,256]{4,3,2,1,0:T(8,128)S(1)}, u32[]{:S(2)}, u32[]{:S(2)}) collective-permute-start(f32[4,3,2,8,256]{4,3,2,1,0:T(8,128)S(1)} %get-tuple-element.96), channel_id=1, source_target_pairs={{0,24},{1,25},{2,26},{3,27},{4,28},{5,29},{6,30},{7,31},{8,0},{9,1... | collective-permute-start | bytes 589832 | tf_op jit(solution)/shard_map/ppermute | solution.py:344
  107.8 1.5 %collective-permute-start.17 = (f32[4,3,2,8,256]{4,3,2,1,0:T(8,128)S(1)}, f32[4,3,2,8,256]{4,3,2,1,0:T(8,128)}, u32[]{:S(2)}, u32[]{:S(2)}) collective-permute-start(f32[4,3,2,8,256]{4,3,2,1,0:T(8,128)S(1)} %get-tuple-element.97), channel_id=1, source_target_pairs={{0,16},{1,17},{2,18},{3,19},{4,20},{5,21},{6,22},{7,23},{8,24},{9,... | collective-permute-start | bytes 589832 | tf_op jit(solution)/shard_map/ppermute | solution.py:344
  109.4 2.3 %collective-permute-start.16 = (f32[4,3,2,8,256]{4,3,2,1,0:T(8,128)S(1)}, f32[4,3,2,8,256]{4,3,2,1,0:T(8,128)}, u32[]{:S(2)}, u32[]{:S(2)}) collective-permute-start(f32[4,3,2,8,256]{4,3,2,1,0:T(8,128)S(1)} %get-tuple-element.91), channel_id=1, source_target_pairs={{0,8},{1,9},{2,10},{3,11},{4,12},{5,13},{6,14},{7,15},{8,16},{9,17... | collective-permute-start | bytes 589832 | tf_op jit(solution)/shard_map/ppermute | solution.py:344
  111.7 2.5 %collective-permute-done.19 = f32[4,3,2,8,256]{4,3,2,1,0:T(8,128)S(1)} collective-permute-done((f32[4,3,2,8,256]{4,3,2,1,0:T(8,128)S(1)}, f32[4,3,2,8,256]{4,3,2,1,0:T(8,128)S(1)}, u32[]{:S(2)}, u32[]{:S(2)}) %collective-permute-start.19) | collective-permute-done | bytes 196640 | tf_op jit(solution)/shard_map/ppermute | solution.py:344
  114.2 1.0 collective-permute-done.17
  115.2 2.0 %collective-permute-done.16 = f32[4,3,2,8,256]{4,3,2,1,0:T(8,128)} collective-permute-done((f32[4,3,2,8,256]{4,3,2,1,0:T(8,128)S(1)}, f32[4,3,2,8,256]{4,3,2,1,0:T(8,128)}, u32[]{:S(2)}, u32[]{:S(2)}) %collective-permute-start.16) | collective-permute-done | bytes 196640 | tf_op jit(solution)/shard_map/ppermute | solution.py:344
  117.2 1.2 fusion.5
  118.4 6.2 %collective-permute-start.25 = (f32[3,2,8,256]{3,2,1,0:T(8,128)S(1)}, f32[3,2,8,256]{3,2,1,0:T(8,128)S(1)}, u32[]{:S(2)}, u32[]{:S(2)}) collective-permute-start(f32[3,2,8,256]{3,2,1,0:T(8,128)S(1)} %get-tuple-element.99), channel_id=1, source_target_pairs={{0,6},{1,7},{2,0},{3,1},{4,2},{5,3},{6,4},{7,5},{8,14},{9,15},{10,... | collective-permute-start | bytes 147464 | tf_op jit(solution)/shard_map/ppermute | solution.py:349
  124.6 1.0 collective-permute-start.24
  125.7 2.8 %collective-permute-start.23 = (f32[3,2,8,256]{3,2,1,0:T(8,128)S(1)}, f32[3,2,8,256]{3,2,1,0:T(8,128)S(1)}, u32[]{:S(2)}, u32[]{:S(2)}) collective-permute-start(f32[3,2,8,256]{3,2,1,0:T(8,128)S(1)} %get-tuple-element.98), channel_id=1, source_target_pairs={{0,2},{1,3},{2,4},{3,5},{4,6},{5,7},{6,0},{7,1},{8,10},{9,11},{10,... | collective-permute-start | bytes 147464 | tf_op jit(solution)/shard_map/ppermute | solution.py:349
  128.5 4.2 %collective-permute-done.24 = f32[3,2,8,256]{3,2,1,0:T(8,128)S(1)} collective-permute-done((f32[3,2,8,256]{3,2,1,0:T(8,128)S(1)}, f32[3,2,8,256]{3,2,1,0:T(8,128)S(1)}, u32[]{:S(2)}, u32[]{:S(2)}) %collective-permute-start.24) | collective-permute-done | bytes 49184 | tf_op jit(solution)/shard_map/ppermute | solution.py:349
  132.6 0.6 fusion.7
  (47 shorter events, 1.2 us)
Async XLA Ops:
  0.0 4.9 %collective-permute-start = (f32[3,256,256]{2,1,0:T(8,128)}, f32[3,256,256]{2,1,0:T(8,128)S(1)}, u32[]{:S(2)}, u32[]{:S(2)}) collective-permute-start(f32[3,256,256]{2,1,0:T(8,128)} %refs_0_.7), channel_id=1, source_target_pairs={{32,0},{96,64},{160,128},{224,192},{0,32},{64,96},{128,160},{192,2... | collective-permute-start | bytes 2359304 | tf_op jit(solution)/shard_map/ppermute | solution.py:288
  0.0 5.0 %collective-permute-start.1 = (f32[3,256,256]{2,1,0:T(8,128)}, f32[3,256,256]{2,1,0:T(8,128)S(1)}, u32[]{:S(2)}, u32[]{:S(2)}) collective-permute-start(f32[3,256,256]{2,1,0:T(8,128)} %refs_1_.7), channel_id=1, source_target_pairs={{32,0},{96,64},{160,128},{224,192},{0,32},{64,96},{128,160},{192,2... | collective-permute-start | bytes 2359304 | tf_op jit(solution)/shard_map/ppermute | solution.py:288
  4.9 1.4 %copy-start.4 = (f32[3,2,256,256]{3,2,1,0:T(8,128)}, f32[3,2,256,256]{3,2,1,0:T(8,128)S(1)}, u32[]{:S(2)}) copy-start(f32[3,2,256,256]{3,2,1,0:T(8,128)S(1)} %get-tuple-element.54.refs_4_.refs_5_) | copy-start | bytes 4718596
  4.9 1.7 %copy-start.6 = (f32[3,256,256]{2,1,0:T(8,128)}, f32[3,256,256]{2,1,0:T(8,128)S(1)}, u32[]{:S(2)}) copy-start(f32[3,256,256]{2,1,0:T(8,128)S(1)} %collective-permute-done.refs_5_.refs_6_) | copy-start | bytes 2359300
  5.0 1.0 copy-start.7
  7.7 14.9 %copy-start.3 = (f32[2,256,256]{2,1,0:T(8,128)}, f32[2,256,256]{2,1,0:T(8,128)S(1)}, u32[]{:S(2)}) copy-start(f32[2,256,256]{2,1,0:T(8,128)S(1)} %get-tuple-element.58._) | copy-start | bytes 1572868
  7.7 26.8 %collective-permute-start.4 = (f32[2,256,256]{2,1,0:T(8,128)S(1)}, f32[2,256,256]{2,1,0:T(8,128)S(1)}, u32[]{:S(2)}, u32[]{:S(2)}) collective-permute-start(f32[2,256,256]{2,1,0:T(8,128)S(1)} %get-tuple-element.58._), channel_id=1, source_target_pairs={{32,224},{96,32},{160,96},{224,160},{33,225},{97,33},{161,97},{225... | collective-permute-start | bytes 1572872 | tf_op jit(solution)/shard_map/ppermute | solution.py:316
  8.4 26.1 %collective-permute-start.5 = (f32[2,256,256]{2,1,0:T(8,128)}, f32[2,256,256]{2,1,0:T(8,128)}, u32[]{:S(2)}, u32[]{:S(2)}) collective-permute-start(f32[2,256,256]{2,1,0:T(8,128)} %get-tuple-element.62), channel_id=1, source_target_pairs={{32,0},{96,64},{160,128},{224,192},{0,32},{64,96},{128,160},{192,2... | collective-permute-start | bytes 1572872 | tf_op jit(solution)/shard_map/ppermute | solution.py:317
  22.6 1.1 copy-start.5
  24.9 13.9 %collective-permute-start.2 = (f32[2,256,256]{2,1,0:T(8,128)}, f32[2,256,256]{2,1,0:T(8,128)}, u32[]{:S(2)}, u32[]{:S(2)}) collective-permute-start(f32[2,256,256]{2,1,0:T(8,128)} %get-tuple-element.56), channel_id=1, source_target_pairs={{32,224},{96,32},{160,96},{224,160},{33,225},{97,33},{161,97},{225... | collective-permute-start | bytes 1572872 | tf_op jit(solution)/shard_map/ppermute | solution.py:316
  26.3 12.5 %collective-permute-start.3 = (f32[2,256,256]{2,1,0:T(8,128)S(1)}, f32[2,256,256]{2,1,0:T(8,128)}, u32[]{:S(2)}, u32[]{:S(2)}) collective-permute-start(f32[2,256,256]{2,1,0:T(8,128)S(1)} %get-tuple-element.57), channel_id=1, source_target_pairs={{32,0},{96,64},{160,128},{224,192},{0,32},{64,96},{128,160},{192,2... | collective-permute-start | bytes 1572872 | tf_op jit(solution)/shard_map/ppermute | solution.py:317
  36.7 4.6 %copy-start.2 = (f32[2,256,256]{2,1,0:T(8,128)}, f32[2,256,256]{2,1,0:T(8,128)S(1)}, u32[]{:S(2)}) copy-start(f32[2,256,256]{2,1,0:T(8,128)S(1)} %get-tuple-element.67._) | copy-start | bytes 1572868
  36.7 11.9 %collective-permute-start.8 = (f32[2,256,256]{2,1,0:T(8,128)S(1)}, f32[2,256,256]{2,1,0:T(8,128)S(1)}, u32[]{:S(2)}, u32[]{:S(2)}) collective-permute-start(f32[2,256,256]{2,1,0:T(8,128)S(1)} %get-tuple-element.67._), channel_id=1, source_target_pairs={{32,224},{96,32},{160,96},{224,160},{33,225},{97,33},{161,97},{225... | collective-permute-start | bytes 1572872 | tf_op jit(solution)/shard_map/ppermute | solution.py:316
  37.4 11.2 %collective-permute-start.9 = (f32[2,256,256]{2,1,0:T(8,128)}, f32[2,256,256]{2,1,0:T(8,128)}, u32[]{:S(2)}, u32[]{:S(2)}) collective-permute-start(f32[2,256,256]{2,1,0:T(8,128)} %get-tuple-element.71), channel_id=1, source_target_pairs={{32,0},{96,64},{160,128},{224,192},{0,32},{64,96},{128,160},{192,2... | collective-permute-start | bytes 1572872 | tf_op jit(solution)/shard_map/ppermute | solution.py:317
  41.3 17.1 %collective-permute-start.6 = (f32[2,256,256]{2,1,0:T(8,128)}, f32[2,256,256]{2,1,0:T(8,128)}, u32[]{:S(2)}, u32[]{:S(2)}) collective-permute-start(f32[2,256,256]{2,1,0:T(8,128)} %get-tuple-element.65), channel_id=1, source_target_pairs={{32,224},{96,32},{160,96},{224,160},{33,225},{97,33},{161,97},{225... | collective-permute-start | bytes 1572872 | tf_op jit(solution)/shard_map/ppermute | solution.py:316
  42.8 15.6 %collective-permute-start.7 = (f32[2,256,256]{2,1,0:T(8,128)}, f32[2,256,256]{2,1,0:T(8,128)}, u32[]{:S(2)}, u32[]{:S(2)}) collective-permute-start(f32[2,256,256]{2,1,0:T(8,128)} %get-tuple-element.66), channel_id=1, source_target_pairs={{32,0},{96,64},{160,128},{224,192},{0,32},{64,96},{128,160},{192,2... | collective-permute-start | bytes 1572872 | tf_op jit(solution)/shard_map/ppermute | solution.py:317
  49.9 11.0 %copy-start.1 = (f32[2,256,256]{2,1,0:T(8,128)}, f32[2,256,256]{2,1,0:T(8,128)S(1)}, u32[]{:S(2)}) copy-start(f32[2,256,256]{2,1,0:T(8,128)S(1)} %get-tuple-element.76._) | copy-start | bytes 1572868
  49.9 16.0 %collective-permute-start.12 = (f32[2,256,256]{2,1,0:T(8,128)S(1)}, f32[2,256,256]{2,1,0:T(8,128)S(1)}, u32[]{:S(2)}, u32[]{:S(2)}) collective-permute-start(f32[2,256,256]{2,1,0:T(8,128)S(1)} %get-tuple-element.76._), channel_id=1, source_target_pairs={{32,224},{96,32},{160,96},{224,160},{33,225},{97,33},{161,97},{225... | collective-permute-start | bytes 1572872 | tf_op jit(solution)/shard_map/ppermute | solution.py:316
  50.6 15.3 %collective-permute-start.13 = (f32[2,256,256]{2,1,0:T(8,128)S(1)}, f32[2,256,256]{2,1,0:T(8,128)}, u32[]{:S(2)}, u32[]{:S(2)}) collective-permute-start(f32[2,256,256]{2,1,0:T(8,128)S(1)} %get-tuple-element.80), channel_id=1, source_target_pairs={{32,0},{96,64},{160,128},{224,192},{0,32},{64,96},{128,160},{192,2... | collective-permute-start | bytes 1572872 | tf_op jit(solution)/shard_map/ppermute | solution.py:317
  61.0 11.9 %collective-permute-start.10 = (f32[2,256,256]{2,1,0:T(8,128)}, f32[2,256,256]{2,1,0:T(8,128)}, u32[]{:S(2)}, u32[]{:S(2)}) collective-permute-start(f32[2,256,256]{2,1,0:T(8,128)} %get-tuple-element.74), channel_id=1, source_target_pairs={{32,224},{96,32},{160,96},{224,160},{33,225},{97,33},{161,97},{225... | collective-permute-start | bytes 1572872 | tf_op jit(solution)/shard_map/ppermute | solution.py:316
  62.4 10.4 %collective-permute-start.11 = (f32[2,256,256]{2,1,0:T(8,128)}, f32[2,256,256]{2,1,0:T(8,128)}, u32[]{:S(2)}, u32[]{:S(2)}) collective-permute-start(f32[2,256,256]{2,1,0:T(8,128)} %get-tuple-element.75), channel_id=1, source_target_pairs={{32,0},{96,64},{160,128},{224,192},{0,32},{64,96},{128,160},{192,2... | collective-permute-start | bytes 1572872 | tf_op jit(solution)/shard_map/ppermute | solution.py:317
  67.2 7.1 %copy-start = (f32[2,256,256]{2,1,0:T(8,128)}, f32[2,256,256]{2,1,0:T(8,128)S(1)}, u32[]{:S(2)}) copy-start(f32[2,256,256]{2,1,0:T(8,128)S(1)} %get-tuple-element.84._) | copy-start | bytes 1572868
  67.2 20.2 %collective-permute-start.15 = (f32[2,256,256]{2,1,0:T(8,128)S(1)}, f32[2,256,256]{2,1,0:T(8,128)S(1)}, u32[]{:S(2)}, u32[]{:S(2)}) collective-permute-start(f32[2,256,256]{2,1,0:T(8,128)S(1)} %get-tuple-element.84._), channel_id=1, source_target_pairs={{32,0},{96,64},{160,128},{224,192},{0,32},{64,96},{128,160},{192,2... | collective-permute-start | bytes 1572872 | tf_op jit(solution)/shard_map/ppermute | solution.py:319
  74.4 18.1 %collective-permute-start.14 = (f32[2,256,256]{2,1,0:T(8,128)S(1)}, f32[2,256,256]{2,1,0:T(8,128)}, u32[]{:S(2)}, u32[]{:S(2)}) collective-permute-start(f32[2,256,256]{2,1,0:T(8,128)S(1)} %get-tuple-element.83), channel_id=1, source_target_pairs={{32,0},{96,64},{160,128},{224,192},{0,32},{64,96},{128,160},{192,2... | collective-permute-start | bytes 1572872 | tf_op jit(solution)/shard_map/ppermute | solution.py:319
  98.6 9.2 %collective-permute-start.22 = (f32[4,3,2,8,256]{4,3,2,1,0:T(8,128)S(1)}, f32[4,3,2,8,256]{4,3,2,1,0:T(8,128)S(1)}, u32[]{:S(2)}, u32[]{:S(2)}) collective-permute-start(f32[4,3,2,8,256]{4,3,2,1,0:T(8,128)S(1)} %get-tuple-element.92), channel_id=1, source_target_pairs={{0,25},{1,24},{2,27},{3,26},{4,29},{5,28},{6,31},{7,30},{8,1},{9,0... | collective-permute-start | bytes 589832 | tf_op jit(solution)/shard_map/ppermute | solution.py:344
  101.0 8.4 %collective-permute-start.21 = (f32[4,3,2,8,256]{4,3,2,1,0:T(8,128)S(1)}, f32[4,3,2,8,256]{4,3,2,1,0:T(8,128)S(1)}, u32[]{:S(2)}, u32[]{:S(2)}) collective-permute-start(f32[4,3,2,8,256]{4,3,2,1,0:T(8,128)S(1)} %get-tuple-element.93), channel_id=1, source_target_pairs={{0,17},{1,16},{2,19},{3,18},{4,21},{5,20},{6,23},{7,22},{8,25},{9,... | collective-permute-start | bytes 589832 | tf_op jit(solution)/shard_map/ppermute | solution.py:344
  103.1 8.6 %collective-permute-start.20 = (f32[4,3,2,8,256]{4,3,2,1,0:T(8,128)S(1)}, f32[4,3,2,8,256]{4,3,2,1,0:T(8,128)S(1)}, u32[]{:S(2)}, u32[]{:S(2)}) collective-permute-start(f32[4,3,2,8,256]{4,3,2,1,0:T(8,128)S(1)} %get-tuple-element.94), channel_id=1, source_target_pairs={{0,9},{1,8},{2,11},{3,10},{4,13},{5,12},{6,15},{7,14},{8,17},{9,16... | collective-permute-start | bytes 589832 | tf_op jit(solution)/shard_map/ppermute | solution.py:344
  103.6 10.6 %collective-permute-start.19 = (f32[4,3,2,8,256]{4,3,2,1,0:T(8,128)S(1)}, f32[4,3,2,8,256]{4,3,2,1,0:T(8,128)S(1)}, u32[]{:S(2)}, u32[]{:S(2)}) collective-permute-start(f32[4,3,2,8,256]{4,3,2,1,0:T(8,128)S(1)} %get-tuple-element.95), channel_id=1, source_target_pairs={{0,1},{1,0},{2,3},{3,2},{4,5},{5,4},{6,7},{7,6},{8,9},{9,8},{10,11... | collective-permute-start | bytes 589832 | tf_op jit(solution)/shard_map/ppermute | solution.py:344
  105.5 8.7 %collective-permute-start.18 = (f32[4,3,2,8,256]{4,3,2,1,0:T(8,128)S(1)}, f32[4,3,2,8,256]{4,3,2,1,0:T(8,128)S(1)}, u32[]{:S(2)}, u32[]{:S(2)}) collective-permute-start(f32[4,3,2,8,256]{4,3,2,1,0:T(8,128)S(1)} %get-tuple-element.96), channel_id=1, source_target_pairs={{0,24},{1,25},{2,26},{3,27},{4,28},{5,29},{6,30},{7,31},{8,0},{9,1... | collective-permute-start | bytes 589832 | tf_op jit(solution)/shard_map/ppermute | solution.py:344
  107.8 7.4 %collective-permute-start.17 = (f32[4,3,2,8,256]{4,3,2,1,0:T(8,128)S(1)}, f32[4,3,2,8,256]{4,3,2,1,0:T(8,128)}, u32[]{:S(2)}, u32[]{:S(2)}) collective-permute-start(f32[4,3,2,8,256]{4,3,2,1,0:T(8,128)S(1)} %get-tuple-element.97), channel_id=1, source_target_pairs={{0,16},{1,17},{2,18},{3,19},{4,20},{5,21},{6,22},{7,23},{8,24},{9,... | collective-permute-start | bytes 589832 | tf_op jit(solution)/shard_map/ppermute | solution.py:344
  109.4 7.8 %collective-permute-start.16 = (f32[4,3,2,8,256]{4,3,2,1,0:T(8,128)S(1)}, f32[4,3,2,8,256]{4,3,2,1,0:T(8,128)}, u32[]{:S(2)}, u32[]{:S(2)}) collective-permute-start(f32[4,3,2,8,256]{4,3,2,1,0:T(8,128)S(1)} %get-tuple-element.91), channel_id=1, source_target_pairs={{0,8},{1,9},{2,10},{3,11},{4,12},{5,13},{6,14},{7,15},{8,16},{9,17... | collective-permute-start | bytes 589832 | tf_op jit(solution)/shard_map/ppermute | solution.py:344
  118.4 10.1 %collective-permute-start.25 = (f32[3,2,8,256]{3,2,1,0:T(8,128)S(1)}, f32[3,2,8,256]{3,2,1,0:T(8,128)S(1)}, u32[]{:S(2)}, u32[]{:S(2)}) collective-permute-start(f32[3,2,8,256]{3,2,1,0:T(8,128)S(1)} %get-tuple-element.99), channel_id=1, source_target_pairs={{0,6},{1,7},{2,0},{3,1},{4,2},{5,3},{6,4},{7,5},{8,14},{9,15},{10,... | collective-permute-start | bytes 147464 | tf_op jit(solution)/shard_map/ppermute | solution.py:349
  124.6 8.0 %collective-permute-start.24 = (f32[3,2,8,256]{3,2,1,0:T(8,128)S(1)}, f32[3,2,8,256]{3,2,1,0:T(8,128)S(1)}, u32[]{:S(2)}, u32[]{:S(2)}) collective-permute-start(f32[3,2,8,256]{3,2,1,0:T(8,128)S(1)} %get-tuple-element.100), channel_id=1, source_target_pairs={{0,4},{1,5},{2,6},{3,7},{4,0},{5,1},{6,2},{7,3},{8,12},{9,13},{10,... | collective-permute-start | bytes 147464 | tf_op jit(solution)/shard_map/ppermute | solution.py:349
  125.7 7.0 %collective-permute-start.23 = (f32[3,2,8,256]{3,2,1,0:T(8,128)S(1)}, f32[3,2,8,256]{3,2,1,0:T(8,128)S(1)}, u32[]{:S(2)}, u32[]{:S(2)}) collective-permute-start(f32[3,2,8,256]{3,2,1,0:T(8,128)S(1)} %get-tuple-element.98), channel_id=1, source_target_pairs={{0,2},{1,3},{2,4},{3,5},{4,6},{5,7},{6,0},{7,1},{8,10},{9,11},{10,... | collective-permute-start | bytes 147464 | tf_op jit(solution)/shard_map/ppermute | solution.py:349

commit v3 on v2

--- a/solution.py
+++ b/solution.py
@@ -64,27 +64,26 @@
     return both + from_left(mid_imag, matrices, 1), both - from_left(mid_real, matrices, 2)
 
 
-def entry_body(light, fields, s_real, s_imag, measured, table, x_ramp, y_ramp, out, psi, *refs):
-    if light == 0:
-        s_near, i_near, t_near, field, seen, sems = refs
-    else:
-        s_near, i_near, t_near = s_real, s_imag, table
-        field, seen, sems = refs
+def entry_body(light, fields, s_real, s_imag, measured, table, x_ramp, y_ramp, out, psi_out,
+               s_near, i_near, t_near, field, seen, psi, sems):
     slabs = field.shape[0]
     last = slabs - 1
-    copies = [pltpu.make_async_copy(fields.at[last, light], field.at[last], sems.at[0])]
-    if light == 0:
-        copies += [
-            pltpu.make_async_copy(s_real, s_near, sems.at[1]),
-            pltpu.make_async_copy(s_imag, i_near, sems.at[2]),
-            pltpu.make_async_copy(table.at[0], t_near.at[0], sems.at[3]),
-            pltpu.make_async_copy(table.at[1], t_near.at[1], sems.at[4]),
-            pltpu.make_async_copy(table.at[2], t_near.at[2], sems.at[5]),
-        ]
+    copies = [
+        pltpu.make_async_copy(fields.at[last, light], field.at[last], sems.at[0]),
+        pltpu.make_async_copy(s_real, s_near, sems.at[1]),
+        pltpu.make_async_copy(s_imag, i_near, sems.at[2]),
+        pltpu.make_async_copy(table.at[0], t_near.at[0], sems.at[3]),
+        pltpu.make_async_copy(table.at[1], t_near.at[1], sems.at[4]),
+        pltpu.make_async_copy(table.at[2], t_near.at[2], sems.at[5]),
+    ]
     later = [pltpu.make_async_copy(measured.at[light], seen, sems.at[6])]
     later += [
         pltpu.make_async_copy(fields.at[slab, light], field.at[slab], sems.at[7 + slab])
         for slab in range(last)
+    ]
+    stores = [
+        pltpu.make_async_copy(psi.at[slab], psi_out.at[slab], sems.at[7 + slabs + slab])
+        for slab in range(slabs)
     ]
     for copy in copies + later:
         copy.start()
@@ -100,18 +99,22 @@
     for copy in copies:
         copy.wait()
     tilt(last)
+    stores[last].start()
     a_real, a_imag = s_near[last], i_near[last]
     f_real, f_imag = psi[last, 0], psi[last, 1]
+    for copy in later:
+        copy.wait()
+    for slab in range(last):
+        tilt(slab)
+        stores[slab].start()
     real, imag = adjoint(
         a_real * f_real - a_imag * f_imag, -(a_real * f_imag + a_imag * f_real), t_near
     )
-    for copy in later:
-        copy.wait()
     weight = 2.0 * (real * real + imag * imag - seen[...])
     out[0] = weight * real
     out[1] = -(weight * imag)
-    for slab in range(last):
-        tilt(slab)
+    for store in stores:
+        store.wait()
 
 
 def keep_body(flag, _, *refs):
@@ -129,15 +132,31 @@
             copy.wait()
 
 
-def section_body(scale, entries, chains, flag, *refs):
-    chis, refs = refs[:entries], refs[entries:]
-    s_real, s_imag, table, psi, *refs = refs
+def section_body(scale, kinds, flag, *refs):
+    arrives, comes, chains, leaves, near = kinds
+    refs = list(refs)
+    sems = refs.pop()
+    chi = refs.pop(0) if arrives else None
+    partner = refs.pop(0) if comes else None
+    s_real, s_imag, table, psi = refs[:4]
+    del refs[:4]
     if chains:
-        low_real, low_imag, grad_in, out, middle, grad, fields, screens, sems = refs
+        low_real, low_imag = refs[:2]
+        del refs[:2]
+    grad_in = refs.pop(0)
+    middle_out = refs.pop(0) if chains else None
+    if leaves:
+        out, grad = refs[:2]
+        del refs[:2]
     else:
-        grad_in, out, grad, fields, sems = refs
-    slabs = fields.shape[0]
-    shape = (grad.shape[0], grad.shape[3], grad.shape[4])
+        grad, out = refs[:2]
+        del refs[:2]
+    middle = refs.pop(0) if chains else None
+    if not near:
+        fields = refs.pop(0)
+    screens = refs.pop(0) if chains else None
+    slabs = psi.shape[0]
+    rows = grad.shape[3]
 
     def field_copy(slab):
         return pltpu.make_async_copy(psi.at[slab], fields.at[slab], sems.at[slab])
@@ -148,10 +167,15 @@
             pltpu.make_async_copy(low_imag.at[slab], screens.at[1, slab], sems.at[2 * slabs + slab]),
         ]
 
+    def add(slab, part, value):
+        blocks = value.reshape(grad.shape[0], rows, value.shape[1])
+        grad[:, slab, part] = grad_in[:, slab, part] + blocks
+
     @pl.when(flag[0] > 0)
     def _():
-        for slab in reversed(range(slabs)):
-            field_copy(slab).start()
+        if not near:
+            for slab in reversed(range(slabs)):
+                field_copy(slab).start()
         if chains:
 
             @pl.when(flag[0] == 1)
@@ -160,11 +184,19 @@
                     for copy in low_copies(slab):
                         copy.start()
 
-        for index, chi in enumerate(chis):
-
-            @pl.when(flag[0] == (index + 1 if entries > 1 or chains else flag[0]))
-            def _(chi=chi):
+        if arrives and comes:
+
+            @pl.when(flag[0] == 1)
+            def _():
                 out[...] = chi[...]
+
+            @pl.when(flag[0] == 2)
+            def _():
+                fetch = pltpu.make_async_copy(partner, out, sems.at[3 * slabs])
+                fetch.start()
+                fetch.wait()
+        else:
+            out[...] = chi[...] if arrives else partner[...]
 
         def step(index, carry):
             slab = slabs - 1 - index
@@ -172,20 +204,24 @@
             a_real, a_imag = s_real[slab], s_imag[slab]
             out[0] = a_real * real + a_imag * imag
             out[1] = a_real * imag - a_imag * real
-            field_copy(slab).wait()
-            p_real, p_imag = fields[slab, 0], fields[slab, 1]
-            g_real = scale * (p_real * real + p_imag * imag)
-            g_imag = scale * (p_real * imag - p_imag * real)
-            grad[:, slab, 0] = grad_in[:, slab, 0] + g_real.reshape(shape)
-            grad[:, slab, 1] = grad_in[:, slab, 1] + g_imag.reshape(shape)
+            if near:
+                p_real, p_imag = psi[slab, 0], psi[slab, 1]
+            else:
+                field_copy(slab).wait()
+                p_real, p_imag = fields[slab, 0], fields[slab, 1]
+            add(slab, 0, scale * (p_real * real + p_imag * imag))
+            add(slab, 1, scale * (p_real * imag - p_imag * real))
             return carry
 
         lax.fori_loop(0, slabs, step, 0)
         if chains:
-            middle[...] = out[...]
 
             @pl.when(flag[0] == 1)
             def _():
+                middle[...] = out[...]
+                store = pltpu.make_async_copy(middle, middle_out, sems.at[3 * slabs + 1])
+                store.start()
+
                 def onward(index, carry):
                     slab = slabs - 1 - index
                     real, imag = adjoint(out[0], out[1], table)
@@ -197,6 +233,7 @@
                     return carry
 
                 lax.fori_loop(0, slabs, onward, 0)
+                store.wait()
 
     @pl.when(flag[0] == 0)
     def _():
@@ -245,78 +282,109 @@
             name="keep",
         )(flag, far(after), *map(far, values))
 
-    def entry(light, s_real, s_imag, table):
-        first = light == 0
+    def entry(light):
         return pl.pallas_call(
             functools.partial(entry_body, light),
-            out_shape=[state_shape, psi_shape]
-            + ([like(s_real), like(s_imag), like(table)] if first else []),
-            in_specs=[HBM] + ([HBM] if first else [VMEM]) * 2 + [HBM, HBM if first else VMEM, VMEM, VMEM],
-            out_specs=[VMEM] * (5 if first else 2),
+            out_shape=[state_shape, pltpu.MemorySpace.HBM(psi_shape.shape, F32)]
+            + [like(value) for value in (screen_real, screen_imag, matrices)],
+            in_specs=[HBM] * 5 + [VMEM] * 2,
+            out_specs=[VMEM, HBM] + [VMEM] * 3,
             scratch_shapes=[
                 pltpu.VMEM((slabs, 2, extent, extent), BF16),
                 pltpu.VMEM((extent, extent), F32),
-                pltpu.SemaphoreType.DMA((7 + slabs,)),
+                pltpu.VMEM(psi_shape.shape, F32),
+                pltpu.SemaphoreType.DMA((7 + 2 * slabs,)),
             ],
             compiler_params=params,
             cost_estimate=cost(2),
             name="entry",
-        )(far(fields), *((far(s_real), far(s_imag)) if first else (s_real, s_imag)), far(measured),
-          far(table) if first else table, x_ramp[light], y_ramp[light])
-
-    def section(flag, chis, s_real, s_imag, table, psi, low, grad):
-        entries, chains = len(chis), low is not None
-        outs = 2 if chains else 1
-        aliased = 1 + entries + 4 + (2 if chains else 0)
+        )(*map(far, (fields, screen_real, screen_imag, measured, matrices)), x_ramp[light], y_ramp[light])
+
+    def section(flag, chi, partner, s_real, s_imag, table, psi, low, grad, leaves, near):
+        arrives, comes, chains = chi is not None, partner is not None, low is not None
+        where, place = (VMEM, lambda value: value) if near else (HBM, far)
+        operands = [(SMEM, flag)]
+        if arrives:
+            operands.append((VMEM, chi))
+        if comes:
+            operands.append((HBM, far(partner)) if arrives else (VMEM, partner))
+        operands += [(VMEM, s_real), (VMEM, s_imag), (VMEM, table), (where, place(psi))]
+        if chains:
+            operands += [(HBM, far(part)) for part in low]
+        operands.append((VMEM, grad))
+        results, scratch = [(VMEM, grad_shape)], []
+        if leaves:
+            results.insert(0, (VMEM, state_shape))
+        else:
+            scratch.append(pltpu.VMEM(state_shape.shape, F32))
+        if chains:
+            results.insert(0, (HBM, pltpu.MemorySpace.HBM(state_shape.shape, F32)))
+            scratch.append(pltpu.VMEM(state_shape.shape, F32))
+        if not near:
+            scratch.append(pltpu.VMEM(psi_shape.shape, F32))
+        if chains:
+            scratch.append(pltpu.VMEM((2, slabs, extent, extent), F32))
+        scratch.append(pltpu.SemaphoreType.DMA((3 * slabs + 2,)))
+        kinds = (arrives, comes, chains, leaves, near)
         return pl.pallas_call(
-            functools.partial(section_body, scale, entries, chains),
-            out_shape=[state_shape] * outs + [grad_shape],
-            in_specs=[SMEM] + [VMEM] * (entries + 3) + [HBM] * (3 if chains else 1) + [VMEM],
-            out_specs=[VMEM] * (outs + 1),
-            scratch_shapes=[pltpu.VMEM(psi_shape.shape, F32)]
-            + ([pltpu.VMEM((2, slabs, extent, extent), F32)] if chains else [])
-            + [pltpu.SemaphoreType.DMA((3 * slabs,))],
-            input_output_aliases={aliased: outs},
+            functools.partial(section_body, scale, kinds),
+            out_shape=[shape for _, shape in results],
+            in_specs=[spec for spec, _ in operands],
+            out_specs=[spec for spec, _ in results],
+            scratch_shapes=scratch,
+            input_output_aliases={len(operands) - 1: len(results) - 1},
             compiler_params=params,
-            cost_estimate=cost(slabs * outs),
+            cost_estimate=cost(slabs * (2 if chains else 1)),
             name="section",
-        )(flag, *chis, s_real, s_imag, table, far(psi), *([far(part) for part in low] if chains else []), grad)
+        )(*[value for _, value in operands])
 
     pairs = segments // 2
     swap = [(2 * c + 1, 2 * c) for c in range(pairs)] + [(2 * c, 2 * c + 1) for c in range(pairs)]
-    down = [(2 * c + 1, 2 * ((c - 1) % pairs) + 1) for c in range(pairs)]
     low = [lax.ppermute(screen_real, "depth", swap), lax.ppermute(screen_imag, "depth", swap)]
     matrices = jnp.asarray(operator_matrices(extent))
     upper = position % 2 == 1
     stage_of = pairs - 1 - position // 2
-    arrived, psis, near = [], [], [screen_real, screen_imag, matrices]
-    for light in range(lights):
-        chi, psi, *held = entry(light, *near)
-        near = held or near
-        arrived.append(chi)
-        psis.append(psi)
     grad = jnp.zeros(grad_shape.shape, F32)
-    middle = [None] * lights
-    for stage in range(pairs + 1):
+    arrived, middle, psis = [None] * lights, [None] * lights, [None] * lights
+
+    def taken(stage):
         first = jnp.logical_and(upper, stage_of == stage).astype(jnp.int32)[None]
         second = jnp.logical_and(jnp.logical_not(upper), stage_of == stage - 1)
-        second = second.astype(jnp.int32)[None]
-        flag = first + 2 * second if stage < pairs else second
-        if stage > 0:
-            near = keep(flag, before, screen_real, screen_imag, matrices)
+        return first, second.astype(jnp.int32)[None]
+
+    for stage in range(pairs - 1):
+        here = pairs - 1 - stage
+        first, second = taken(stage)
+        flag = first + 2 * second
         for light in range(lights):
-            chis = [value for value in (arrived[light], middle[light]) if value is not None]
-            left, *middles, grad = section(
-                flag, chis, *near, psis[light], low if stage < pairs - 1 else None, grad
+            if stage == 0:
+                arrived[light], psis[light], *near = entry(light)
+            else:
+                near = keep(flag, before, screen_real, screen_imag, matrices)
+            middle_now, before, grad = section(
+                flag, arrived[light], middle[light], *near, psis[light], low, grad, True, False
             )
-            if light == 0:
-                before = left
-            arrived[light] = middle[light] = None
-            if stage < pairs - 1:
-                arrived[light] = lax.ppermute(left, "depth", down)
-                middle[light] = lax.ppermute(middles[0], "depth", swap)
-            elif stage < pairs:
-                middle[light] = lax.ppermute(left, "depth", swap)
+            arrived[light] = lax.ppermute(before, "depth", [(2 * here + 1, 2 * here - 1)])
+            middle[light] = lax.ppermute(
+                middle_now, "depth", [(2 * here + 1, 2 * here), (2 * here, 2 * here + 1)]
+            )
+    first, second = taken(pairs - 1)
+    flag = first + 2 * second
+    lefts = []
+    for light in range(lights):
+        near = keep(flag, before, screen_real, screen_imag, matrices)
+        left, grad = section(
+            flag, arrived[light], middle[light], *near, psis[light], None, grad, True, False
+        )
+        before = left
+        lefts.append(left)
+    _, last = taken(pairs)
+    for light in range(lights):
+        near = keep(last, lefts[light], screen_real, screen_imag, matrices)
+        if light > 0:
+            lefts[light], grad = lax.optimization_barrier((lefts[light], grad))
+        handed = lax.ppermute(lefts[light], "depth", [(1, 0)])
+        (grad,) = section(last, None, handed, *near, psis[light], None, grad, False, False)
     return owned_sum(grad, groups, columns)
 
 

time: 134 us -> 127 us (0.948)
  starting transfers between devices: 85.3 us -> 37.9 us
  waiting for transfers between devices: 9.75 us -> 55.5 us
  Pallas kernels: 32 us -> 28.4 us
  local copies, waits for them, and re-layouts: 3.26 us -> 1.63 us
    ppermute x14, starting transfers between devices: 61.6 us -> 18.7 us  [the longest x6 8.82 us: on_device(): lax.ppermute(middle_now, 'depth', [(2 * here + 1, 2 * here), (2 * here, 2...]
    ppermute x14, waiting for transfers between devices: 0.04 us -> 38.3 us  [the longest x2 38.3 us: on_device(): handed = lax.ppermute(lefts[light], 'depth', [(1, 0)])]
    ppermute x7, waiting for transfers between devices: 5.55 us -> 15.2 us  [owned_sum(): total = total + lax.ppermute(block(c, d), 'illum', route)]
    pallas_call x10, Pallas kernels: 24.5 us -> 16.2 us  [section(): pl.pallas_call(functools.partial(section_body, scale, kinds), out_shape=[...]
    ppermute x7, starting transfers between devices: 13.1 us -> 7.79 us  [owned_sum(): total = total + lax.ppermute(block(c, d), 'illum', route)]
    pallas_call x2, Pallas kernels: 5.77 us -> 8.71 us  [entry(): pl.pallas_call(functools.partial(entry_body, light), out_shape=[state_sha...]
    ppermute x3, waiting for transfers between devices: 4.16 us -> 1.96 us  [owned_sum(): result = result + lax.ppermute(sent, 'illum', route)]
    pallas_call x4 -> x8, Pallas kernels: 1.71 us -> 3.45 us  [keep(): pl.pallas_call(keep_body, out_shape=[like(value) for value in values], in...]
  transfers between devices with their start and end apart: 26 -> 26, of which waited for: 4 -> 9; matrix products, arithmetic and copies ran while one was open for 1% -> 1% of each run, Pallas kernels for 19% -> 15%
where the time goes in v3:
time: 127 us
  waiting for transfers between devices  55.5 us (44%)
  starting transfers between devices  37.9 us (30%)
  Pallas kernels  28.4 us (22%)
  other arithmetic  2.64 us (2%)
  local copies, waits for them, and re-layouts  1.63 us (1%)
    ppermute x2, waiting for transfers between devices, on_device(): handed = lax.ppermute(lefts[light], 'depth', [(1, 0)])  38.3 us
    pallas_call x10, Pallas kernels, section(): pl.pallas_call(functools.partial(section_body, scale, kinds), out_shape=[...  16.2 us
    ppermute x7, waiting for transfers between devices, owned_sum(): total = total + lax.ppermute(block(c, d), 'illum', route)  15.2 us
    ppermute x3, starting transfers between devices, owned_sum(): result = result + lax.ppermute(sent, 'illum', route)  10.9 us
    ppermute x6, starting transfers between devices, on_device(): lax.ppermute(middle_now, 'depth', [(2 * here + 1, 2 * here), (2 * here, 2...  8.82 us
    pallas_call x2, Pallas kernels, entry(): pl.pallas_call(functools.partial(entry_body, light), out_shape=[state_sha...  8.71 us
    ppermute x7, starting transfers between devices, owned_sum(): total = total + lax.ppermute(block(c, d), 'illum', route)  7.79 us
    ppermute x6, starting transfers between devices, on_device(): lax.ppermute(before, 'depth', [(2 * here + 1, 2 * here - 1)])  7.27 us
  transfers between devices with their start and end apart: 26, of which 9 were waited for; matrix products, arithmetic and copies ran while one was open for 1% of the time, Pallas kernels for 15%

profile of v3, /device:TPU:32, one launch (start us, length us, event | category | flops | bytes accessed | tf_op | source)
XLA Modules:
  0.0 126.6 jit_solution(8811335636574799319)
XLA Ops:
  0.0 0.5 collective-permute-start.1
  0.5 0.7 fusion.25
  1.5 4.4 %entry.3 = (f32[2,256,256]{2,1,0:T(8,128)S(1)}, f32[3,2,256,256]{3,2,1,0:T(8,128)}, f32[3,256,256]{2,1,0:T(8,128)S(1)}, f32[3,256,256]{2,1,0:T(8,128)S(1)}, bf16[3,2,256,256]{3,2,1,0:T(8,128)(2,1)S(1)}) custom-call(bf16[3,2,2,256,256]{4,3,2,1,0:T(8,128)(2,1)} %fields.3, f32[3,256,256]{2,1,0:T(8,128)} %refs_0_.15, f32[3,256,256]{2,1,0:T(8,128)} %refs_1_.15, ...), custom_call_target="tpu_custom_call" | custom-call | flops 1207959552 | bytes 1048576 | tf_op jit(solution)/shard_map/entry/pallas_call | solution.py:286
  5.9 1.0 copy-done.8
  7.1 1.2 section.10
  8.3 1.5 %collective-permute-start.4 = (f32[2,256,256]{2,1,0:T(8,128)}, f32[2,256,256]{2,1,0:T(8,128)}, u32[]{:S(2)}, u32[]{:S(2)}) collective-permute-start(f32[2,256,256]{2,1,0:T(8,128)} %get-tuple-element.76), channel_id=1, source_target_pairs={{224,160},{225,161},{226,162},{227,163},{228,164},{229,165},{230,1... | collective-permute-start | bytes 1572872 | tf_op jit(solution)/shard_map/ppermute | solution.py:367
  9.8 1.5 %collective-permute-start.5 = (f32[2,256,256]{2,1,0:T(8,128)}, f32[2,256,256]{2,1,0:T(8,128)}, u32[]{:S(2)}, u32[]{:S(2)}) collective-permute-start(f32[2,256,256]{2,1,0:T(8,128)} %get-tuple-element.77), channel_id=1, source_target_pairs={{224,192},{192,224},{225,193},{193,225},{226,194},{194,226},{227,1... | collective-permute-start | bytes 1572872 | tf_op jit(solution)/shard_map/ppermute | solution.py:368
  11.4 4.3 %entry.2 = (f32[2,256,256]{2,1,0:T(8,128)S(1)}, f32[3,2,256,256]{3,2,1,0:T(8,128)}, f32[3,256,256]{2,1,0:T(8,128)S(1)}, f32[3,256,256]{2,1,0:T(8,128)S(1)}, bf16[3,2,256,256]{3,2,1,0:T(8,128)(2,1)S(1)}) custom-call(bf16[3,2,2,256,256]{4,3,2,1,0:T(8,128)(2,1)} %fields.3, f32[3,256,256]{2,1,0:T(8,128)} %refs_0_.15, f32[3,256,256]{2,1,0:T(8,128)} %refs_1_.15, ...), custom_call_target="tpu_custom_call" | custom-call | flops 1207959552 | bytes 1048576 | tf_op jit(solution)/shard_map/entry/pallas_call | solution.py:286
  16.1 0.7 collective-permute-start.2
  16.8 1.5 %collective-permute-start.3 = (f32[2,256,256]{2,1,0:T(8,128)}, f32[2,256,256]{2,1,0:T(8,128)}, u32[]{:S(2)}, u32[]{:S(2)}) collective-permute-start(f32[2,256,256]{2,1,0:T(8,128)} %get-tuple-element.75), channel_id=1, source_target_pairs={{224,192},{192,224},{225,193},{193,225},{226,194},{194,226},{227,1... | collective-permute-start | bytes 1572872 | tf_op jit(solution)/shard_map/ppermute | solution.py:368
  18.3 1.3 %section.12 = (f32[2,256,256]{2,1,0:T(8,128)}, f32[2,256,256]{2,1,0:T(8,128)S(1)}, f32[32,3,2,8,256]{4,3,2,1,0:T(8,128)S(1)}) custom-call(s32[1]{0:T(128)} %bitcast.3.flag, f32[2,256,256]{2,1,0:T(8,128)} %collective-permute-done.4.refs_0_, f32[2,256,256]{2,1,0:T(8,128)} %collective-permute-done.5.refs_1_, ...), custom_call_target="tpu_custom_call", output_to_operand_aliasing={{2}: (9, {})} | custom-call | flops 3623878656 | bytes 1048576 | tf_op jit(solution)/shard_map/section/pallas_call | solution.py:329
  19.7 1.5 %collective-permute-start.8 = (f32[2,256,256]{2,1,0:T(8,128)S(1)}, f32[2,256,256]{2,1,0:T(8,128)}, u32[]{:S(2)}, u32[]{:S(2)}) collective-permute-start(f32[2,256,256]{2,1,0:T(8,128)S(1)} %get-tuple-element.82._), channel_id=1, source_target_pairs={{160,96},{161,97},{162,98},{163,99},{164,100},{165,101},{166,102},... | collective-permute-start | bytes 1572872 | tf_op jit(solution)/shard_map/ppermute | solution.py:367
  21.1 1.5 %collective-permute-start.9 = (f32[2,256,256]{2,1,0:T(8,128)}, f32[2,256,256]{2,1,0:T(8,128)}, u32[]{:S(2)}, u32[]{:S(2)}) collective-permute-start(f32[2,256,256]{2,1,0:T(8,128)} %get-tuple-element.89), channel_id=1, source_target_pairs={{160,128},{128,160},{161,129},{129,161},{162,130},{130,162},{163,1... | collective-permute-start | bytes 1572872 | tf_op jit(solution)/shard_map/ppermute | solution.py:368
  22.7 0.5 section.13
  23.2 0.7 collective-permute-start.6
  23.9 1.5 %collective-permute-start.7 = (f32[2,256,256]{2,1,0:T(8,128)}, f32[2,256,256]{2,1,0:T(8,128)}, u32[]{:S(2)}, u32[]{:S(2)}) collective-permute-start(f32[2,256,256]{2,1,0:T(8,128)} %get-tuple-element.88), channel_id=1, source_target_pairs={{160,128},{128,160},{161,129},{129,161},{162,130},{130,162},{163,1... | collective-permute-start | bytes 1572872 | tf_op jit(solution)/shard_map/ppermute | solution.py:368
  25.5 1.3 %section.14 = (f32[2,256,256]{2,1,0:T(8,128)}, f32[2,256,256]{2,1,0:T(8,128)S(1)}, f32[32,3,2,8,256]{4,3,2,1,0:T(8,128)S(1)}) custom-call(s32[1]{0:T(128)} %bitcast.2.flag, f32[2,256,256]{2,1,0:T(8,128)} %collective-permute-done.8.refs_0_, f32[2,256,256]{2,1,0:T(8,128)} %collective-permute-done.9.refs_1_, ...), custom_call_target="tpu_custom_call", output_to_operand_aliasing={{2}: (9, {})} | custom-call | flops 3623878656 | bytes 1048576 | tf_op jit(solution)/shard_map/section/pallas_call | solution.py:329
  26.8 1.5 %collective-permute-start.12 = (f32[2,256,256]{2,1,0:T(8,128)S(1)}, f32[2,256,256]{2,1,0:T(8,128)}, u32[]{:S(2)}, u32[]{:S(2)}) collective-permute-start(f32[2,256,256]{2,1,0:T(8,128)S(1)} %get-tuple-element.94._), channel_id=1, source_target_pairs={{96,32},{97,33},{98,34},{99,35},{100,36},{101,37},{102,38},{103,39... | collective-permute-start | bytes 1572872 | tf_op jit(solution)/shard_map/ppermute | solution.py:367
  28.3 1.5 %collective-permute-start.13 = (f32[2,256,256]{2,1,0:T(8,128)}, f32[2,256,256]{2,1,0:T(8,128)}, u32[]{:S(2)}, u32[]{:S(2)}) collective-permute-start(f32[2,256,256]{2,1,0:T(8,128)} %get-tuple-element.101), channel_id=1, source_target_pairs={{96,64},{64,96},{97,65},{65,97},{98,66},{66,98},{99,67},{67,99},{1... | collective-permute-start | bytes 1572872 | tf_op jit(solution)/shard_map/ppermute | solution.py:368
  29.8 0.3 section.15
  30.1 1.5 %collective-permute-start.10 = (f32[2,256,256]{2,1,0:T(8,128)S(1)}, f32[2,256,256]{2,1,0:T(8,128)}, u32[]{:S(2)}, u32[]{:S(2)}) collective-permute-start(f32[2,256,256]{2,1,0:T(8,128)S(1)} %get-tuple-element.99._), channel_id=1, source_target_pairs={{96,32},{97,33},{98,34},{99,35},{100,36},{101,37},{102,38},{103,39... | collective-permute-start | bytes 1572872 | tf_op jit(solution)/shard_map/ppermute | solution.py:367
  31.6 1.4 %collective-permute-start.11 = (f32[2,256,256]{2,1,0:T(8,128)}, f32[2,256,256]{2,1,0:T(8,128)}, u32[]{:S(2)}, u32[]{:S(2)}) collective-permute-start(f32[2,256,256]{2,1,0:T(8,128)} %get-tuple-element.100), channel_id=1, source_target_pairs={{96,64},{64,96},{97,65},{65,97},{98,66},{66,98},{99,67},{67,99},{1... | collective-permute-start | bytes 1572872 | tf_op jit(solution)/shard_map/ppermute | solution.py:368
  33.1 1.3 %section.16 = (f32[2,256,256]{2,1,0:T(8,128)S(1)}, f32[32,3,2,8,256]{4,3,2,1,0:T(8,128)S(1)}) custom-call(s32[1]{0:T(128)} %bitcast.1.flag, f32[2,256,256]{2,1,0:T(8,128)} %collective-permute-done.12.refs_0_, f32[2,256,256]{2,1,0:T(8,128)} %collective-permute-done.13.refs_1_, ...), custom_call_target="tpu_custom_call", output_to_operand_aliasing={{1}: (7, {})} | custom-call | flops 1811939328 | bytes 1048576 | tf_op jit(solution)/shard_map/section/pallas_call | solution.py:329
  34.5 1.3 %collective-permute-start.14 = (f32[2,256,256]{2,1,0:T(8,128)S(1)}, f32[2,256,256]{2,1,0:T(8,128)S(1)}, u32[]{:S(2)}, u32[]{:S(2)}) collective-permute-start(f32[2,256,256]{2,1,0:T(8,128)S(1)} %get-tuple-element.106._), channel_id=1, source_target_pairs={{32,0},{33,1},{34,2},{35,3},{36,4},{37,5},{38,6},{39,7},{40,8},{41... | collective-permute-start | bytes 1572872 | tf_op jit(solution)/shard_map/ppermute | solution.py:386
  35.8 1.6 %keep.14 = (f32[3,256,256]{2,1,0:T(8,128)S(1)}, f32[3,256,256]{2,1,0:T(8,128)S(1)}, bf16[3,2,256,256]{3,2,1,0:T(8,128)(2,1)S(1)}) custom-call(s32[1]{0:T(128)} %bitcast.flag, f32[2,256,256]{2,1,0:T(8,128)} %copy-done, f32[3,256,256]{2,1,0:T(8,128)} %refs_0_.15, f32[3,256,256]{2,1,0:T(8,128)} %refs_1_.15, bf16[3,2,256,256]{3,2,1,0:T(8,128)(2,1)} %constant.488.clone.table.refs_2_), custom_call_target="tpu_custom_call" | custom-call | flops 603979776 | bytes 1048576 | tf_op jit(solution)/shard_map/keep/pallas_call | solution.py:274
  37.5 1.3 %section.17 = (f32[2,256,256]{2,1,0:T(8,128)S(1)}, f32[32,3,2,8,256]{4,3,2,1,0:T(8,128)S(1)}) custom-call(s32[1]{0:T(128)} %bitcast.1.flag, f32[2,256,256]{2,1,0:T(8,128)} %collective-permute-done.10.refs_0_, f32[2,256,256]{2,1,0:T(8,128)} %collective-permute-done.11.refs_1_, ...), custom_call_target="tpu_custom_call", output_to_operand_aliasing={{1}: (7, {})} | custom-call | flops 1811939328 | bytes 1048576 | tf_op jit(solution)/shard_map/section/pallas_call | solution.py:329
  38.9 30.7 %collective-permute-done.14.refs_0_ = f32[2,256,256]{2,1,0:T(8,128)S(1)} collective-permute-done((f32[2,256,256]{2,1,0:T(8,128)S(1)}, f32[2,256,256]{2,1,0:T(8,128)S(1)}, u32[]{:S(2)}, u32[]{:S(2)}) %collective-permute-start.14) | collective-permute-done | bytes 524320 | tf_op jit(solution)/shard_map/ppermute | solution.py:386
  69.5 4.2 %section.18.refs_5_ = f32[32,3,2,8,256]{4,3,2,1,0:T(8,128)S(1)} custom-call(s32[1]{0:T(128)} %bitcast.flag, f32[2,256,256]{2,1,0:T(8,128)S(1)} %collective-permute-done.14.refs_0_, f32[3,256,256]{2,1,0:T(8,128)S(1)} %get-tuple-element.112.refs_1_, f32[3,256,256]{2,1,0:T(8,128)S(1)} %get-tuple-element.113.refs_2_, ...), custom_call_target="tpu_custom_call", output_to_operand_aliasing={{}: (6, {})} | custom-call | flops 1811939328 | bytes 1048576 | tf_op jit(solution)/shard_map/section/pallas_call | solution.py:329
  73.8 1.3 %collective-permute-start.15 = (f32[2,256,256]{2,1,0:T(8,128)S(1)}, f32[2,256,256]{2,1,0:T(8,128)S(1)}, u32[]{:S(2)}, u32[]{:S(2)}) collective-permute-start(f32[2,256,256]{2,1,0:T(8,128)S(1)} %get-tuple-element.116._), channel_id=1, source_target_pairs={{32,0},{33,1},{34,2},{35,3},{36,4},{37,5},{38,6},{39,7},{40,8},{41... | collective-permute-start | bytes 1572872 | tf_op jit(solution)/shard_map/ppermute | solution.py:386
  75.2 1.6 %keep.15 = (f32[3,256,256]{2,1,0:T(8,128)S(1)}, f32[3,256,256]{2,1,0:T(8,128)S(1)}, bf16[3,2,256,256]{3,2,1,0:T(8,128)(2,1)S(1)}) custom-call(s32[1]{0:T(128)} %bitcast.flag, f32[2,256,256]{2,1,0:T(8,128)} %copy-done.1, f32[3,256,256]{2,1,0:T(8,128)} %refs_0_.15, f32[3,256,256]{2,1,0:T(8,128)} %refs_1_.15, bf16[3,2,256,256]{3,2,1,0:T(8,128)(2,1)} %constant.488.clone.table.refs_2_), custom_call_target="tpu_custom_call" | custom-call | flops 603979776 | bytes 1048576 | tf_op jit(solution)/shard_map/keep/pallas_call | solution.py:274
  76.9 7.6 %collective-permute-done.15.refs_0_ = f32[2,256,256]{2,1,0:T(8,128)S(1)} collective-permute-done((f32[2,256,256]{2,1,0:T(8,128)S(1)}, f32[2,256,256]{2,1,0:T(8,128)S(1)}, u32[]{:S(2)}, u32[]{:S(2)}) %collective-permute-start.15) | collective-permute-done | bytes 524320 | tf_op jit(solution)/shard_map/ppermute | solution.py:386
  84.5 4.2 %section.19 = f32[32,3,2,8,256]{4,3,2,1,0:T(8,128)S(1)} custom-call(s32[1]{0:T(128)} %bitcast.flag, f32[2,256,256]{2,1,0:T(8,128)S(1)} %collective-permute-done.15.refs_0_, f32[3,256,256]{2,1,0:T(8,128)S(1)} %get-tuple-element.117.refs_1_, f32[3,256,256]{2,1,0:T(8,128)S(1)} %get-tuple-element.118.refs_2_, ...), custom_call_target="tpu_custom_call", output_to_operand_aliasing={{}: (6, {})} | custom-call | flops 1811939328 | bytes 1048576 | tf_op jit(solution)/shard_map/section/pallas_call | solution.py:329
  88.9 1.6 %collective-permute-start.16 = (f32[4,3,2,8,256]{4,3,2,1,0:T(8,128)S(1)}, f32[4,3,2,8,256]{4,3,2,1,0:T(8,128)S(1)}, u32[]{:S(2)}, u32[]{:S(2)}) collective-permute-start(f32[4,3,2,8,256]{4,3,2,1,0:T(8,128)S(1)} %get-tuple-element.121), channel_id=1, source_target_pairs={{0,8},{1,9},{2,10},{3,11},{4,12},{5,13},{6,14},{7,15},{8,16},{9,17... | collective-permute-start | bytes 589832 | tf_op jit(solution)/shard_map/ppermute | solution.py:412
  90.5 2.7 %collective-permute-start.17 = (f32[4,3,2,8,256]{4,3,2,1,0:T(8,128)S(1)}, f32[4,3,2,8,256]{4,3,2,1,0:T(8,128)S(1)}, u32[]{:S(2)}, u32[]{:S(2)}) collective-permute-start(f32[4,3,2,8,256]{4,3,2,1,0:T(8,128)S(1)} %get-tuple-element.127), channel_id=1, source_target_pairs={{0,16},{1,17},{2,18},{3,19},{4,20},{5,21},{6,22},{7,23},{8,24},{9,... | collective-permute-start | bytes 589832 | tf_op jit(solution)/shard_map/ppermute | solution.py:412
  93.2 1.4 %collective-permute-start.18 = (f32[4,3,2,8,256]{4,3,2,1,0:T(8,128)S(1)}, f32[4,3,2,8,256]{4,3,2,1,0:T(8,128)S(1)}, u32[]{:S(2)}, u32[]{:S(2)}) collective-permute-start(f32[4,3,2,8,256]{4,3,2,1,0:T(8,128)S(1)} %get-tuple-element.126), channel_id=1, source_target_pairs={{0,24},{1,25},{2,26},{3,27},{4,28},{5,29},{6,30},{7,31},{8,0},{9,1... | collective-permute-start | bytes 589832 | tf_op jit(solution)/shard_map/ppermute | solution.py:412
  94.7 1.9 %collective-permute-start.20 = (f32[4,3,2,8,256]{4,3,2,1,0:T(8,128)S(1)}, f32[4,3,2,8,256]{4,3,2,1,0:T(8,128)S(1)}, u32[]{:S(2)}, u32[]{:S(2)}) collective-permute-start(f32[4,3,2,8,256]{4,3,2,1,0:T(8,128)S(1)} %get-tuple-element.124), channel_id=1, source_target_pairs={{0,9},{1,8},{2,11},{3,10},{4,13},{5,12},{6,15},{7,14},{8,17},{9,16... | collective-permute-start | bytes 589832 | tf_op jit(solution)/shard_map/ppermute | solution.py:412
  96.7 3.8 %collective-permute-done.16 = f32[4,3,2,8,256]{4,3,2,1,0:T(8,128)S(1)} collective-permute-done((f32[4,3,2,8,256]{4,3,2,1,0:T(8,128)S(1)}, f32[4,3,2,8,256]{4,3,2,1,0:T(8,128)S(1)}, u32[]{:S(2)}, u32[]{:S(2)}) %collective-permute-start.16) | collective-permute-done | bytes 196640 | tf_op jit(solution)/shard_map/ppermute | solution.py:412
  100.5 3.7 %collective-permute-done.17 = f32[4,3,2,8,256]{4,3,2,1,0:T(8,128)S(1)} collective-permute-done((f32[4,3,2,8,256]{4,3,2,1,0:T(8,128)S(1)}, f32[4,3,2,8,256]{4,3,2,1,0:T(8,128)S(1)}, u32[]{:S(2)}, u32[]{:S(2)}) %collective-permute-start.17) | collective-permute-done | bytes 196640 | tf_op jit(solution)/shard_map/ppermute | solution.py:412
  104.2 1.0 collective-permute-done.20
  105.3 3.4 %collective-permute-done.21 = f32[4,3,2,8,256]{4,3,2,1,0:T(8,128)} collective-permute-done((f32[4,3,2,8,256]{4,3,2,1,0:T(8,128)S(1)}, f32[4,3,2,8,256]{4,3,2,1,0:T(8,128)}, u32[]{:S(2)}, u32[]{:S(2)}) %collective-permute-start.21) | collective-permute-done | bytes 196640 | tf_op jit(solution)/shard_map/ppermute | solution.py:412
  108.7 3.3 %collective-permute-done.22 = f32[4,3,2,8,256]{4,3,2,1,0:T(8,128)} collective-permute-done((f32[4,3,2,8,256]{4,3,2,1,0:T(8,128)S(1)}, f32[4,3,2,8,256]{4,3,2,1,0:T(8,128)}, u32[]{:S(2)}, u32[]{:S(2)}) %collective-permute-start.22) | collective-permute-done | bytes 196640 | tf_op jit(solution)/shard_map/ppermute | solution.py:412
  111.9 1.2 fusion.5
  113.1 3.7 %collective-permute-start.23 = (f32[3,2,8,256]{3,2,1,0:T(8,128)S(1)}, f32[3,2,8,256]{3,2,1,0:T(8,128)S(1)}, u32[]{:S(2)}, u32[]{:S(2)}) collective-permute-start(f32[3,2,8,256]{3,2,1,0:T(8,128)S(1)} %get-tuple-element.128), channel_id=1, source_target_pairs={{0,2},{1,3},{2,4},{3,5},{4,6},{5,7},{6,0},{7,1},{8,10},{9,11},{10,... | collective-permute-start | bytes 147464 | tf_op jit(solution)/shard_map/ppermute | solution.py:417
  116.9 4.1 %collective-permute-start.24 = (f32[3,2,8,256]{3,2,1,0:T(8,128)S(1)}, f32[3,2,8,256]{3,2,1,0:T(8,128)S(1)}, u32[]{:S(2)}, u32[]{:S(2)}) collective-permute-start(f32[3,2,8,256]{3,2,1,0:T(8,128)S(1)} %get-tuple-element.130), channel_id=1, source_target_pairs={{0,4},{1,5},{2,6},{3,7},{4,0},{5,1},{6,2},{7,3},{8,12},{9,13},{10,... | collective-permute-start | bytes 147464 | tf_op jit(solution)/shard_map/ppermute | solution.py:417
  121.0 3.0 %collective-permute-start.25 = (f32[3,2,8,256]{3,2,1,0:T(8,128)S(1)}, f32[3,2,8,256]{3,2,1,0:T(8,128)S(1)}, u32[]{:S(2)}, u32[]{:S(2)}) collective-permute-start(f32[3,2,8,256]{3,2,1,0:T(8,128)S(1)} %get-tuple-element.129), channel_id=1, source_target_pairs={{0,6},{1,7},{2,0},{3,1},{4,2},{5,3},{6,4},{7,5},{8,14},{9,15},{10,... | collective-permute-start | bytes 147464 | tf_op jit(solution)/shard_map/ppermute | solution.py:417
  124.0 0.9 collective-permute-done.24
  125.0 1.0 collective-permute-done.25
  126.0 0.6 fusion.7
  (53 shorter events, 1.5 us)
Async XLA Ops:
  0.0 5.9 %collective-permute-start = (f32[3,256,256]{2,1,0:T(8,128)}, f32[3,256,256]{2,1,0:T(8,128)S(1)}, u32[]{:S(2)}, u32[]{:S(2)}) collective-permute-start(f32[3,256,256]{2,1,0:T(8,128)} %refs_0_.15), channel_id=1, source_target_pairs={{32,0},{96,64},{160,128},{224,192},{0,32},{64,96},{128,160},{192,2... | collective-permute-start | bytes 2359304 | tf_op jit(solution)/shard_map/ppermute | solution.py:343
  0.0 5.9 %collective-permute-start.1 = (f32[3,256,256]{2,1,0:T(8,128)}, f32[3,256,256]{2,1,0:T(8,128)S(1)}, u32[]{:S(2)}, u32[]{:S(2)}) collective-permute-start(f32[3,256,256]{2,1,0:T(8,128)} %refs_1_.15), channel_id=1, source_target_pairs={{32,0},{96,64},{160,128},{224,192},{0,32},{64,96},{128,160},{192,2... | collective-permute-start | bytes 2359304 | tf_op jit(solution)/shard_map/ppermute | solution.py:343
  5.9 1.2 copy-start.7
  5.9 1.0 copy-start.8
  8.3 10.0 %collective-permute-start.4 = (f32[2,256,256]{2,1,0:T(8,128)}, f32[2,256,256]{2,1,0:T(8,128)}, u32[]{:S(2)}, u32[]{:S(2)}) collective-permute-start(f32[2,256,256]{2,1,0:T(8,128)} %get-tuple-element.76), channel_id=1, source_target_pairs={{224,160},{225,161},{226,162},{227,163},{228,164},{229,165},{230,1... | collective-permute-start | bytes 1572872 | tf_op jit(solution)/shard_map/ppermute | solution.py:367
  9.8 8.5 %collective-permute-start.5 = (f32[2,256,256]{2,1,0:T(8,128)}, f32[2,256,256]{2,1,0:T(8,128)}, u32[]{:S(2)}, u32[]{:S(2)}) collective-permute-start(f32[2,256,256]{2,1,0:T(8,128)} %get-tuple-element.77), channel_id=1, source_target_pairs={{224,192},{192,224},{225,193},{193,225},{226,194},{194,226},{227,1... | collective-permute-start | bytes 1572872 | tf_op jit(solution)/shard_map/ppermute | solution.py:368
  16.1 2.2 %copy-start.5 = (f32[2,256,256]{2,1,0:T(8,128)}, f32[2,256,256]{2,1,0:T(8,128)S(1)}, u32[]{:S(2)}) copy-start(f32[2,256,256]{2,1,0:T(8,128)S(1)} %get-tuple-element.74._) | copy-start | bytes 1572868
  16.1 6.6 %collective-permute-start.2 = (f32[2,256,256]{2,1,0:T(8,128)S(1)}, f32[2,256,256]{2,1,0:T(8,128)S(1)}, u32[]{:S(2)}, u32[]{:S(2)}) collective-permute-start(f32[2,256,256]{2,1,0:T(8,128)S(1)} %get-tuple-element.74._), channel_id=1, source_target_pairs={{224,160},{225,161},{226,162},{227,163},{228,164},{229,165},{230,1... | collective-permute-start | bytes 1572872 | tf_op jit(solution)/shard_map/ppermute | solution.py:367
  16.8 5.9 %collective-permute-start.3 = (f32[2,256,256]{2,1,0:T(8,128)}, f32[2,256,256]{2,1,0:T(8,128)}, u32[]{:S(2)}, u32[]{:S(2)}) collective-permute-start(f32[2,256,256]{2,1,0:T(8,128)} %get-tuple-element.75), channel_id=1, source_target_pairs={{224,192},{192,224},{225,193},{193,225},{226,194},{194,226},{227,1... | collective-permute-start | bytes 1572872 | tf_op jit(solution)/shard_map/ppermute | solution.py:368
  19.7 3.0 %copy-start.4 = (f32[2,256,256]{2,1,0:T(8,128)}, f32[2,256,256]{2,1,0:T(8,128)S(1)}, u32[]{:S(2)}) copy-start(f32[2,256,256]{2,1,0:T(8,128)S(1)} %get-tuple-element.82._) | copy-start | bytes 1572868
  19.7 5.8 %collective-permute-start.8 = (f32[2,256,256]{2,1,0:T(8,128)S(1)}, f32[2,256,256]{2,1,0:T(8,128)}, u32[]{:S(2)}, u32[]{:S(2)}) collective-permute-start(f32[2,256,256]{2,1,0:T(8,128)S(1)} %get-tuple-element.82._), channel_id=1, source_target_pairs={{160,96},{161,97},{162,98},{163,99},{164,100},{165,101},{166,102},... | collective-permute-start | bytes 1572872 | tf_op jit(solution)/shard_map/ppermute | solution.py:367
  21.1 4.3 %collective-permute-start.9 = (f32[2,256,256]{2,1,0:T(8,128)}, f32[2,256,256]{2,1,0:T(8,128)}, u32[]{:S(2)}, u32[]{:S(2)}) collective-permute-start(f32[2,256,256]{2,1,0:T(8,128)} %get-tuple-element.89), channel_id=1, source_target_pairs={{160,128},{128,160},{161,129},{129,161},{162,130},{130,162},{163,1... | collective-permute-start | bytes 1572872 | tf_op jit(solution)/shard_map/ppermute | solution.py:368
  23.2 2.2 %copy-start.3 = (f32[2,256,256]{2,1,0:T(8,128)}, f32[2,256,256]{2,1,0:T(8,128)S(1)}, u32[]{:S(2)}) copy-start(f32[2,256,256]{2,1,0:T(8,128)S(1)} %get-tuple-element.87._) | copy-start | bytes 1572868
  23.2 6.6 %collective-permute-start.6 = (f32[2,256,256]{2,1,0:T(8,128)S(1)}, f32[2,256,256]{2,1,0:T(8,128)S(1)}, u32[]{:S(2)}, u32[]{:S(2)}) collective-permute-start(f32[2,256,256]{2,1,0:T(8,128)S(1)} %get-tuple-element.87._), channel_id=1, source_target_pairs={{160,96},{161,97},{162,98},{163,99},{164,100},{165,101},{166,102},... | collective-permute-start | bytes 1572872 | tf_op jit(solution)/shard_map/ppermute | solution.py:367
  23.9 5.9 %collective-permute-start.7 = (f32[2,256,256]{2,1,0:T(8,128)}, f32[2,256,256]{2,1,0:T(8,128)}, u32[]{:S(2)}, u32[]{:S(2)}) collective-permute-start(f32[2,256,256]{2,1,0:T(8,128)} %get-tuple-element.88), channel_id=1, source_target_pairs={{160,128},{128,160},{161,129},{129,161},{162,130},{130,162},{163,1... | collective-permute-start | bytes 1572872 | tf_op jit(solution)/shard_map/ppermute | solution.py:368
  26.8 2.9 %copy-start.2 = (f32[2,256,256]{2,1,0:T(8,128)}, f32[2,256,256]{2,1,0:T(8,128)S(1)}, u32[]{:S(2)}) copy-start(f32[2,256,256]{2,1,0:T(8,128)S(1)} %get-tuple-element.94._) | copy-start | bytes 1572868
  26.8 6.3 %collective-permute-start.12 = (f32[2,256,256]{2,1,0:T(8,128)S(1)}, f32[2,256,256]{2,1,0:T(8,128)}, u32[]{:S(2)}, u32[]{:S(2)}) collective-permute-start(f32[2,256,256]{2,1,0:T(8,128)S(1)} %get-tuple-element.94._), channel_id=1, source_target_pairs={{96,32},{97,33},{98,34},{99,35},{100,36},{101,37},{102,38},{103,39... | collective-permute-start | bytes 1572872 | tf_op jit(solution)/shard_map/ppermute | solution.py:367
  28.3 4.8 %collective-permute-start.13 = (f32[2,256,256]{2,1,0:T(8,128)}, f32[2,256,256]{2,1,0:T(8,128)}, u32[]{:S(2)}, u32[]{:S(2)}) collective-permute-start(f32[2,256,256]{2,1,0:T(8,128)} %get-tuple-element.101), channel_id=1, source_target_pairs={{96,64},{64,96},{97,65},{65,97},{98,66},{66,98},{99,67},{67,99},{1... | collective-permute-start | bytes 1572872 | tf_op jit(solution)/shard_map/ppermute | solution.py:368
  30.1 2.9 %copy-start.6 = (f32[2,256,256]{2,1,0:T(8,128)}, f32[2,256,256]{2,1,0:T(8,128)S(1)}, u32[]{:S(2)}) copy-start(f32[2,256,256]{2,1,0:T(8,128)S(1)} %get-tuple-element.99._) | copy-start | bytes 1572868
  30.1 7.3 %collective-permute-start.10 = (f32[2,256,256]{2,1,0:T(8,128)S(1)}, f32[2,256,256]{2,1,0:T(8,128)}, u32[]{:S(2)}, u32[]{:S(2)}) collective-permute-start(f32[2,256,256]{2,1,0:T(8,128)S(1)} %get-tuple-element.99._), channel_id=1, source_target_pairs={{96,32},{97,33},{98,34},{99,35},{100,36},{101,37},{102,38},{103,39... | collective-permute-start | bytes 1572872 | tf_op jit(solution)/shard_map/ppermute | solution.py:367
  31.6 5.9 %collective-permute-start.11 = (f32[2,256,256]{2,1,0:T(8,128)}, f32[2,256,256]{2,1,0:T(8,128)}, u32[]{:S(2)}, u32[]{:S(2)}) collective-permute-start(f32[2,256,256]{2,1,0:T(8,128)} %get-tuple-element.100), channel_id=1, source_target_pairs={{96,64},{64,96},{97,65},{65,97},{98,66},{66,98},{99,67},{67,99},{1... | collective-permute-start | bytes 1572872 | tf_op jit(solution)/shard_map/ppermute | solution.py:368
  34.5 1.3 %copy-start = (f32[2,256,256]{2,1,0:T(8,128)}, f32[2,256,256]{2,1,0:T(8,128)S(1)}, u32[]{:S(2)}) copy-start(f32[2,256,256]{2,1,0:T(8,128)S(1)} %get-tuple-element.106._) | copy-start | bytes 1572868
  34.5 35.1 %collective-permute-start.14 = (f32[2,256,256]{2,1,0:T(8,128)S(1)}, f32[2,256,256]{2,1,0:T(8,128)S(1)}, u32[]{:S(2)}, u32[]{:S(2)}) collective-permute-start(f32[2,256,256]{2,1,0:T(8,128)S(1)} %get-tuple-element.106._), channel_id=1, source_target_pairs={{32,0},{33,1},{34,2},{35,3},{36,4},{37,5},{38,6},{39,7},{40,8},{41... | collective-permute-start | bytes 1572872 | tf_op jit(solution)/shard_map/ppermute | solution.py:386
  38.9 34.9 %copy-start.1 = (f32[2,256,256]{2,1,0:T(8,128)}, f32[2,256,256]{2,1,0:T(8,128)S(1)}, u32[]{:S(2)}) copy-start(f32[2,256,256]{2,1,0:T(8,128)S(1)} %get-tuple-element.116._) | copy-start | bytes 1572868
  73.8 10.7 %collective-permute-start.15 = (f32[2,256,256]{2,1,0:T(8,128)S(1)}, f32[2,256,256]{2,1,0:T(8,128)S(1)}, u32[]{:S(2)}, u32[]{:S(2)}) collective-permute-start(f32[2,256,256]{2,1,0:T(8,128)S(1)} %get-tuple-element.116._), channel_id=1, source_target_pairs={{32,0},{33,1},{34,2},{35,3},{36,4},{37,5},{38,6},{39,7},{40,8},{41... | collective-permute-start | bytes 1572872 | tf_op jit(solution)/shard_map/ppermute | solution.py:386
  88.9 11.6 %collective-permute-start.16 = (f32[4,3,2,8,256]{4,3,2,1,0:T(8,128)S(1)}, f32[4,3,2,8,256]{4,3,2,1,0:T(8,128)S(1)}, u32[]{:S(2)}, u32[]{:S(2)}) collective-permute-start(f32[4,3,2,8,256]{4,3,2,1,0:T(8,128)S(1)} %get-tuple-element.121), channel_id=1, source_target_pairs={{0,8},{1,9},{2,10},{3,11},{4,12},{5,13},{6,14},{7,15},{8,16},{9,17... | collective-permute-start | bytes 589832 | tf_op jit(solution)/shard_map/ppermute | solution.py:412
  90.5 13.7 %collective-permute-start.17 = (f32[4,3,2,8,256]{4,3,2,1,0:T(8,128)S(1)}, f32[4,3,2,8,256]{4,3,2,1,0:T(8,128)S(1)}, u32[]{:S(2)}, u32[]{:S(2)}) collective-permute-start(f32[4,3,2,8,256]{4,3,2,1,0:T(8,128)S(1)} %get-tuple-element.127), channel_id=1, source_target_pairs={{0,16},{1,17},{2,18},{3,19},{4,20},{5,21},{6,22},{7,23},{8,24},{9,... | collective-permute-start | bytes 589832 | tf_op jit(solution)/shard_map/ppermute | solution.py:412
  93.2 11.0 %collective-permute-start.18 = (f32[4,3,2,8,256]{4,3,2,1,0:T(8,128)S(1)}, f32[4,3,2,8,256]{4,3,2,1,0:T(8,128)S(1)}, u32[]{:S(2)}, u32[]{:S(2)}) collective-permute-start(f32[4,3,2,8,256]{4,3,2,1,0:T(8,128)S(1)} %get-tuple-element.126), channel_id=1, source_target_pairs={{0,24},{1,25},{2,26},{3,27},{4,28},{5,29},{6,30},{7,31},{8,0},{9,1... | collective-permute-start | bytes 589832 | tf_op jit(solution)/shard_map/ppermute | solution.py:412
  94.6 9.6 %collective-permute-start.19 = (f32[4,3,2,8,256]{4,3,2,1,0:T(8,128)S(1)}, f32[4,3,2,8,256]{4,3,2,1,0:T(8,128)S(1)}, u32[]{:S(2)}, u32[]{:S(2)}) collective-permute-start(f32[4,3,2,8,256]{4,3,2,1,0:T(8,128)S(1)} %get-tuple-element.125), channel_id=1, source_target_pairs={{0,1},{1,0},{2,3},{3,2},{4,5},{5,4},{6,7},{7,6},{8,9},{9,8},{10,11... | collective-permute-start | bytes 589832 | tf_op jit(solution)/shard_map/ppermute | solution.py:412
  94.7 10.5 %collective-permute-start.20 = (f32[4,3,2,8,256]{4,3,2,1,0:T(8,128)S(1)}, f32[4,3,2,8,256]{4,3,2,1,0:T(8,128)S(1)}, u32[]{:S(2)}, u32[]{:S(2)}) collective-permute-start(f32[4,3,2,8,256]{4,3,2,1,0:T(8,128)S(1)} %get-tuple-element.124), channel_id=1, source_target_pairs={{0,9},{1,8},{2,11},{3,10},{4,13},{5,12},{6,15},{7,14},{8,17},{9,16... | collective-permute-start | bytes 589832 | tf_op jit(solution)/shard_map/ppermute | solution.py:412
  100.5 8.2 %collective-permute-start.21 = (f32[4,3,2,8,256]{4,3,2,1,0:T(8,128)S(1)}, f32[4,3,2,8,256]{4,3,2,1,0:T(8,128)}, u32[]{:S(2)}, u32[]{:S(2)}) collective-permute-start(f32[4,3,2,8,256]{4,3,2,1,0:T(8,128)S(1)} %get-tuple-element.123), channel_id=1, source_target_pairs={{0,17},{1,16},{2,19},{3,18},{4,21},{5,20},{6,23},{7,22},{8,25},{9,... | collective-permute-start | bytes 589832 | tf_op jit(solution)/shard_map/ppermute | solution.py:412
  104.2 7.7 %collective-permute-start.22 = (f32[4,3,2,8,256]{4,3,2,1,0:T(8,128)S(1)}, f32[4,3,2,8,256]{4,3,2,1,0:T(8,128)}, u32[]{:S(2)}, u32[]{:S(2)}) collective-permute-start(f32[4,3,2,8,256]{4,3,2,1,0:T(8,128)S(1)} %get-tuple-element.122), channel_id=1, source_target_pairs={{0,25},{1,24},{2,27},{3,26},{4,29},{5,28},{6,31},{7,30},{8,1},{9,0... | collective-permute-start | bytes 589832 | tf_op jit(solution)/shard_map/ppermute | solution.py:412
  113.1 10.9 %collective-permute-start.23 = (f32[3,2,8,256]{3,2,1,0:T(8,128)S(1)}, f32[3,2,8,256]{3,2,1,0:T(8,128)S(1)}, u32[]{:S(2)}, u32[]{:S(2)}) collective-permute-start(f32[3,2,8,256]{3,2,1,0:T(8,128)S(1)} %get-tuple-element.128), channel_id=1, source_target_pairs={{0,2},{1,3},{2,4},{3,5},{4,6},{5,7},{6,0},{7,1},{8,10},{9,11},{10,... | collective-permute-start | bytes 147464 | tf_op jit(solution)/shard_map/ppermute | solution.py:417
  116.9 8.1 %collective-permute-start.24 = (f32[3,2,8,256]{3,2,1,0:T(8,128)S(1)}, f32[3,2,8,256]{3,2,1,0:T(8,128)S(1)}, u32[]{:S(2)}, u32[]{:S(2)}) collective-permute-start(f32[3,2,8,256]{3,2,1,0:T(8,128)S(1)} %get-tuple-element.130), channel_id=1, source_target_pairs={{0,4},{1,5},{2,6},{3,7},{4,0},{5,1},{6,2},{7,3},{8,12},{9,13},{10,... | collective-permute-start | bytes 147464 | tf_op jit(solution)/shard_map/ppermute | solution.py:417
  121.0 5.0 %collective-permute-start.25 = (f32[3,2,8,256]{3,2,1,0:T(8,128)S(1)}, f32[3,2,8,256]{3,2,1,0:T(8,128)S(1)}, u32[]{:S(2)}, u32[]{:S(2)}) collective-permute-start(f32[3,2,8,256]{3,2,1,0:T(8,128)S(1)} %get-tuple-element.129), channel_id=1, source_target_pairs={{0,6},{1,7},{2,0},{3,1},{4,2},{5,3},{6,4},{7,5},{8,14},{9,15},{10,... | collective-permute-start | bytes 147464 | tf_op jit(solution)/shard_map/ppermute | solution.py:417

commit v4 on v3

--- a/solution.py
+++ b/solution.py
@@ -70,8 +70,8 @@
     last = slabs - 1
     copies = [
         pltpu.make_async_copy(fields.at[last, light], field.at[last], sems.at[0]),
-        pltpu.make_async_copy(s_real, s_near, sems.at[1]),
-        pltpu.make_async_copy(s_imag, i_near, sems.at[2]),
+        pltpu.make_async_copy(s_real.at[last], s_near.at[last], sems.at[1]),
+        pltpu.make_async_copy(s_imag.at[last], i_near.at[last], sems.at[2]),
         pltpu.make_async_copy(table.at[0], t_near.at[0], sems.at[3]),
         pltpu.make_async_copy(table.at[1], t_near.at[1], sems.at[4]),
         pltpu.make_async_copy(table.at[2], t_near.at[2], sems.at[5]),
@@ -85,7 +85,12 @@
         pltpu.make_async_copy(psi.at[slab], psi_out.at[slab], sems.at[7 + slabs + slab])
         for slab in range(slabs)
     ]
-    for copy in copies + later:
+    rest = [
+        pltpu.make_async_copy(source.at[slab], target.at[slab], sems.at[7 + 2 * slabs + 2 * slab + part])
+        for slab in range(last)
+        for part, (source, target) in enumerate(((s_real, s_near), (s_imag, i_near)))
+    ]
+    for copy in copies + later + rest:
         copy.start()
     c_x, d_x = x_ramp[0], x_ramp[1]
     c_y, d_y = y_ramp[0], y_ramp[1]
@@ -113,8 +118,8 @@
     weight = 2.0 * (real * real + imag * imag - seen[...])
     out[0] = weight * real
     out[1] = -(weight * imag)
-    for store in stores:
-        store.wait()
+    for copy in rest + stores:
+        copy.wait()
 
 
 def keep_body(flag, _, *refs):
@@ -293,7 +298,7 @@
                 pltpu.VMEM((slabs, 2, extent, extent), BF16),
                 pltpu.VMEM((extent, extent), F32),
                 pltpu.VMEM(psi_shape.shape, F32),
-                pltpu.SemaphoreType.DMA((7 + 2 * slabs,)),
+                pltpu.SemaphoreType.DMA((7 + 4 * slabs,)),
             ],
             compiler_params=params,
             cost_estimate=cost(2),

time: 127 us -> 127 us (level)
  transfers between devices with their start and end apart: 26 -> 26, of which waited for: 9 -> 9; matrix products, arithmetic and copies ran while one was open for 1% -> 1% of each run, Pallas kernels for 15% -> 14%
where the time goes in v4:
time: 127 us; the launch traced here: 126 us
  waiting for transfers between devices  55.5 us (44%)
  starting transfers between devices  37.9 us (30%)
  Pallas kernels  27.8 us (22%)
  other arithmetic  2.64 us (2%)
  local copies, waits for them, and re-layouts  1.63 us (1%)
    ppermute x2, waiting for transfers between devices, on_device(): handed = lax.ppermute(lefts[light], 'depth', [(1, 0)])  38.3 us
    pallas_call x10, Pallas kernels, section(): pl.pallas_call(functools.partial(section_body, scale, kinds), out_shape=[...  16.2 us
    ppermute x7, waiting for transfers between devices, owned_sum(): total = total + lax.ppermute(block(c, d), 'illum', route)  15.2 us
    ppermute x3, starting transfers between devices, owned_sum(): result = result + lax.ppermute(sent, 'illum', route)  10.9 us
    ppermute x6, starting transfers between devices, on_device(): lax.ppermute(middle_now, 'depth', [(2 * here + 1, 2 * here), (2 * here, 2...  8.82 us
    pallas_call x2, Pallas kernels, entry(): pl.pallas_call(functools.partial(entry_body, light), out_shape=[state_sha...  8.18 us
    ppermute x7, starting transfers between devices, owned_sum(): total = total + lax.ppermute(block(c, d), 'illum', route)  7.79 us
    ppermute x6, starting transfers between devices, on_device(): lax.ppermute(before, 'depth', [(2 * here + 1, 2 * here - 1)])  7.27 us
  transfers between devices with their start and end apart: 26, of which 9 were waited for; matrix products, arithmetic and copies ran while one was open for 1% of the time, Pallas kernels for 14%

profile of v4, /device:TPU:32, one launch (start us, length us, event | category | flops | bytes accessed | tf_op | source)
XLA Modules:
  0.0 126.1 jit_solution(11559698461032930803)
XLA Ops:
  0.0 0.5 collective-permute-start.1
  0.5 0.7 fusion.25
  1.5 4.1 %entry.3 = (f32[2,256,256]{2,1,0:T(8,128)S(1)}, f32[3,2,256,256]{3,2,1,0:T(8,128)}, f32[3,256,256]{2,1,0:T(8,128)S(1)}, f32[3,256,256]{2,1,0:T(8,128)S(1)}, bf16[3,2,256,256]{3,2,1,0:T(8,128)(2,1)S(1)}) custom-call(bf16[3,2,2,256,256]{4,3,2,1,0:T(8,128)(2,1)} %fields.3, f32[3,256,256]{2,1,0:T(8,128)} %refs_0_.15, f32[3,256,256]{2,1,0:T(8,128)} %refs_1_.15, ...), custom_call_target="tpu_custom_call" | custom-call | flops 1207959552 | bytes 1048576 | tf_op jit(solution)/shard_map/entry/pallas_call | solution.py:291
  5.7 1.0 copy-done.8
  6.8 1.2 section.10
  8.0 1.5 %collective-permute-start.4 = (f32[2,256,256]{2,1,0:T(8,128)}, f32[2,256,256]{2,1,0:T(8,128)}, u32[]{:S(2)}, u32[]{:S(2)}) collective-permute-start(f32[2,256,256]{2,1,0:T(8,128)} %get-tuple-element.76), channel_id=1, source_target_pairs={{224,160},{225,161},{226,162},{227,163},{228,164},{229,165},{230,1... | collective-permute-start | bytes 1572872 | tf_op jit(solution)/shard_map/ppermute | solution.py:372
  9.5 1.5 %collective-permute-start.5 = (f32[2,256,256]{2,1,0:T(8,128)}, f32[2,256,256]{2,1,0:T(8,128)}, u32[]{:S(2)}, u32[]{:S(2)}) collective-permute-start(f32[2,256,256]{2,1,0:T(8,128)} %get-tuple-element.77), channel_id=1, source_target_pairs={{224,192},{192,224},{225,193},{193,225},{226,194},{194,226},{227,1... | collective-permute-start | bytes 1572872 | tf_op jit(solution)/shard_map/ppermute | solution.py:373
  11.1 4.1 %entry.2 = (f32[2,256,256]{2,1,0:T(8,128)S(1)}, f32[3,2,256,256]{3,2,1,0:T(8,128)}, f32[3,256,256]{2,1,0:T(8,128)S(1)}, f32[3,256,256]{2,1,0:T(8,128)S(1)}, bf16[3,2,256,256]{3,2,1,0:T(8,128)(2,1)S(1)}) custom-call(bf16[3,2,2,256,256]{4,3,2,1,0:T(8,128)(2,1)} %fields.3, f32[3,256,256]{2,1,0:T(8,128)} %refs_0_.15, f32[3,256,256]{2,1,0:T(8,128)} %refs_1_.15, ...), custom_call_target="tpu_custom_call" | custom-call | flops 1207959552 | bytes 1048576 | tf_op jit(solution)/shard_map/entry/pallas_call | solution.py:291
  15.5 0.7 collective-permute-start.2
  16.2 1.5 %collective-permute-start.3 = (f32[2,256,256]{2,1,0:T(8,128)}, f32[2,256,256]{2,1,0:T(8,128)}, u32[]{:S(2)}, u32[]{:S(2)}) collective-permute-start(f32[2,256,256]{2,1,0:T(8,128)} %get-tuple-element.75), channel_id=1, source_target_pairs={{224,192},{192,224},{225,193},{193,225},{226,194},{194,226},{227,1... | collective-permute-start | bytes 1572872 | tf_op jit(solution)/shard_map/ppermute | solution.py:373
  17.8 1.3 %section.12 = (f32[2,256,256]{2,1,0:T(8,128)}, f32[2,256,256]{2,1,0:T(8,128)S(1)}, f32[32,3,2,8,256]{4,3,2,1,0:T(8,128)S(1)}) custom-call(s32[1]{0:T(128)} %bitcast.3.flag, f32[2,256,256]{2,1,0:T(8,128)} %collective-permute-done.4.refs_0_, f32[2,256,256]{2,1,0:T(8,128)} %collective-permute-done.5.refs_1_, ...), custom_call_target="tpu_custom_call", output_to_operand_aliasing={{2}: (9, {})} | custom-call | flops 3623878656 | bytes 1048576 | tf_op jit(solution)/shard_map/section/pallas_call | solution.py:334
  19.1 1.5 %collective-permute-start.8 = (f32[2,256,256]{2,1,0:T(8,128)S(1)}, f32[2,256,256]{2,1,0:T(8,128)}, u32[]{:S(2)}, u32[]{:S(2)}) collective-permute-start(f32[2,256,256]{2,1,0:T(8,128)S(1)} %get-tuple-element.82._), channel_id=1, source_target_pairs={{160,96},{161,97},{162,98},{163,99},{164,100},{165,101},{166,102},... | collective-permute-start | bytes 1572872 | tf_op jit(solution)/shard_map/ppermute | solution.py:372
  20.6 1.5 %collective-permute-start.9 = (f32[2,256,256]{2,1,0:T(8,128)}, f32[2,256,256]{2,1,0:T(8,128)}, u32[]{:S(2)}, u32[]{:S(2)}) collective-permute-start(f32[2,256,256]{2,1,0:T(8,128)} %get-tuple-element.89), channel_id=1, source_target_pairs={{160,128},{128,160},{161,129},{129,161},{162,130},{130,162},{163,1... | collective-permute-start | bytes 1572872 | tf_op jit(solution)/shard_map/ppermute | solution.py:373
  22.2 0.5 section.13
  22.7 0.7 collective-permute-start.6
  23.4 1.5 %collective-permute-start.7 = (f32[2,256,256]{2,1,0:T(8,128)}, f32[2,256,256]{2,1,0:T(8,128)}, u32[]{:S(2)}, u32[]{:S(2)}) collective-permute-start(f32[2,256,256]{2,1,0:T(8,128)} %get-tuple-element.88), channel_id=1, source_target_pairs={{160,128},{128,160},{161,129},{129,161},{162,130},{130,162},{163,1... | collective-permute-start | bytes 1572872 | tf_op jit(solution)/shard_map/ppermute | solution.py:373
  24.9 1.3 %section.14 = (f32[2,256,256]{2,1,0:T(8,128)}, f32[2,256,256]{2,1,0:T(8,128)S(1)}, f32[32,3,2,8,256]{4,3,2,1,0:T(8,128)S(1)}) custom-call(s32[1]{0:T(128)} %bitcast.2.flag, f32[2,256,256]{2,1,0:T(8,128)} %collective-permute-done.8.refs_0_, f32[2,256,256]{2,1,0:T(8,128)} %collective-permute-done.9.refs_1_, ...), custom_call_target="tpu_custom_call", output_to_operand_aliasing={{2}: (9, {})} | custom-call | flops 3623878656 | bytes 1048576 | tf_op jit(solution)/shard_map/section/pallas_call | solution.py:334
  26.3 1.5 %collective-permute-start.12 = (f32[2,256,256]{2,1,0:T(8,128)S(1)}, f32[2,256,256]{2,1,0:T(8,128)}, u32[]{:S(2)}, u32[]{:S(2)}) collective-permute-start(f32[2,256,256]{2,1,0:T(8,128)S(1)} %get-tuple-element.94._), channel_id=1, source_target_pairs={{96,32},{97,33},{98,34},{99,35},{100,36},{101,37},{102,38},{103,39... | collective-permute-start | bytes 1572872 | tf_op jit(solution)/shard_map/ppermute | solution.py:372
  27.8 1.5 %collective-permute-start.13 = (f32[2,256,256]{2,1,0:T(8,128)}, f32[2,256,256]{2,1,0:T(8,128)}, u32[]{:S(2)}, u32[]{:S(2)}) collective-permute-start(f32[2,256,256]{2,1,0:T(8,128)} %get-tuple-element.101), channel_id=1, source_target_pairs={{96,64},{64,96},{97,65},{65,97},{98,66},{66,98},{99,67},{67,99},{1... | collective-permute-start | bytes 1572872 | tf_op jit(solution)/shard_map/ppermute | solution.py:373
  29.3 0.3 section.15
  29.6 1.5 %collective-permute-start.10 = (f32[2,256,256]{2,1,0:T(8,128)S(1)}, f32[2,256,256]{2,1,0:T(8,128)}, u32[]{:S(2)}, u32[]{:S(2)}) collective-permute-start(f32[2,256,256]{2,1,0:T(8,128)S(1)} %get-tuple-element.99._), channel_id=1, source_target_pairs={{96,32},{97,33},{98,34},{99,35},{100,36},{101,37},{102,38},{103,39... | collective-permute-start | bytes 1572872 | tf_op jit(solution)/shard_map/ppermute | solution.py:372
  31.1 1.4 %collective-permute-start.11 = (f32[2,256,256]{2,1,0:T(8,128)}, f32[2,256,256]{2,1,0:T(8,128)}, u32[]{:S(2)}, u32[]{:S(2)}) collective-permute-start(f32[2,256,256]{2,1,0:T(8,128)} %get-tuple-element.100), channel_id=1, source_target_pairs={{96,64},{64,96},{97,65},{65,97},{98,66},{66,98},{99,67},{67,99},{1... | collective-permute-start | bytes 1572872 | tf_op jit(solution)/shard_map/ppermute | solution.py:373
  32.6 1.3 %section.16 = (f32[2,256,256]{2,1,0:T(8,128)S(1)}, f32[32,3,2,8,256]{4,3,2,1,0:T(8,128)S(1)}) custom-call(s32[1]{0:T(128)} %bitcast.1.flag, f32[2,256,256]{2,1,0:T(8,128)} %collective-permute-done.12.refs_0_, f32[2,256,256]{2,1,0:T(8,128)} %collective-permute-done.13.refs_1_, ...), custom_call_target="tpu_custom_call", output_to_operand_aliasing={{1}: (7, {})} | custom-call | flops 1811939328 | bytes 1048576 | tf_op jit(solution)/shard_map/section/pallas_call | solution.py:334
  34.0 1.3 %collective-permute-start.14 = (f32[2,256,256]{2,1,0:T(8,128)S(1)}, f32[2,256,256]{2,1,0:T(8,128)S(1)}, u32[]{:S(2)}, u32[]{:S(2)}) collective-permute-start(f32[2,256,256]{2,1,0:T(8,128)S(1)} %get-tuple-element.106._), channel_id=1, source_target_pairs={{32,0},{33,1},{34,2},{35,3},{36,4},{37,5},{38,6},{39,7},{40,8},{41... | collective-permute-start | bytes 1572872 | tf_op jit(solution)/shard_map/ppermute | solution.py:391
  35.3 1.6 %keep.14 = (f32[3,256,256]{2,1,0:T(8,128)S(1)}, f32[3,256,256]{2,1,0:T(8,128)S(1)}, bf16[3,2,256,256]{3,2,1,0:T(8,128)(2,1)S(1)}) custom-call(s32[1]{0:T(128)} %bitcast.flag, f32[2,256,256]{2,1,0:T(8,128)} %copy-done, f32[3,256,256]{2,1,0:T(8,128)} %refs_0_.15, f32[3,256,256]{2,1,0:T(8,128)} %refs_1_.15, bf16[3,2,256,256]{3,2,1,0:T(8,128)(2,1)} %constant.488.clone.table.refs_2_), custom_call_target="tpu_custom_call" | custom-call | flops 603979776 | bytes 1048576 | tf_op jit(solution)/shard_map/keep/pallas_call | solution.py:279
  37.0 1.3 %section.17 = (f32[2,256,256]{2,1,0:T(8,128)S(1)}, f32[32,3,2,8,256]{4,3,2,1,0:T(8,128)S(1)}) custom-call(s32[1]{0:T(128)} %bitcast.1.flag, f32[2,256,256]{2,1,0:T(8,128)} %collective-permute-done.10.refs_0_, f32[2,256,256]{2,1,0:T(8,128)} %collective-permute-done.11.refs_1_, ...), custom_call_target="tpu_custom_call", output_to_operand_aliasing={{1}: (7, {})} | custom-call | flops 1811939328 | bytes 1048576 | tf_op jit(solution)/shard_map/section/pallas_call | solution.py:334
  38.3 30.9 %collective-permute-done.14.refs_0_ = f32[2,256,256]{2,1,0:T(8,128)S(1)} collective-permute-done((f32[2,256,256]{2,1,0:T(8,128)S(1)}, f32[2,256,256]{2,1,0:T(8,128)S(1)}, u32[]{:S(2)}, u32[]{:S(2)}) %collective-permute-start.14) | collective-permute-done | bytes 524320 | tf_op jit(solution)/shard_map/ppermute | solution.py:391
  69.3 4.2 %section.18.refs_5_ = f32[32,3,2,8,256]{4,3,2,1,0:T(8,128)S(1)} custom-call(s32[1]{0:T(128)} %bitcast.flag, f32[2,256,256]{2,1,0:T(8,128)S(1)} %collective-permute-done.14.refs_0_, f32[3,256,256]{2,1,0:T(8,128)S(1)} %get-tuple-element.112.refs_1_, f32[3,256,256]{2,1,0:T(8,128)S(1)} %get-tuple-element.113.refs_2_, ...), custom_call_target="tpu_custom_call", output_to_operand_aliasing={{}: (6, {})} | custom-call | flops 1811939328 | bytes 1048576 | tf_op jit(solution)/shard_map/section/pallas_call | solution.py:334
  73.5 1.3 %collective-permute-start.15 = (f32[2,256,256]{2,1,0:T(8,128)S(1)}, f32[2,256,256]{2,1,0:T(8,128)S(1)}, u32[]{:S(2)}, u32[]{:S(2)}) collective-permute-start(f32[2,256,256]{2,1,0:T(8,128)S(1)} %get-tuple-element.116._), channel_id=1, source_target_pairs={{32,0},{33,1},{34,2},{35,3},{36,4},{37,5},{38,6},{39,7},{40,8},{41... | collective-permute-start | bytes 1572872 | tf_op jit(solution)/shard_map/ppermute | solution.py:391
  75.0 1.6 %keep.15 = (f32[3,256,256]{2,1,0:T(8,128)S(1)}, f32[3,256,256]{2,1,0:T(8,128)S(1)}, bf16[3,2,256,256]{3,2,1,0:T(8,128)(2,1)S(1)}) custom-call(s32[1]{0:T(128)} %bitcast.flag, f32[2,256,256]{2,1,0:T(8,128)} %copy-done.1, f32[3,256,256]{2,1,0:T(8,128)} %refs_0_.15, f32[3,256,256]{2,1,0:T(8,128)} %refs_1_.15, bf16[3,2,256,256]{3,2,1,0:T(8,128)(2,1)} %constant.488.clone.table.refs_2_), custom_call_target="tpu_custom_call" | custom-call | flops 603979776 | bytes 1048576 | tf_op jit(solution)/shard_map/keep/pallas_call | solution.py:279
  76.6 7.3 %collective-permute-done.15.refs_0_ = f32[2,256,256]{2,1,0:T(8,128)S(1)} collective-permute-done((f32[2,256,256]{2,1,0:T(8,128)S(1)}, f32[2,256,256]{2,1,0:T(8,128)S(1)}, u32[]{:S(2)}, u32[]{:S(2)}) %collective-permute-start.15) | collective-permute-done | bytes 524320 | tf_op jit(solution)/shard_map/ppermute | solution.py:391
  84.0 4.2 %section.19 = f32[32,3,2,8,256]{4,3,2,1,0:T(8,128)S(1)} custom-call(s32[1]{0:T(128)} %bitcast.flag, f32[2,256,256]{2,1,0:T(8,128)S(1)} %collective-permute-done.15.refs_0_, f32[3,256,256]{2,1,0:T(8,128)S(1)} %get-tuple-element.117.refs_1_, f32[3,256,256]{2,1,0:T(8,128)S(1)} %get-tuple-element.118.refs_2_, ...), custom_call_target="tpu_custom_call", output_to_operand_aliasing={{}: (6, {})} | custom-call | flops 1811939328 | bytes 1048576 | tf_op jit(solution)/shard_map/section/pallas_call | solution.py:334
  88.4 1.6 %collective-permute-start.16 = (f32[4,3,2,8,256]{4,3,2,1,0:T(8,128)S(1)}, f32[4,3,2,8,256]{4,3,2,1,0:T(8,128)S(1)}, u32[]{:S(2)}, u32[]{:S(2)}) collective-permute-start(f32[4,3,2,8,256]{4,3,2,1,0:T(8,128)S(1)} %get-tuple-element.121), channel_id=1, source_target_pairs={{0,8},{1,9},{2,10},{3,11},{4,12},{5,13},{6,14},{7,15},{8,16},{9,17... | collective-permute-start | bytes 589832 | tf_op jit(solution)/shard_map/ppermute | solution.py:417
  89.9 2.7 %collective-permute-start.17 = (f32[4,3,2,8,256]{4,3,2,1,0:T(8,128)S(1)}, f32[4,3,2,8,256]{4,3,2,1,0:T(8,128)S(1)}, u32[]{:S(2)}, u32[]{:S(2)}) collective-permute-start(f32[4,3,2,8,256]{4,3,2,1,0:T(8,128)S(1)} %get-tuple-element.127), channel_id=1, source_target_pairs={{0,16},{1,17},{2,18},{3,19},{4,20},{5,21},{6,22},{7,23},{8,24},{9,... | collective-permute-start | bytes 589832 | tf_op jit(solution)/shard_map/ppermute | solution.py:417
  92.7 1.4 %collective-permute-start.18 = (f32[4,3,2,8,256]{4,3,2,1,0:T(8,128)S(1)}, f32[4,3,2,8,256]{4,3,2,1,0:T(8,128)S(1)}, u32[]{:S(2)}, u32[]{:S(2)}) collective-permute-start(f32[4,3,2,8,256]{4,3,2,1,0:T(8,128)S(1)} %get-tuple-element.126), channel_id=1, source_target_pairs={{0,24},{1,25},{2,26},{3,27},{4,28},{5,29},{6,30},{7,31},{8,0},{9,1... | collective-permute-start | bytes 589832 | tf_op jit(solution)/shard_map/ppermute | solution.py:417
  94.2 1.9 %collective-permute-start.20 = (f32[4,3,2,8,256]{4,3,2,1,0:T(8,128)S(1)}, f32[4,3,2,8,256]{4,3,2,1,0:T(8,128)S(1)}, u32[]{:S(2)}, u32[]{:S(2)}) collective-permute-start(f32[4,3,2,8,256]{4,3,2,1,0:T(8,128)S(1)} %get-tuple-element.124), channel_id=1, source_target_pairs={{0,9},{1,8},{2,11},{3,10},{4,13},{5,12},{6,15},{7,14},{8,17},{9,16... | collective-permute-start | bytes 589832 | tf_op jit(solution)/shard_map/ppermute | solution.py:417
  96.1 3.8 %collective-permute-done.16 = f32[4,3,2,8,256]{4,3,2,1,0:T(8,128)S(1)} collective-permute-done((f32[4,3,2,8,256]{4,3,2,1,0:T(8,128)S(1)}, f32[4,3,2,8,256]{4,3,2,1,0:T(8,128)S(1)}, u32[]{:S(2)}, u32[]{:S(2)}) %collective-permute-start.16) | collective-permute-done | bytes 196640 | tf_op jit(solution)/shard_map/ppermute | solution.py:417
  100.0 3.7 %collective-permute-done.17 = f32[4,3,2,8,256]{4,3,2,1,0:T(8,128)S(1)} collective-permute-done((f32[4,3,2,8,256]{4,3,2,1,0:T(8,128)S(1)}, f32[4,3,2,8,256]{4,3,2,1,0:T(8,128)S(1)}, u32[]{:S(2)}, u32[]{:S(2)}) %collective-permute-start.17) | collective-permute-done | bytes 196640 | tf_op jit(solution)/shard_map/ppermute | solution.py:417
  103.7 1.0 collective-permute-done.20
  104.7 3.4 %collective-permute-done.21 = f32[4,3,2,8,256]{4,3,2,1,0:T(8,128)} collective-permute-done((f32[4,3,2,8,256]{4,3,2,1,0:T(8,128)S(1)}, f32[4,3,2,8,256]{4,3,2,1,0:T(8,128)}, u32[]{:S(2)}, u32[]{:S(2)}) %collective-permute-start.21) | collective-permute-done | bytes 196640 | tf_op jit(solution)/shard_map/ppermute | solution.py:417
  108.1 3.3 %collective-permute-done.22 = f32[4,3,2,8,256]{4,3,2,1,0:T(8,128)} collective-permute-done((f32[4,3,2,8,256]{4,3,2,1,0:T(8,128)S(1)}, f32[4,3,2,8,256]{4,3,2,1,0:T(8,128)}, u32[]{:S(2)}, u32[]{:S(2)}) %collective-permute-start.22) | collective-permute-done | bytes 196640 | tf_op jit(solution)/shard_map/ppermute | solution.py:417
  111.4 1.2 fusion.5
  112.6 3.7 %collective-permute-start.23 = (f32[3,2,8,256]{3,2,1,0:T(8,128)S(1)}, f32[3,2,8,256]{3,2,1,0:T(8,128)S(1)}, u32[]{:S(2)}, u32[]{:S(2)}) collective-permute-start(f32[3,2,8,256]{3,2,1,0:T(8,128)S(1)} %get-tuple-element.128), channel_id=1, source_target_pairs={{0,2},{1,3},{2,4},{3,5},{4,6},{5,7},{6,0},{7,1},{8,10},{9,11},{10,... | collective-permute-start | bytes 147464 | tf_op jit(solution)/shard_map/ppermute | solution.py:422
  116.3 4.1 %collective-permute-start.24 = (f32[3,2,8,256]{3,2,1,0:T(8,128)S(1)}, f32[3,2,8,256]{3,2,1,0:T(8,128)S(1)}, u32[]{:S(2)}, u32[]{:S(2)}) collective-permute-start(f32[3,2,8,256]{3,2,1,0:T(8,128)S(1)} %get-tuple-element.130), channel_id=1, source_target_pairs={{0,4},{1,5},{2,6},{3,7},{4,0},{5,1},{6,2},{7,3},{8,12},{9,13},{10,... | collective-permute-start | bytes 147464 | tf_op jit(solution)/shard_map/ppermute | solution.py:422
  120.5 3.0 %collective-permute-start.25 = (f32[3,2,8,256]{3,2,1,0:T(8,128)S(1)}, f32[3,2,8,256]{3,2,1,0:T(8,128)S(1)}, u32[]{:S(2)}, u32[]{:S(2)}) collective-permute-start(f32[3,2,8,256]{3,2,1,0:T(8,128)S(1)} %get-tuple-element.129), channel_id=1, source_target_pairs={{0,6},{1,7},{2,0},{3,1},{4,2},{5,3},{6,4},{7,5},{8,14},{9,15},{10,... | collective-permute-start | bytes 147464 | tf_op jit(solution)/shard_map/ppermute | solution.py:422
  123.5 0.9 collective-permute-done.24
  124.4 1.0 collective-permute-done.25
  125.5 0.6 fusion.7
  (53 shorter events, 1.5 us)
Async XLA Ops:
  0.0 5.6 %collective-permute-start = (f32[3,256,256]{2,1,0:T(8,128)}, f32[3,256,256]{2,1,0:T(8,128)S(1)}, u32[]{:S(2)}, u32[]{:S(2)}) collective-permute-start(f32[3,256,256]{2,1,0:T(8,128)} %refs_0_.15), channel_id=1, source_target_pairs={{32,0},{96,64},{160,128},{224,192},{0,32},{64,96},{128,160},{192,2... | collective-permute-start | bytes 2359304 | tf_op jit(solution)/shard_map/ppermute | solution.py:348
  0.0 5.7 %collective-permute-start.1 = (f32[3,256,256]{2,1,0:T(8,128)}, f32[3,256,256]{2,1,0:T(8,128)S(1)}, u32[]{:S(2)}, u32[]{:S(2)}) collective-permute-start(f32[3,256,256]{2,1,0:T(8,128)} %refs_1_.15), channel_id=1, source_target_pairs={{32,0},{96,64},{160,128},{224,192},{0,32},{64,96},{128,160},{192,2... | collective-permute-start | bytes 2359304 | tf_op jit(solution)/shard_map/ppermute | solution.py:348
  5.6 1.2 copy-start.7
  5.7 1.0 copy-start.8
  8.0 9.7 %collective-permute-start.4 = (f32[2,256,256]{2,1,0:T(8,128)}, f32[2,256,256]{2,1,0:T(8,128)}, u32[]{:S(2)}, u32[]{:S(2)}) collective-permute-start(f32[2,256,256]{2,1,0:T(8,128)} %get-tuple-element.76), channel_id=1, source_target_pairs={{224,160},{225,161},{226,162},{227,163},{228,164},{229,165},{230,1... | collective-permute-start | bytes 1572872 | tf_op jit(solution)/shard_map/ppermute | solution.py:372
  9.5 8.3 %collective-permute-start.5 = (f32[2,256,256]{2,1,0:T(8,128)}, f32[2,256,256]{2,1,0:T(8,128)}, u32[]{:S(2)}, u32[]{:S(2)}) collective-permute-start(f32[2,256,256]{2,1,0:T(8,128)} %get-tuple-element.77), channel_id=1, source_target_pairs={{224,192},{192,224},{225,193},{193,225},{226,194},{194,226},{227,1... | collective-permute-start | bytes 1572872 | tf_op jit(solution)/shard_map/ppermute | solution.py:373
  15.5 2.2 %copy-start.5 = (f32[2,256,256]{2,1,0:T(8,128)}, f32[2,256,256]{2,1,0:T(8,128)S(1)}, u32[]{:S(2)}) copy-start(f32[2,256,256]{2,1,0:T(8,128)S(1)} %get-tuple-element.74._) | copy-start | bytes 1572868
  15.5 6.6 %collective-permute-start.2 = (f32[2,256,256]{2,1,0:T(8,128)S(1)}, f32[2,256,256]{2,1,0:T(8,128)S(1)}, u32[]{:S(2)}, u32[]{:S(2)}) collective-permute-start(f32[2,256,256]{2,1,0:T(8,128)S(1)} %get-tuple-element.74._), channel_id=1, source_target_pairs={{224,160},{225,161},{226,162},{227,163},{228,164},{229,165},{230,1... | collective-permute-start | bytes 1572872 | tf_op jit(solution)/shard_map/ppermute | solution.py:372
  16.2 5.9 %collective-permute-start.3 = (f32[2,256,256]{2,1,0:T(8,128)}, f32[2,256,256]{2,1,0:T(8,128)}, u32[]{:S(2)}, u32[]{:S(2)}) collective-permute-start(f32[2,256,256]{2,1,0:T(8,128)} %get-tuple-element.75), channel_id=1, source_target_pairs={{224,192},{192,224},{225,193},{193,225},{226,194},{194,226},{227,1... | collective-permute-start | bytes 1572872 | tf_op jit(solution)/shard_map/ppermute | solution.py:373
  19.1 3.0 %copy-start.4 = (f32[2,256,256]{2,1,0:T(8,128)}, f32[2,256,256]{2,1,0:T(8,128)S(1)}, u32[]{:S(2)}) copy-start(f32[2,256,256]{2,1,0:T(8,128)S(1)} %get-tuple-element.82._) | copy-start | bytes 1572868
  19.1 5.8 %collective-permute-start.8 = (f32[2,256,256]{2,1,0:T(8,128)S(1)}, f32[2,256,256]{2,1,0:T(8,128)}, u32[]{:S(2)}, u32[]{:S(2)}) collective-permute-start(f32[2,256,256]{2,1,0:T(8,128)S(1)} %get-tuple-element.82._), channel_id=1, source_target_pairs={{160,96},{161,97},{162,98},{163,99},{164,100},{165,101},{166,102},... | collective-permute-start | bytes 1572872 | tf_op jit(solution)/shard_map/ppermute | solution.py:372
  20.6 4.3 %collective-permute-start.9 = (f32[2,256,256]{2,1,0:T(8,128)}, f32[2,256,256]{2,1,0:T(8,128)}, u32[]{:S(2)}, u32[]{:S(2)}) collective-permute-start(f32[2,256,256]{2,1,0:T(8,128)} %get-tuple-element.89), channel_id=1, source_target_pairs={{160,128},{128,160},{161,129},{129,161},{162,130},{130,162},{163,1... | collective-permute-start | bytes 1572872 | tf_op jit(solution)/shard_map/ppermute | solution.py:373
  22.7 2.2 %copy-start.3 = (f32[2,256,256]{2,1,0:T(8,128)}, f32[2,256,256]{2,1,0:T(8,128)S(1)}, u32[]{:S(2)}) copy-start(f32[2,256,256]{2,1,0:T(8,128)S(1)} %get-tuple-element.87._) | copy-start | bytes 1572868
  22.7 6.6 %collective-permute-start.6 = (f32[2,256,256]{2,1,0:T(8,128)S(1)}, f32[2,256,256]{2,1,0:T(8,128)S(1)}, u32[]{:S(2)}, u32[]{:S(2)}) collective-permute-start(f32[2,256,256]{2,1,0:T(8,128)S(1)} %get-tuple-element.87._), channel_id=1, source_target_pairs={{160,96},{161,97},{162,98},{163,99},{164,100},{165,101},{166,102},... | collective-permute-start | bytes 1572872 | tf_op jit(solution)/shard_map/ppermute | solution.py:372
  23.4 5.9 %collective-permute-start.7 = (f32[2,256,256]{2,1,0:T(8,128)}, f32[2,256,256]{2,1,0:T(8,128)}, u32[]{:S(2)}, u32[]{:S(2)}) collective-permute-start(f32[2,256,256]{2,1,0:T(8,128)} %get-tuple-element.88), channel_id=1, source_target_pairs={{160,128},{128,160},{161,129},{129,161},{162,130},{130,162},{163,1... | collective-permute-start | bytes 1572872 | tf_op jit(solution)/shard_map/ppermute | solution.py:373
  26.3 2.9 %copy-start.2 = (f32[2,256,256]{2,1,0:T(8,128)}, f32[2,256,256]{2,1,0:T(8,128)S(1)}, u32[]{:S(2)}) copy-start(f32[2,256,256]{2,1,0:T(8,128)S(1)} %get-tuple-element.94._) | copy-start | bytes 1572868
  26.3 6.3 %collective-permute-start.12 = (f32[2,256,256]{2,1,0:T(8,128)S(1)}, f32[2,256,256]{2,1,0:T(8,128)}, u32[]{:S(2)}, u32[]{:S(2)}) collective-permute-start(f32[2,256,256]{2,1,0:T(8,128)S(1)} %get-tuple-element.94._), channel_id=1, source_target_pairs={{96,32},{97,33},{98,34},{99,35},{100,36},{101,37},{102,38},{103,39... | collective-permute-start | bytes 1572872 | tf_op jit(solution)/shard_map/ppermute | solution.py:372
  27.8 4.8 %collective-permute-start.13 = (f32[2,256,256]{2,1,0:T(8,128)}, f32[2,256,256]{2,1,0:T(8,128)}, u32[]{:S(2)}, u32[]{:S(2)}) collective-permute-start(f32[2,256,256]{2,1,0:T(8,128)} %get-tuple-element.101), channel_id=1, source_target_pairs={{96,64},{64,96},{97,65},{65,97},{98,66},{66,98},{99,67},{67,99},{1... | collective-permute-start | bytes 1572872 | tf_op jit(solution)/shard_map/ppermute | solution.py:373
  29.6 2.9 %copy-start.6 = (f32[2,256,256]{2,1,0:T(8,128)}, f32[2,256,256]{2,1,0:T(8,128)S(1)}, u32[]{:S(2)}) copy-start(f32[2,256,256]{2,1,0:T(8,128)S(1)} %get-tuple-element.99._) | copy-start | bytes 1572868
  29.6 7.3 %collective-permute-start.10 = (f32[2,256,256]{2,1,0:T(8,128)S(1)}, f32[2,256,256]{2,1,0:T(8,128)}, u32[]{:S(2)}, u32[]{:S(2)}) collective-permute-start(f32[2,256,256]{2,1,0:T(8,128)S(1)} %get-tuple-element.99._), channel_id=1, source_target_pairs={{96,32},{97,33},{98,34},{99,35},{100,36},{101,37},{102,38},{103,39... | collective-permute-start | bytes 1572872 | tf_op jit(solution)/shard_map/ppermute | solution.py:372
  31.1 5.9 %collective-permute-start.11 = (f32[2,256,256]{2,1,0:T(8,128)}, f32[2,256,256]{2,1,0:T(8,128)}, u32[]{:S(2)}, u32[]{:S(2)}) collective-permute-start(f32[2,256,256]{2,1,0:T(8,128)} %get-tuple-element.100), channel_id=1, source_target_pairs={{96,64},{64,96},{97,65},{65,97},{98,66},{66,98},{99,67},{67,99},{1... | collective-permute-start | bytes 1572872 | tf_op jit(solution)/shard_map/ppermute | solution.py:373
  33.9 1.3 %copy-start = (f32[2,256,256]{2,1,0:T(8,128)}, f32[2,256,256]{2,1,0:T(8,128)S(1)}, u32[]{:S(2)}) copy-start(f32[2,256,256]{2,1,0:T(8,128)S(1)} %get-tuple-element.106._) | copy-start | bytes 1572868
  34.0 35.3 %collective-permute-start.14 = (f32[2,256,256]{2,1,0:T(8,128)S(1)}, f32[2,256,256]{2,1,0:T(8,128)S(1)}, u32[]{:S(2)}, u32[]{:S(2)}) collective-permute-start(f32[2,256,256]{2,1,0:T(8,128)S(1)} %get-tuple-element.106._), channel_id=1, source_target_pairs={{32,0},{33,1},{34,2},{35,3},{36,4},{37,5},{38,6},{39,7},{40,8},{41... | collective-permute-start | bytes 1572872 | tf_op jit(solution)/shard_map/ppermute | solution.py:391
  38.3 35.2 %copy-start.1 = (f32[2,256,256]{2,1,0:T(8,128)}, f32[2,256,256]{2,1,0:T(8,128)S(1)}, u32[]{:S(2)}) copy-start(f32[2,256,256]{2,1,0:T(8,128)S(1)} %get-tuple-element.116._) | copy-start | bytes 1572868
  73.5 10.4 %collective-permute-start.15 = (f32[2,256,256]{2,1,0:T(8,128)S(1)}, f32[2,256,256]{2,1,0:T(8,128)S(1)}, u32[]{:S(2)}, u32[]{:S(2)}) collective-permute-start(f32[2,256,256]{2,1,0:T(8,128)S(1)} %get-tuple-element.116._), channel_id=1, source_target_pairs={{32,0},{33,1},{34,2},{35,3},{36,4},{37,5},{38,6},{39,7},{40,8},{41... | collective-permute-start | bytes 1572872 | tf_op jit(solution)/shard_map/ppermute | solution.py:391
  88.4 11.6 %collective-permute-start.16 = (f32[4,3,2,8,256]{4,3,2,1,0:T(8,128)S(1)}, f32[4,3,2,8,256]{4,3,2,1,0:T(8,128)S(1)}, u32[]{:S(2)}, u32[]{:S(2)}) collective-permute-start(f32[4,3,2,8,256]{4,3,2,1,0:T(8,128)S(1)} %get-tuple-element.121), channel_id=1, source_target_pairs={{0,8},{1,9},{2,10},{3,11},{4,12},{5,13},{6,14},{7,15},{8,16},{9,17... | collective-permute-start | bytes 589832 | tf_op jit(solution)/shard_map/ppermute | solution.py:417
  89.9 13.7 %collective-permute-start.17 = (f32[4,3,2,8,256]{4,3,2,1,0:T(8,128)S(1)}, f32[4,3,2,8,256]{4,3,2,1,0:T(8,128)S(1)}, u32[]{:S(2)}, u32[]{:S(2)}) collective-permute-start(f32[4,3,2,8,256]{4,3,2,1,0:T(8,128)S(1)} %get-tuple-element.127), channel_id=1, source_target_pairs={{0,16},{1,17},{2,18},{3,19},{4,20},{5,21},{6,22},{7,23},{8,24},{9,... | collective-permute-start | bytes 589832 | tf_op jit(solution)/shard_map/ppermute | solution.py:417
  92.7 11.0 %collective-permute-start.18 = (f32[4,3,2,8,256]{4,3,2,1,0:T(8,128)S(1)}, f32[4,3,2,8,256]{4,3,2,1,0:T(8,128)S(1)}, u32[]{:S(2)}, u32[]{:S(2)}) collective-permute-start(f32[4,3,2,8,256]{4,3,2,1,0:T(8,128)S(1)} %get-tuple-element.126), channel_id=1, source_target_pairs={{0,24},{1,25},{2,26},{3,27},{4,28},{5,29},{6,30},{7,31},{8,0},{9,1... | collective-permute-start | bytes 589832 | tf_op jit(solution)/shard_map/ppermute | solution.py:417
  94.1 9.6 %collective-permute-start.19 = (f32[4,3,2,8,256]{4,3,2,1,0:T(8,128)S(1)}, f32[4,3,2,8,256]{4,3,2,1,0:T(8,128)S(1)}, u32[]{:S(2)}, u32[]{:S(2)}) collective-permute-start(f32[4,3,2,8,256]{4,3,2,1,0:T(8,128)S(1)} %get-tuple-element.125), channel_id=1, source_target_pairs={{0,1},{1,0},{2,3},{3,2},{4,5},{5,4},{6,7},{7,6},{8,9},{9,8},{10,11... | collective-permute-start | bytes 589832 | tf_op jit(solution)/shard_map/ppermute | solution.py:417
  94.2 10.5 %collective-permute-start.20 = (f32[4,3,2,8,256]{4,3,2,1,0:T(8,128)S(1)}, f32[4,3,2,8,256]{4,3,2,1,0:T(8,128)S(1)}, u32[]{:S(2)}, u32[]{:S(2)}) collective-permute-start(f32[4,3,2,8,256]{4,3,2,1,0:T(8,128)S(1)} %get-tuple-element.124), channel_id=1, source_target_pairs={{0,9},{1,8},{2,11},{3,10},{4,13},{5,12},{6,15},{7,14},{8,17},{9,16... | collective-permute-start | bytes 589832 | tf_op jit(solution)/shard_map/ppermute | solution.py:417
  100.0 8.2 %collective-permute-start.21 = (f32[4,3,2,8,256]{4,3,2,1,0:T(8,128)S(1)}, f32[4,3,2,8,256]{4,3,2,1,0:T(8,128)}, u32[]{:S(2)}, u32[]{:S(2)}) collective-permute-start(f32[4,3,2,8,256]{4,3,2,1,0:T(8,128)S(1)} %get-tuple-element.123), channel_id=1, source_target_pairs={{0,17},{1,16},{2,19},{3,18},{4,21},{5,20},{6,23},{7,22},{8,25},{9,... | collective-permute-start | bytes 589832 | tf_op jit(solution)/shard_map/ppermute | solution.py:417
  103.7 7.7 %collective-permute-start.22 = (f32[4,3,2,8,256]{4,3,2,1,0:T(8,128)S(1)}, f32[4,3,2,8,256]{4,3,2,1,0:T(8,128)}, u32[]{:S(2)}, u32[]{:S(2)}) collective-permute-start(f32[4,3,2,8,256]{4,3,2,1,0:T(8,128)S(1)} %get-tuple-element.122), channel_id=1, source_target_pairs={{0,25},{1,24},{2,27},{3,26},{4,29},{5,28},{6,31},{7,30},{8,1},{9,0... | collective-permute-start | bytes 589832 | tf_op jit(solution)/shard_map/ppermute | solution.py:417
  112.6 10.9 %collective-permute-start.23 = (f32[3,2,8,256]{3,2,1,0:T(8,128)S(1)}, f32[3,2,8,256]{3,2,1,0:T(8,128)S(1)}, u32[]{:S(2)}, u32[]{:S(2)}) collective-permute-start(f32[3,2,8,256]{3,2,1,0:T(8,128)S(1)} %get-tuple-element.128), channel_id=1, source_target_pairs={{0,2},{1,3},{2,4},{3,5},{4,6},{5,7},{6,0},{7,1},{8,10},{9,11},{10,... | collective-permute-start | bytes 147464 | tf_op jit(solution)/shard_map/ppermute | solution.py:422
  116.3 8.1 %collective-permute-start.24 = (f32[3,2,8,256]{3,2,1,0:T(8,128)S(1)}, f32[3,2,8,256]{3,2,1,0:T(8,128)S(1)}, u32[]{:S(2)}, u32[]{:S(2)}) collective-permute-start(f32[3,2,8,256]{3,2,1,0:T(8,128)S(1)} %get-tuple-element.130), channel_id=1, source_target_pairs={{0,4},{1,5},{2,6},{3,7},{4,0},{5,1},{6,2},{7,3},{8,12},{9,13},{10,... | collective-permute-start | bytes 147464 | tf_op jit(solution)/shard_map/ppermute | solution.py:422
  120.5 5.0 %collective-permute-start.25 = (f32[3,2,8,256]{3,2,1,0:T(8,128)S(1)}, f32[3,2,8,256]{3,2,1,0:T(8,128)S(1)}, u32[]{:S(2)}, u32[]{:S(2)}) collective-permute-start(f32[3,2,8,256]{3,2,1,0:T(8,128)S(1)} %get-tuple-element.129), channel_id=1, source_target_pairs={{0,6},{1,7},{2,0},{3,1},{4,2},{5,3},{6,4},{7,5},{8,14},{9,15},{10,... | collective-permute-start | bytes 147464 | tf_op jit(solution)/shard_map/ppermute | solution.py:422
